TPU v7x, 32 devices: a whole 2x2x4 slice. The times are simulated.
32 devices in a mesh: seq: 16 (over z, y, x), head: 2 (over core).
Axes of the slice: x: 2, y: 2, z: 4, core: 2. Of those that a mesh axis runs over, the one named last changes fastest.
Arguments:
- inputs: bfloat16 [2, 2048, 2048], P(None, 'seq'), may hold values from -6 to 6
- norm_gain1: bfloat16 [2048], P('seq'), may hold values from 0.099609375 to 1.8984375
- w_query: bfloat16 [2048, 256], P('seq', 'head'), may hold values from -0.125 to 0.125
- w_key: bfloat16 [2048, 256], P('seq', 'head'), may hold values from -0.125 to 0.125
- w_value: bfloat16 [2048, 2048], P('seq', 'head'), may hold values from -0.125 to 0.125
- w_out: bfloat16 [2048, 2048], P('head', 'seq'), may hold values from -1 to 1
- norm_gain2: bfloat16 [2048], P('seq'), may hold values from 0.099609375 to 1.8984375
- w_gate: bfloat16 [2048, 5632], P('seq', 'head'), may hold values from -0.125 to 0.125
- w_up: bfloat16 [2048, 5632], P('seq', 'head'), may hold values from -0.125 to 0.125
- w_down: bfloat16 [5632, 2048], P('head', 'seq'), may hold values from -0.078125 to 0.078125
- cotangent: bfloat16 [2, 2048, 2048], P(None, 'seq'), may hold values from -6 to 6
Outputs:
- outputs: bfloat16 [2, 2048, 2048], P(None, 'seq')
- input_grad: bfloat16 [2, 2048, 2048], P(None, 'seq')
- grad_gain1: float32 [2048], P('seq')
- grad_query: float32 [2048, 256], P('seq', 'head')
- grad_key: float32 [2048, 256], P('seq', 'head')
- grad_value: float32 [2048, 2048], P('seq', 'head')
- grad_out: float32 [2048, 2048], P('head', 'seq')
- grad_gain2: float32 [2048], P('seq')
- grad_gate: float32 [2048, 5632], P('seq', 'head')
- grad_up: float32 [2048, 5632], P('seq', 'head')
- grad_down: float32 [5632, 2048], P('head', 'seq')
All inputs are finite; a program needn't handle non-finite values.
Results may differ from a plain program's by a relative error of at most 0.017.
Values may be sent and summed in bfloat16 or wider, within the bound.
A program may use at most 320 MiB of HBM per device.

v0:
```python
import jax
import jax.numpy as jnp
from jax import lax
from jax.sharding import PartitionSpec as P

F = 16
DV = 128


epsilon = 1e-05
highest = lax.Precision.HIGHEST


def entering(part, axis, combine, identity, reverse):
    count = lax.axis_size(axis)
    place = lax.axis_index(axis)
    ahead = count - 1 - place if reverse else place
    gathered = jax.tree.map(lambda a: lax.all_gather(a, axis), part)
    state = jax.tree.map(lambda a, e: jnp.zeros_like(a) + jnp.asarray(e, a.dtype), part, identity)

    def one(turn, state):
        source = count - 1 - turn if reverse else turn
        return combine(
            state, jax.tree.map(lambda a: lax.dynamic_index_in_dim(a, source, 0, False), gathered)
        )

    return lax.fori_loop(0, ahead, one, state)


def rms_apply(values, gain):
    scale = lax.rsqrt(jnp.mean(values * values, axis=-1, keepdims=True) + epsilon)
    return values * scale * gain


def feature_map(projected):
    count = projected.shape[0]
    pieces = projected.reshape(count, -1, F)
    square = (pieces[:, :, :, None] * pieces[:, :, None, :]).reshape(count, pieces.shape[1], F * F)
    return jnp.concatenate(
        [jnp.ones_like(pieces[:, :, :1]), pieces * F ** (-0.25), square * (2.0 * F) ** (-0.5)],
        axis=-1,
    )


def swiglu(gate, up_part):
    return jax.nn.silu(gate) * up_part


def round_trip(values):
    return lax.optimization_barrier(values.astype(jnp.bfloat16)).astype(jnp.float32)


def add_pair(earlier, later):
    return (earlier[0] + later[0], earlier[1] + later[1])


def block_pass(tokens, upstream, gathered):
    gain_one, query_w, key_w, value_w, out_w, gain_two, gate_w, up_w, down_w = gathered
    f32 = jnp.float32
    bf16 = jnp.bfloat16
    stream = tokens.astype(f32)
    count = stream.shape[0]
    normed_f, norm_one_pull = jax.vjp(rms_apply, stream, gain_one.astype(f32))
    normed = normed_f.astype(bf16)
    queries = jnp.dot(normed, query_w, preferred_element_type=f32)
    keys_all = jnp.dot(normed, key_w, preferred_element_type=f32)
    values = jnp.dot(normed, value_w, preferred_element_type=f32).astype(bf16)
    query_feat_f, query_pull = jax.vjp(feature_map, queries)
    key_feat_f, key_pull = jax.vjp(feature_map, keys_all)
    query_feat = jnp.transpose(query_feat_f.astype(bf16), (1, 0, 2))
    key_feat = jnp.transpose(key_feat_f.astype(bf16), (1, 0, 2))
    value_heads = jnp.transpose(values.reshape(count, -1, DV), (1, 0, 2))
    causal = (jnp.arange(count)[:, None] >= jnp.arange(count)[None, :]).astype(f32)
    scores = jnp.einsum("htf,hsf->hts", query_feat, key_feat, preferred_element_type=f32) * causal
    weighted = scores.astype(bf16)
    num_local = jnp.einsum("hts,hsd->htd", weighted, value_heads, preferred_element_type=f32)
    den_local = jnp.sum(weighted.astype(f32), axis=-1)
    states = jnp.einsum("hsf,hsd->hfd", key_feat, value_heads, preferred_element_type=f32)
    totals = jnp.sum(key_feat.astype(f32), axis=1)
    state_before, total_before = entering(
        (states, totals), "seq", add_pair, (jnp.zeros_like(states), jnp.zeros_like(totals)), False
    )
    query_wide = query_feat.astype(f32)
    numer = num_local + jnp.einsum("htf,hfd->htd", query_wide, state_before, precision=highest)
    denom = den_local + jnp.einsum("htf,hf->ht", query_wide, total_before, precision=highest)
    ratio = numer / denom[..., None]
    heads_out = jnp.transpose(ratio, (1, 0, 2)).reshape(count, -1).astype(bf16)
    attended = lax.psum(jnp.dot(heads_out, out_w, preferred_element_type=f32), "head")
    middle = stream + attended
    normed_two_f, norm_two_pull = jax.vjp(rms_apply, middle, gain_two.astype(f32))
    normed_two = normed_two_f.astype(bf16)
    gate = jnp.dot(normed_two, gate_w, preferred_element_type=f32)
    up_part = jnp.dot(normed_two, up_w, preferred_element_type=f32)
    active, active_pull = jax.vjp(swiglu, gate, up_part)
    hidden = active.astype(bf16)
    branch = lax.psum(
        jnp.dot(hidden, down_w, preferred_element_type=f32).astype(jnp.bfloat16), "head"
    ).astype(jnp.float32)
    result = (middle + branch).astype(bf16)
    grad_down = jnp.dot(hidden.T, upstream, preferred_element_type=f32)
    d_hidden = jnp.dot(upstream, down_w.T, preferred_element_type=f32)
    d_gate_f, d_up_f = active_pull(d_hidden)
    d_gate = d_gate_f.astype(bf16)
    d_up = d_up_f.astype(bf16)
    grad_gate = jnp.dot(normed_two.T, d_gate, preferred_element_type=f32)
    grad_up = jnp.dot(normed_two.T, d_up, preferred_element_type=f32)
    d_normed_two = lax.psum(
        jnp.dot(d_gate, gate_w.T, preferred_element_type=f32)
        + jnp.dot(d_up, up_w.T, preferred_element_type=f32),
        "head",
    )
    d_middle_norm, grad_gain2 = norm_two_pull(d_normed_two)
    d_middle = upstream.astype(f32) + d_middle_norm
    d_attended = d_middle.astype(bf16)
    grad_out = jnp.dot(heads_out.T, d_attended, preferred_element_type=f32)
    d_heads = jnp.transpose(
        jnp.dot(d_attended, out_w.T, preferred_element_type=f32).reshape(count, -1, DV), (1, 0, 2)
    )
    d_numer = (d_heads / denom[..., None]).astype(bf16)
    d_denom = -jnp.sum(d_heads * ratio, axis=-1) / denom
    d_numer_wide = d_numer.astype(f32)
    d_before = jnp.einsum("htf,htd->hfd", query_wide, d_numer_wide, precision=highest)
    d_total_before = jnp.einsum("htf,ht->hf", query_wide, d_denom, precision=highest)
    d_state, d_total = entering(
        (d_before, d_total_before),
        "seq",
        add_pair,
        (jnp.zeros_like(d_before), jnp.zeros_like(d_total_before)),
        True,
    )
    d_scores = (
        (
            jnp.einsum("htd,hsd->hts", d_numer, value_heads, preferred_element_type=f32)
            + d_denom[..., None]
        )
        * causal
    ).astype(bf16)
    d_values = jnp.einsum(
        "hts,htd->hsd", weighted, d_numer, preferred_element_type=f32
    ) + jnp.einsum("hsf,hfd->hsd", key_feat.astype(f32), d_state, precision=highest)
    d_query_feat = (
        jnp.einsum("hts,hsf->htf", d_scores, key_feat, preferred_element_type=f32)
        + jnp.einsum("htd,hfd->htf", d_numer_wide, state_before, precision=highest)
        + d_denom[..., None] * total_before[:, None, :]
    )
    d_key_feat = (
        jnp.einsum("hts,htf->hsf", d_scores, query_feat, preferred_element_type=f32)
        + jnp.einsum("hsd,hfd->hsf", value_heads.astype(f32), d_state, precision=highest)
        + d_total[:, None, :]
    )
    d_queries = query_pull(jnp.transpose(round_trip(d_query_feat), (1, 0, 2)))[0].astype(bf16)
    d_keys = key_pull(jnp.transpose(round_trip(d_key_feat), (1, 0, 2)))[0].astype(bf16)
    d_values_flat = jnp.transpose(d_values, (1, 0, 2)).reshape(count, -1).astype(bf16)
    grad_query = jnp.dot(normed.T, d_queries, preferred_element_type=f32)
    grad_key = jnp.dot(normed.T, d_keys, preferred_element_type=f32)
    grad_value = jnp.dot(normed.T, d_values_flat, preferred_element_type=f32)
    d_normed_part = (
        jnp.dot(d_queries, query_w.T, preferred_element_type=f32)
        + jnp.dot(d_keys, key_w.T, preferred_element_type=f32)
        + jnp.dot(d_values_flat, value_w.T, preferred_element_type=f32)
    )
    d_normed = lax.psum(d_normed_part.astype(jnp.bfloat16), "head").astype(jnp.float32)
    d_stream_norm, grad_gain1 = norm_one_pull(d_normed)
    input_grad = (d_middle + d_stream_norm).astype(bf16)
    return (
        result,
        input_grad,
        grad_gain1,
        grad_query,
        grad_key,
        grad_value,
        grad_out,
        grad_gain2,
        grad_gate,
        grad_up,
        grad_down,
    )


def local(
    inputs, norm_gain1, w_query, w_key, w_value, w_out, norm_gain2, w_gate, w_up, w_down, cotangent
):
    micro = inputs.shape[0]
    summed = None
    results = []
    input_grads = []
    for step_index in range(micro):
        gathered = (
            lax.all_gather(norm_gain1, "seq", axis=0, tiled=True),
            lax.all_gather(w_query, "seq", axis=0, tiled=True),
            lax.all_gather(w_key, "seq", axis=0, tiled=True),
            lax.all_gather(w_value, "seq", axis=0, tiled=True),
            lax.all_gather(w_out, "seq", axis=1, tiled=True),
            lax.all_gather(norm_gain2, "seq", axis=0, tiled=True),
            lax.all_gather(w_gate, "seq", axis=0, tiled=True),
            lax.all_gather(w_up, "seq", axis=0, tiled=True),
            lax.all_gather(w_down, "seq", axis=1, tiled=True),
        )
        (
            result,
            input_grad,
            grad_gain1,
            grad_query,
            grad_key,
            grad_value,
            grad_out,
            grad_gain2,
            grad_gate,
            grad_up,
            grad_down,
        ) = block_pass(inputs[step_index], cotangent[step_index], gathered)
        results.append(result)
        input_grads.append(input_grad)
        fresh = (
            lax.psum_scatter(grad_gain1, "seq", scatter_dimension=0, tiled=True),
            lax.psum_scatter(grad_query, "seq", scatter_dimension=0, tiled=True),
            lax.psum_scatter(grad_key, "seq", scatter_dimension=0, tiled=True),
            lax.psum_scatter(grad_value, "seq", scatter_dimension=0, tiled=True),
            lax.psum_scatter(grad_out, "seq", scatter_dimension=1, tiled=True),
            lax.psum_scatter(grad_gain2, "seq", scatter_dimension=0, tiled=True),
            lax.psum_scatter(grad_gate, "seq", scatter_dimension=0, tiled=True),
            lax.psum_scatter(grad_up, "seq", scatter_dimension=0, tiled=True),
            lax.psum_scatter(grad_down, "seq", scatter_dimension=1, tiled=True),
        )
        summed = (
            fresh
            if summed is None
            else tuple((older + newer for older, newer in zip(summed, fresh)))
        )
    return (
        jnp.stack(results),
        jnp.stack(input_grads),
        summed[0],
        summed[1],
        summed[2],
        summed[3],
        summed[4],
        summed[5],
        summed[6],
        summed[7],
        summed[8],
    )


def solution(mesh):
    return jax.shard_map(
        local,
        mesh=mesh,
        in_specs=(
            P(None, "seq", None),
            P("seq"),
            P("seq", "head"),
            P("seq", "head"),
            P("seq", "head"),
            P("head", "seq"),
            P("seq"),
            P("seq", "head"),
            P("seq", "head"),
            P("head", "seq"),
            P(None, "seq", None),
        ),
        out_specs=(
            P(None, "seq", None),
            P(None, "seq", None),
            P("seq"),
            P("seq", "head"),
            P("seq", "head"),
            P("seq", "head"),
            P("head", "seq"),
            P("seq"),
            P("seq", "head"),
            P("seq", "head"),
            P("head", "seq"),
        ),
        check_vma=False,
    )
```

profile of v0, /device:TPU:0, one launch (start us, length us, event | category | flops | bytes accessed | tf_op | source)
XLA Modules:
  0.0 4330.8 jit_solution(3564727050307700977)
XLA Ops:
  8.0 42.4 all-gather.8
  50.4 42.0 all_gather.86
  107.9 73.6 %all_gather.85 = bf16[2048,128]{1,0:T(8,128)(2,1)S(1)} all-gather(bf16[128,128]{1,0:T(8,128)(2,1)S(1)} %copy-done.115), channel_id=1, replica_groups=mesh['seq'=16,'head'=2] {'seq'}, dimensions={0}, use_global_device_ids=true | all-gather | bytes 557056 | tf_op jit(solution)/shard_map/all_gather | solution.py:190
  186.0 55.2 %all-gather.3 = f32[128,273]{1,0:T(8,128)} all-gather(f32[8,273]{1,0:T(8,128)S(1)} %get-tuple-element.294), channel_id=5, replica_groups=mesh['seq'=16,'head'=2] {'seq'}, dimensions={0}, use_global_device_ids=true | all-gather | bytes 148512 | tf_op jit(solution)/shard_map/all_gather | solution.py:18
  241.1 51.5 %all-gather.1 = f32[128,273]{1,0:T(8,128)} all-gather(f32[8,273]{1,0:T(8,128)S(1)} %get-tuple-element.293), channel_id=3, replica_groups=mesh['seq'=16,'head'=2] {'seq'}, dimensions={0}, use_global_device_ids=true | all-gather | bytes 148512 | tf_op jit(solution)/shard_map/all_gather | solution.py:18
  298.3 190.1 %all-gather.32.cloned.1.call-done = f32[128,273,128]{2,0,1:T(8,128)} async-done(((f32[8,273,128]{2,0,1:T(8,128)}), f32[128,273,128]{2,0,1:T(8,128)}) %all-gather.32.cloned.1.call-update) | async-done | bytes 17891344 | tf_op jit(solution)/shard_map/all_gather | solution.py:18
  488.8 372.5 %all-gather.30.cloned.1.call-done = f32[128,273,128]{2,0,1:T(8,128)} async-done(((f32[8,273,128]{2,0,1:T(8,128)}), f32[128,273,128]{2,0,1:T(8,128)}) %all-gather.30.cloned.1.call-update) | async-done | bytes 17891344 | tf_op jit(solution)/shard_map/all_gather | solution.py:18
  861.5 11.8 while.52
  881.1 73.2 %all-gather.22.cloned.1.call-done = bf16[1024,2048]{1,0:T(8,128)(2,1)} async-done(((bf16[1024,128]{1,0:T(8,128)(2,1)}), bf16[1024,2048]{1,0:T(8,128)(2,1)}) %all-gather.22.cloned.1.call-update) | async-done | bytes 4194320 | tf_op jit(solution)/shard_map/all_gather | solution.py:193
  962.3 37.6 all-gather.9
  1003.1 123.0 %all-gather.24.cloned.1.call-done = bf16[2048,2816]{1,0:T(8,128)(2,1)} async-done(((bf16[128,2816]{1,0:T(8,128)(2,1)}), bf16[2048,2816]{1,0:T(8,128)(2,1)}) %all-gather.24.cloned.1.call-update) | async-done | bytes 11534352 | tf_op jit(solution)/shard_map/all_gather | solution.py:195
  1133.2 136.5 %all-gather.26.cloned.1.call-done = bf16[2048,2816]{1,0:T(8,128)(2,1)} async-done(((bf16[128,2816]{1,0:T(8,128)(2,1)}), bf16[2048,2816]{1,0:T(8,128)(2,1)}) %all-gather.26.cloned.1.call-update) | async-done | bytes 11534352 | tf_op jit(solution)/shard_map/all_gather | solution.py:196
  1285.2 168.3 %all-gather.28.cloned.1.call-done = bf16[2816,2048]{1,0:T(8,128)(2,1)} async-done(((bf16[2816,128]{1,0:T(8,128)(2,1)}), bf16[2816,2048]{1,0:T(8,128)(2,1)}) %all-gather.28.cloned.1.call-update) | async-done | bytes 11534352 | tf_op jit(solution)/shard_map/all_gather | solution.py:197
  1453.5 10.5 multiply_convert_fusion
  1474.0 11.2 multiply_convert_fusion.1
  1508.4 19.6 all-reduce.10.cloned.1.call-done
  1562.0 51.1 %all-gather.7 = f32[128,273]{1,0:T(8,128)} all-gather(f32[8,273]{1,0:T(8,128)S(1)} %bitcast.505), channel_id=9, replica_groups=mesh['seq'=16,'head'=2] {'seq'}, dimensions={0}, use_global_device_ids=true | all-gather | bytes 148512 | tf_op jit(solution)/shard_map/all_gather | solution.py:18
  1613.1 59.5 %all-gather.5 = f32[128,273]{1,0:T(8,128)} all-gather(f32[8,273]{1,0:T(8,128)S(1)} %bitcast.506), channel_id=7, replica_groups=mesh['seq'=16,'head'=2] {'seq'}, dimensions={0}, use_global_device_ids=true | all-gather | bytes 148512 | tf_op jit(solution)/shard_map/all_gather | solution.py:18
  1682.6 234.1 %all-gather.36.cloned.1.call-done = f32[128,273,128]{2,0,1:T(8,128)} async-done(((f32[8,273,128]{2,0,1:T(8,128)}), f32[128,273,128]{2,0,1:T(8,128)}) %all-gather.36.cloned.1.call-update) | async-done | bytes 17891344 | tf_op jit(solution)/shard_map/all_gather | solution.py:18
  1916.8 35.3 while.55
  1957.7 331.4 %all-gather.34.cloned.1.call-done = f32[128,273,128]{2,0,1:T(8,128)} async-done(((f32[8,273,128]{2,0,1:T(8,128)}), f32[128,273,128]{2,0,1:T(8,128)}) %all-gather.34.cloned.1.call-update) | async-done | bytes 17891344 | tf_op jit(solution)/shard_map/all_gather | solution.py:18
  2289.2 35.6 while.54
  2361.5 14.9 convolution_add_fusion.2
  2387.0 15.1 convolution_add_fusion.1
  2413.1 15.1 convolution_add_fusion
  2439.3 77.4 %all-reduce.2 = (f32[2048]{0:T(1024)S(1)}, f32[2048]{0:T(1024)S(1)}) all-reduce(f32[2048]{0:T(1024)S(1)} %add.389, f32[2048]{0:T(1024)S(1)} %add.394), channel_id=19, replica_groups=mesh['seq'=16,'head'=2] {'seq'}, use_global_device_ids=true, to_apply=%region_39.40.clone | all-reduce | flops 4096 | bytes 32768
  2523.2 93.1 %reduce-scatter.14.cloned.1.call-done = f32[1024,128]{1,0:T(8,128)} async-done(((f32[1024,2048]{1,0:T(8,128)}), f32[1024,128]{1,0:T(8,128)}) %reduce-scatter.14.cloned.1.call-update) | async-done | bytes 524304 | tf_op jit(solution)/shard_map/reduce_scatter | solution.py:219
  2616.3 82.5 %reduce-scatter.10.cloned.1.call-done = f32[128,128]{1,0:T(8,128)} async-done(((f32[2048,128]{1,0:T(8,128)}), f32[128,128]{1,0:T(8,128)}) %reduce-scatter.10.cloned.1.call-update) | async-done | bytes 65552 | tf_op jit(solution)/shard_map/reduce_scatter | solution.py:217
  2698.8 472.4 %reduce-scatter.16.cloned.1.call-done = f32[128,2816]{1,0:T(8,128)} async-done(((f32[2048,2816]{1,0:T(8,128)}), f32[128,2816]{1,0:T(8,128)}) %reduce-scatter.16.cloned.1.call-update) | async-done | bytes 1441808 | tf_op jit(solution)/shard_map/reduce_scatter | solution.py:221
  3171.1 482.6 %reduce-scatter.18.cloned.1.call-done = f32[128,2816]{1,0:T(8,128)} async-done(((f32[2048,2816]{1,0:T(8,128)}), f32[128,2816]{1,0:T(8,128)}) %reduce-scatter.18.cloned.1.call-update) | async-done | bytes 1441808 | tf_op jit(solution)/shard_map/reduce_scatter | solution.py:222
  3653.8 482.6 %reduce-scatter.20.cloned.1.call-done = f32[2816,128]{1,0:T(8,128)} async-done(((f32[2816,2048]{1,0:T(8,128)}), f32[2816,128]{1,0:T(8,128)}) %reduce-scatter.20.cloned.1.call-update) | async-done | bytes 1441808 | tf_op jit(solution)/shard_map/reduce_scatter | solution.py:223
  4136.4 187.6 %reduce-scatter.12.cloned.1.call-done = f32[128,1024]{1,0:T(8,128)} async-done(((f32[2048,1024]{1,0:T(8,128)}), f32[128,1024]{1,0:T(8,128)}) %reduce-scatter.12.cloned.1.call-update) | async-done | bytes 524304 | tf_op jit(solution)/shard_map/reduce_scatter | solution.py:218
  (549 shorter events, 295.0 us)
Async XLA Ops:
  7.2 85.4 %copy-start.7 = (bf16[2,128,2048]{2,1,0:T(8,128)(2,1)S(1)}, bf16[2,128,2048]{2,1,0:T(8,128)(2,1)}, u32[]{:S(2)}) copy-start(bf16[2,128,2048]{2,1,0:T(8,128)(2,1)} %param.19) | copy-start | bytes 3145732
  7.2 88.0 %all-gather.20.cloned.1.call-start = ((), (), s32[]{:S(2)}) async-start(), calls=%async_computation.7 | async-start | bytes 4456448 | tf_op jit(solution)/shard_map/all_gather | solution.py:192
  7.9 480.4 %all-gather.32.cloned.1.call-start = ((), (), s32[]{:S(2)}) async-start(), calls=%async_computation.13 | async-start | bytes 19009536 | tf_op jit(solution)/shard_map/all_gather | solution.py:18
  92.9 89.9 %copy-start.120 = (f32[128]{0:T(128)}, f32[128]{0:T(128)S(1)}, u32[]{:S(2)}) copy-start(f32[128]{0:T(128)S(1)} %fusion.142) | copy-start | bytes 1540
  93.5 200.7 %copy-start.34 = (bf16[128,8,16,16]{0,3,2,1:T(8,128)(2,1)}, bf16[128,8,16,16]{0,3,2,1:T(8,128)(2,1)S(1)}, u32[]{:S(2)}) copy-start(bf16[128,8,16,16]{0,3,2,1:T(8,128)(2,1)S(1)} %multiply_convert_fusion.5) | copy-start | bytes 1572868
  99.9 761.4 %all-gather.30.cloned.1.call-start = ((), (), s32[]{:S(2)}) async-start(), calls=%async_computation.12 | async-start | bytes 19009536 | tf_op jit(solution)/shard_map/all_gather | solution.py:18
  101.4 193.4 %copy-start.96 = (bf16[128,8,16]{0,2,1:T(8,128)(2,1)}, bf16[128,8,16]{0,2,1:T(8,128)(2,1)S(1)}, u32[]{:S(2)}) copy-start(bf16[128,8,16]{0,2,1:T(8,128)(2,1)S(1)} %get-tuple-element.385) | copy-start | bytes 98308
  101.6 193.2 %copy-start.32 = (bf16[128,8,16,16]{0,3,2,1:T(8,128)(2,1)}, bf16[128,8,16,16]{0,3,2,1:T(8,128)(2,1)S(1)}, u32[]{:S(2)}) copy-start(bf16[128,8,16,16]{0,3,2,1:T(8,128)(2,1)S(1)} %multiply_convert_fusion.8) | copy-start | bytes 1572868
  107.2 847.1 %all-gather.22.cloned.1.call-start = ((), (), s32[]{:S(2)}) async-start(), calls=%async_computation.8 | async-start | bytes 4456448 | tf_op jit(solution)/shard_map/all_gather | solution.py:193
  107.8 892.2 %all-reduce.12.cloned.1.call-start = ((), (), s32[]{:S(2)}) async-start(), calls=%async_computation.24 | async-start | bytes 4194304 | tf_op jit(solution)/shard_map/psum | solution.py:88
  294.2 194.3 %copy-start.20 = (bf16[8,128,273]{1,2,0:T(8,128)(2,1)}, bf16[8,128,273]{1,2,0:T(8,128)(2,1)S(1)}, u32[]{:S(2)}) copy-start(bf16[8,128,273]{1,2,0:T(8,128)(2,1)S(1)} %get-tuple-element.378) | copy-start | bytes 1677316
  488.4 373.0 %copy-start.90 = (f32[8,273]{1,0:T(8,128)}, f32[8,273]{1,0:T(8,128)S(1)}, u32[]{:S(2)}) copy-start(f32[8,273]{1,0:T(8,128)S(1)} %get-tuple-element.244) | copy-start | bytes 26212
  488.5 386.8 %copy-start.1 = (f32[8,273,128]{2,1,0:T(8,128)}, f32[8,273,128]{2,1,0:T(8,128)S(1)}, u32[]{:S(2)}) copy-start(f32[8,273,128]{2,1,0:T(8,128)S(1)} %get-tuple-element.243) | copy-start | bytes 3354628
  960.1 166.0 %all-gather.24.cloned.1.call-start = ((), (), s32[]{:S(2)}) async-start(), calls=%async_computation.9 | async-start | bytes 12255232 | tf_op jit(solution)/shard_map/all_gather | solution.py:195
  960.7 308.9 %all-gather.26.cloned.1.call-start = ((), (), s32[]{:S(2)}) async-start(), calls=%async_computation.10 | async-start | bytes 12255232 | tf_op jit(solution)/shard_map/all_gather | solution.py:196
  961.5 492.0 %all-gather.28.cloned.1.call-start = ((), (), s32[]{:S(2)}) async-start(), calls=%async_computation.11 | async-start | bytes 12255232 | tf_op jit(solution)/shard_map/all_gather | solution.py:197
  962.2 565.8 %all-reduce.10.cloned.1.call-start = ((), (), s32[]{:S(2)}) async-start(), calls=%async_computation.23 | async-start | bytes 4194304 | tf_op jit(solution)/shard_map/psum | solution.py:107
  1001.9 529.0 %copy-start.11 = (f32[128,2048]{1,0:T(8,128)}, f32[128,2048]{1,0:T(8,128)S(1)}, u32[]{:S(2)}) copy-start(f32[128,2048]{1,0:T(8,128)S(1)} %get-tuple-element.354) | copy-start | bytes 3145732
  1003.1 266.5 %copy-start.9 = (bf16[128,2048]{1,0:T(8,128)(2,1)}, bf16[128,2048]{1,0:T(8,128)(2,1)S(1)}, u32[]{:S(2)}) copy-start(bf16[128,2048]{1,0:T(8,128)(2,1)S(1)} %get-tuple-element.372) | copy-start | bytes 1572868
  1003.1 277.4 %copy-start.23 = (bf16[128,2048]{1,0:T(8,128)(2,1)}, bf16[128,2048]{1,0:T(8,128)(2,1)S(1)}, u32[]{:S(2)}) copy-start(bf16[128,2048]{1,0:T(8,128)(2,1)S(1)} %get-tuple-element.371) | copy-start | bytes 1572868
  1282.3 171.2 %copy-start.45 = (bf16[2,128,2048]{2,1,0:T(8,128)(2,1)S(1)}, bf16[2,128,2048]{2,1,0:T(8,128)(2,1)}, u32[]{:S(2)}) copy-start(bf16[2,128,2048]{2,1,0:T(8,128)(2,1)} %param.29) | copy-start | bytes 3145732
  1508.4 408.3 %all-gather.36.cloned.1.call-start = ((), (), s32[]{:S(2)}) async-start(), calls=%async_computation.15 | async-start | bytes 19009536 | tf_op jit(solution)/shard_map/all_gather | solution.py:18
  1537.8 751.3 %all-gather.34.cloned.1.call-start = ((), (), s32[]{:S(2)}) async-start(), calls=%async_computation.14 | async-start | bytes 19009536 | tf_op jit(solution)/shard_map/all_gather | solution.py:18
  1544.3 892.7 %all-reduce.14.cloned.1.call-start = ((), (), s32[]{:S(2)}) async-start(), calls=%async_computation.25 | async-start | bytes 4194304 | tf_op jit(solution)/shard_map/psum | solution.py:96
  2337.6 185.6 %reduce-scatter.8.cloned.1.call-start = ((), (), s32[]{:S(2)}) async-start(), calls=%async_computation.16 | async-start | bytes 1114112 | tf_op jit(solution)/shard_map/reduce_scatter | solution.py:216
  2340.6 275.6 %reduce-scatter.14.cloned.1.call-start = ((), (), s32[]{:S(2)}) async-start(), calls=%async_computation.19 | async-start | bytes 8912896 | tf_op jit(solution)/shard_map/reduce_scatter | solution.py:219
  2347.6 351.2 %reduce-scatter.10.cloned.1.call-start = ((), (), s32[]{:S(2)}) async-start(), calls=%async_computation.17 | async-start | bytes 1114112 | tf_op jit(solution)/shard_map/reduce_scatter | solution.py:217
  2360.5 810.6 %reduce-scatter.16.cloned.1.call-start = ((), (), s32[]{:S(2)}) async-start(), calls=%async_computation.20 | async-start | bytes 24510464 | tf_op jit(solution)/shard_map/reduce_scatter | solution.py:221
  2376.5 1277.3 %reduce-scatter.18.cloned.1.call-start = ((), (), s32[]{:S(2)}) async-start(), calls=%async_computation.21 | async-start | bytes 24510464 | tf_op jit(solution)/shard_map/reduce_scatter | solution.py:222
  2402.2 1734.2 %reduce-scatter.20.cloned.1.call-start = ((), (), s32[]{:S(2)}) async-start(), calls=%async_computation.22 | async-start | bytes 24510464 | tf_op jit(solution)/shard_map/reduce_scatter | solution.py:223
  2428.2 1895.8 %reduce-scatter.12.cloned.1.call-start = ((), (), s32[]{:S(2)}) async-start(), calls=%async_computation.18 | async-start | bytes 8912896 | tf_op jit(solution)/shard_map/reduce_scatter | solution.py:218
  2435.2 82.7 %copy-start.124 = (f32[128]{0:T(128)S(1)}, f32[128]{0:T(128)}, u32[]{:S(2)}) copy-start(f32[128]{0:T(128)} %copy-done.123) | copy-start | bytes 1540
  (125 other events, 901.6 us)
Sparse Core Ops, SparseCore 0:
  10.8 84.3 all-gather.19
  100.0 388.2 all-gather.31
  490.4 370.9 all-gather.29
  863.9 90.3 all-gather.21
  960.3 19.4 all-reduce.11
  982.7 143.3 all-gather.23
  1129.2 140.3 all-gather.25
  1272.7 180.7 all-gather.27
  1508.5 19.4 all-reduce.9
  1538.0 378.7 all-gather.35
  1918.8 370.3 all-gather.33
  2337.7 17.2 all-reduce.13
  2357.9 78.7 reduce-scatter.7
  2439.5 176.7 reduce-scatter.13
  2618.9 79.7 reduce-scatter.9
  2701.6 469.4 reduce-scatter.15
  3174.0 479.7 reduce-scatter.17
  3656.6 479.7 reduce-scatter.19
  4139.4 184.5 reduce-scatter.11
where the time goes:
time: 4340 us; the launch traced here: 4330 us
  waiting for transfers between devices  3450 us (79%)
  blocking collectives  490 us (11%)
  matrix products  232 us (5%)
  local copies, waits for them, and re-layouts  70.8 us (2%)
  other arithmetic  52.7 us (1%)
    all_gather x4, waiting for transfers between devices, entering(): gathered = jax.tree.map(lambda a: lax.all_gather(a, axis), part)  1130 us
    reduce_scatter x1, waiting for transfers between devices, local(): lax.psum_scatter(grad_down, 'seq', scatter_dimension=1, tiled=True)  483 us
    reduce_scatter x1, waiting for transfers between devices, local(): lax.psum_scatter(grad_up, 'seq', scatter_dimension=0, tiled=True)  483 us
    reduce_scatter x1, waiting for transfers between devices, local(): lax.psum_scatter(grad_gate, 'seq', scatter_dimension=0, tiled=True)  472 us
    all_gather x4, blocking collectives, entering(): gathered = jax.tree.map(lambda a: lax.all_gather(a, axis), part)  217 us
    reduce_scatter x1, waiting for transfers between devices, local(): lax.psum_scatter(grad_value, 'seq', scatter_dimension=0, tiled=True)  188 us
    all_gather x1, waiting for transfers between devices, local(): lax.all_gather(w_down, 'seq', axis=1, tiled=True)  168 us
    all_gather x1, waiting for transfers between devices, local(): lax.all_gather(w_up, 'seq', axis=0, tiled=True)  136 us
  transfers between devices with their start and end apart: 19, of which 16 were waited for; matrix products, arithmetic and copies ran while one was open for 5% of the time, Pallas kernels for 0%

commit v1 on v0

--- a/solution.py
+++ b/solution.py
@@ -1,6 +1,8 @@
 import jax
 import jax.numpy as jnp
 from jax import lax
+from jax.experimental import pallas as pl
+from jax.experimental.pallas import tpu as pltpu
 from jax.sharding import PartitionSpec as P
 
 F = 16
@@ -242,9 +244,576 @@
     )
 
 
+MESH = pl.DeviceIdType.MESH
+bf16 = jnp.bfloat16
+f32 = jnp.float32
+ZED = 4
+VMEM_LIMIT = 60 * 1024 * 1024
+
+
+def where_am_i():
+    place = lax.axis_index("seq")
+    return place % 2, (place // 2) % 2, place // 4, lax.axis_index("head")
+
+
+def index_of(z, y, x):
+    return (z * 2 + y) * 2 + x
+
+
+def remote(src, dst, send, recv, place, head):
+    return pltpu.make_async_remote_copy(
+        src_ref=src, dst_ref=dst, send_sem=send, recv_sem=recv, device_id=(place, head),
+        device_id_type=MESH,
+    )
+
+
+def arrived(dst, send, recv, place, head):
+    remote(dst, dst, send, recv, place, head).wait_recv()
+
+
+def params():
+    return pltpu.CompilerParams(has_side_effects=True, vmem_limit_bytes=VMEM_LIMIT)
+
+
+ANY = pl.BlockSpec(memory_space=pl.ANY)
+VMEM = pl.BlockSpec(memory_space=pltpu.VMEM)
+DMA = pltpu.SemaphoreType.DMA
+ORDER = (0, 1, 3, 2)
+
+
+def gather_kernel(a, m, g, wa, wm, gg, ls, zs, zr, ps, pr, ds, dr):
+    x, y, z, h = where_am_i()
+    me = index_of(z, y, x)
+    at_x, at_y = index_of(z, y, 1 - x), index_of(z, 1 - y, x)
+    half = a.shape[1] // 2
+
+    def rows(zz, yy, xx):
+        return pl.ds(pl.multiple_of(index_of(zz, yy, xx) * 128, 128), 128)
+
+    mine = rows(z, y, x)
+    local = [
+        pltpu.make_async_copy(a, wa.at[mine], ls.at[0]),
+        pltpu.make_async_copy(m.at[z], wm.at[mine], ls.at[1]),
+        pltpu.make_async_copy(g, gg.at[z], ls.at[2]),
+    ]
+    for copy in local:
+        copy.start()
+    sends = []
+    for d in (1, 3, 2):
+        there = index_of((z + d) % ZED, y, x)
+        sends.append(remote(a, wa.at[mine], zs.at[0, d], zr.at[0, d], there, h))
+    for d in (1, 3, 2):
+        there = index_of((z + d) % ZED, y, x)
+        sends.append(remote(m.at[(z + d) % ZED], wm.at[mine], zs.at[1, d], zr.at[1, d], there, h))
+    for d in (1, 3, 2):
+        there = index_of((z + d) % ZED, y, x)
+        sends.append(remote(g.at[h], gg.at[z, h], zs.at[2, d], zr.at[2, d], there, h))
+    for copy in sends:
+        copy.start()
+    local[0].wait()
+    local[1].wait()
+    local[2].wait()
+    sets = [(0, wa, d) for d in ORDER] + [(1, wm, d) for d in ORDER]
+    late = []
+    for turn in range(len(sets) + 1):
+        if turn < len(sets):
+            kind, w, d = sets[turn]
+            zz = (z + ZED - d) % ZED
+            block = w.at[rows(zz, y, x)]
+            if d:
+                arrived(block, zs.at[kind, d], zr.at[kind, d], me, h)
+            for side, there in ((0, at_x), (1, at_y)):
+                copy = remote(block, block, ps.at[kind, d, side], pr.at[kind, d, side], there, h)
+                copy.start()
+                late.append(copy)
+        if turn > 0:
+            kind, w, d = sets[turn - 1]
+            zz = (z + ZED - d) % ZED
+            from_x, from_y = rows(zz, y, 1 - x), rows(zz, 1 - y, x)
+            arrived(w.at[from_x], ps.at[kind, d, 0], pr.at[kind, d, 0], me, h)
+            arrived(w.at[from_y], ps.at[kind, d, 1], pr.at[kind, d, 1], me, h)
+            left = w.at[from_y, pl.ds(0, half)]
+            right = w.at[from_x, pl.ds(half, half)]
+            for side, part, there in ((2, left, at_x), (3, right, at_y)):
+                copy = remote(part, part, ps.at[kind, d, side], pr.at[kind, d, side], there, h)
+                copy.start()
+                late.append(copy)
+    for d in (1, 3, 2):
+        zz = (z + ZED - d) % ZED
+        arrived(gg.at[zz, h], zs.at[2, d], zr.at[2, d], me, h)
+        copy = remote(gg.at[zz, h], gg.at[zz, h], ds.at[d], dr.at[d], me, 1 - h)
+        copy.start()
+        late.append(copy)
+    for kind, w, d in sets:
+        zz = (z + ZED - d) % ZED
+        corner = rows(zz, 1 - y, 1 - x)
+        arrived(w.at[corner, pl.ds(0, half)], ps.at[kind, d, 2], pr.at[kind, d, 2], me, h)
+        arrived(w.at[corner, pl.ds(half, half)], ps.at[kind, d, 3], pr.at[kind, d, 3], me, h)
+    for d in (1, 3, 2):
+        zz = (z + ZED - d) % ZED
+        arrived(gg.at[zz, 1 - h], ds.at[d], dr.at[d], me, 1 - h)
+    for copy in sends + late:
+        copy.wait_send()
+
+
+def gather_all(a, m, g):
+    depth, wide = 16 * a.shape[0], a.shape[1]
+    return pl.pallas_call(
+        gather_kernel,
+        out_shape=(
+            jax.ShapeDtypeStruct((depth, wide), bf16),
+            jax.ShapeDtypeStruct((depth, wide), bf16),
+            jax.ShapeDtypeStruct((ZED,) + g.shape, bf16),
+        ),
+        in_specs=[ANY] * 3,
+        out_specs=(ANY,) * 3,
+        scratch_shapes=[
+            DMA((3,)), DMA((3, 4)), DMA((3, 4)), DMA((2, 4, 4)), DMA((2, 4, 4)), DMA((4,)), DMA((4,)),
+        ],
+        compiler_params=params(),
+        name="gather_all",
+    )(a, m, g)
+
+
+def exchange_kernel(src, dst, ls, ss, rs):
+    x, y, z, h = where_am_i()
+    me = index_of(z, y, x)
+    local = pltpu.make_async_copy(src.at[me], dst.at[me], ls)
+    local.start()
+    copies = []
+    for d in range(1, 16):
+        there = (me + d) % 16
+        copies.append(remote(src.at[there], dst.at[me], ss.at[d], rs.at[d], there, h))
+    for copy in copies:
+        copy.start()
+    local.wait()
+    for d in range(1, 16):
+        arrived(dst.at[(me + 16 - d) % 16], ss.at[d], rs.at[d], me, h)
+    for copy in copies:
+        copy.wait_send()
+
+
+def exchange(blocks):
+    return pl.pallas_call(
+        exchange_kernel,
+        out_shape=jax.ShapeDtypeStruct(blocks.shape, blocks.dtype),
+        in_specs=[ANY],
+        out_specs=ANY,
+        scratch_shapes=[DMA, DMA((16,)), DMA((16,))],
+        compiler_params=params(),
+        name="exchange",
+    )(blocks)
+
+
+def norm_kernel(part, xin, middle, near, other, sem, zs, zr, ds, dr):
+    x, y, z, h = where_am_i()
+    me = index_of(z, y, x)
+    swap = remote(part, other, sem.at[0], sem.at[1], me, 1 - h)
+    swap.start()
+    swap.wait()
+
+    def one(mb):
+        def body(turn, carry):
+            row = pl.ds(pl.multiple_of(turn * 16, 16), 16)
+            mid = xin[mb, row, :].astype(f32) + (part[mb, row, :] + other[mb, row, :])
+            middle[mb, row, :] = mid
+            scale = lax.rsqrt(jnp.mean(mid * mid, axis=-1, keepdims=True) + epsilon)
+            near[z, mb, row, :] = (mid * scale).astype(bf16)
+            return carry
+
+        lax.fori_loop(0, 8, body, 0)
+
+    one(h)
+    copies = []
+    for d in (2, 1, 3):
+        there = index_of((z + d) % ZED, y, x)
+        copies.append(remote(near.at[z, h], near.at[z, h], zs.at[d], zr.at[d], there, h))
+    for copy in copies:
+        copy.start()
+    one(1 - h)
+    for d in (1, 3, 2):
+        zz = (z + ZED - d) % ZED
+        arrived(near.at[zz, h], zs.at[d], zr.at[d], me, h)
+        copy = remote(near.at[zz, h], near.at[zz, h], ds.at[d], dr.at[d], me, 1 - h)
+        copy.start()
+        copies.append(copy)
+    for d in (1, 3, 2):
+        zz = (z + ZED - d) % ZED
+        arrived(near.at[zz, 1 - h], ds.at[d], dr.at[d], me, 1 - h)
+    for copy in copies:
+        copy.wait_send()
+
+
+def norm_two(part, xin):
+    return pl.pallas_call(
+        norm_kernel,
+        out_shape=(
+            jax.ShapeDtypeStruct(part.shape, f32),
+            jax.ShapeDtypeStruct((ZED,) + part.shape, bf16),
+        ),
+        in_specs=[VMEM] * 2,
+        out_specs=(VMEM,) * 2,
+        scratch_shapes=[
+            pltpu.VMEM(part.shape, f32), DMA((2,)), DMA((4,)), DMA((4,)), DMA((4,)), DMA((4,)),
+        ],
+        compiler_params=params(),
+        name="norm_two",
+    )(part, xin)
+
+
+def combine_kernel(t, out, other, summed, landed, sem, zs, zr, ds, dr):
+    x, y, z, h = where_am_i()
+    me = index_of(z, y, x)
+    kinds = t.shape[0]
+    swaps = []
+    for d in (2, 1, 3, 0):
+        zz = (z + d) % ZED
+        for kind in range(kinds):
+            swaps.append(
+                remote(t.at[kind, zz, 1 - h], other.at[kind, zz], sem.at[0, kind, d], sem.at[1, kind, d], me, 1 - h)
+            )
+    for copy in swaps:
+        copy.start()
+    copies = []
+    for d in (2, 1, 3, 0):
+        zz = (z + d) % ZED
+        for kind in range(kinds):
+            arrived(other.at[kind, zz], sem.at[0, kind, d], sem.at[1, kind, d], me, h)
+
+            def add(turn, carry):
+                row = pl.ds(pl.multiple_of(turn * 16, 16), 16)
+                summed[kind, zz, row, :] = (
+                    t[kind, zz, h, row, :].astype(f32) + other[kind, zz, row, :].astype(f32)
+                ).astype(bf16)
+                return carry
+
+            lax.fori_loop(0, 8, add, 0)
+            if d:
+                copy = remote(
+                    summed.at[kind, zz], landed.at[kind, d], zs.at[kind, d], zr.at[kind, d],
+                    index_of(zz, y, x), h,
+                )
+                copy.start()
+                copies.append(copy)
+    for kind in range(kinds):
+        for d in (1, 3, 2):
+            arrived(landed.at[kind, d], zs.at[kind, d], zr.at[kind, d], me, h)
+
+        def total(turn, carry):
+            row = pl.ds(pl.multiple_of(turn * 16, 16), 16)
+            acc = summed[kind, z, row, :].astype(f32)
+            for d in (1, 2, 3):
+                acc = acc + landed[kind, d, row, :].astype(f32)
+            out[kind, h, row, :] = acc.astype(bf16)
+            return carry
+
+        lax.fori_loop(0, 8, total, 0)
+        copy = remote(out.at[kind, h], out.at[kind, h], ds.at[kind], dr.at[kind], me, 1 - h)
+        copy.start()
+        copies.append(copy)
+    for kind in range(kinds):
+        arrived(out.at[kind, 1 - h], ds.at[kind], dr.at[kind], me, 1 - h)
+    for copy in swaps + copies:
+        copy.wait_send()
+
+
+def combine(t):
+    kinds, _, mbs, count, wide = t.shape
+    return pl.pallas_call(
+        combine_kernel,
+        out_shape=jax.ShapeDtypeStruct((kinds, mbs, count, wide), bf16),
+        in_specs=[VMEM],
+        out_specs=VMEM,
+        scratch_shapes=[
+            pltpu.VMEM((kinds, ZED, count, wide), bf16),
+            pltpu.VMEM((kinds, ZED, count, wide), bf16),
+            pltpu.VMEM((kinds, ZED, count, wide), bf16),
+            DMA((2, kinds, 4)), DMA((kinds, 4)), DMA((kinds, 4)), DMA((kinds,)), DMA((kinds,)),
+        ],
+        compiler_params=params(),
+        name="combine",
+    )(t)
+
+
+def pair_kernel(part, out, other, sem):
+    x, y, z, h = where_am_i()
+    me = index_of(z, y, x)
+    swap = remote(part, other, sem.at[0], sem.at[1], me, 1 - h)
+    swap.start()
+    swap.wait()
+    out[...] = part[...] + other[...]
+
+
+def pair_sum(part):
+    return pl.pallas_call(
+        pair_kernel,
+        out_shape=jax.ShapeDtypeStruct(part.shape, part.dtype),
+        in_specs=[VMEM],
+        out_specs=VMEM,
+        scratch_shapes=[pltpu.VMEM(part.shape, part.dtype), DMA((2,))],
+        compiler_params=params(),
+        name="pair_sum",
+    )(part)
+
+
+def scatter_kernel(ga, gm, za, zm, r1x, r1y, r2x, r2y, f1, f2, fin, s1, q1, s2, q2, s3, q3):
+    x, y, z, h = where_am_i()
+    me = index_of(z, y, x)
+    at_x, at_y = index_of(z, y, 1 - x), index_of(z, 1 - y, x)
+    half = ga.shape[-1] // 2
+    low, high = pl.ds(0, half), pl.ds(half, half)
+    sets = [(0, ga, za, d) for d in (2, 1, 3, 0)] + [(1, gm, zm, d) for d in (2, 1, 3, 0)]
+    copies = []
+
+    def start(copy):
+        copy.start()
+        copies.append(copy)
+
+    for n, (kind, g, out, d) in enumerate(sets):
+        zz = (z + d) % ZED
+        start(remote(g.at[zz, :, 1 - x, :, low], r1x.at[n], s1.at[n, 0], q1.at[n, 0], at_x, h))
+        start(remote(g.at[zz, 1 - y, :, :, high], r1y.at[n], s1.at[n, 1], q1.at[n, 1], at_y, h))
+
+    def wide(turns):
+        return pl.ds(pl.multiple_of(turns * 16, 16), 16)
+
+    for turn in range(len(sets) + 1):
+        if turn < len(sets):
+            n = turn
+            kind, g, out, d = sets[n]
+            zz = (z + d) % ZED
+            arrived(r1x.at[n], s1.at[n, 0], q1.at[n, 0], me, h)
+            arrived(r1y.at[n], s1.at[n, 1], q1.at[n, 1], me, h)
+
+            def forward(i, carry):
+                row = wide(i)
+                f1[n, row, :] = (
+                    g[zz, 1 - y, x, row, low].astype(f32) + r1x[n, 1 - y, row, :].astype(f32)
+                ).astype(bf16)
+                f2[n, row, :] = (
+                    g[zz, y, 1 - x, row, high].astype(f32) + r1y[n, 1 - x, row, :].astype(f32)
+                ).astype(bf16)
+                return carry
+
+            lax.fori_loop(0, 8, forward, 0)
+            start(remote(f1.at[n], r2y.at[n], s2.at[n, 0], q2.at[n, 0], at_y, h))
+            start(remote(f2.at[n], r2x.at[n], s2.at[n, 1], q2.at[n, 1], at_x, h))
+        if turn > 0:
+            n = turn - 1
+            kind, g, out, d = sets[n]
+            zz = (z + d) % ZED
+            arrived(r2y.at[n], s2.at[n, 0], q2.at[n, 0], me, h)
+            arrived(r2x.at[n], s2.at[n, 1], q2.at[n, 1], me, h)
+            target = fin.at[n] if d else out.at[z]
+
+            def finish(i, carry):
+                row = wide(i)
+                target[row, low] = (
+                    g[zz, y, x, row, low].astype(f32)
+                    + r1x[n, y, row, :].astype(f32)
+                    + r2y[n, row, :].astype(f32)
+                ).astype(bf16)
+                target[row, high] = (
+                    g[zz, y, x, row, high].astype(f32)
+                    + r1y[n, x, row, :].astype(f32)
+                    + r2x[n, row, :].astype(f32)
+                ).astype(bf16)
+                return carry
+
+            lax.fori_loop(0, 8, finish, 0)
+            if d:
+                start(
+                    remote(fin.at[n], out.at[z], s3.at[kind, d], q3.at[kind, d], index_of(zz, y, x), h)
+                )
+    for kind, g, out, d in sets:
+        if d:
+            arrived(out.at[(z + ZED - d) % ZED], s3.at[kind, d], q3.at[kind, d], me, h)
+    for copy in copies:
+        copy.wait_send()
+
+
+def scatter_all(ga, gm):
+    wide = ga.shape[-1]
+    ga = ga.reshape(ZED, 2, 2, 128, wide)
+    gm = gm.reshape(ZED, 2, 2, 128, wide)
+    give = jax.ShapeDtypeStruct((ZED, 128, wide), bf16)
+    return pl.pallas_call(
+        scatter_kernel,
+        out_shape=(give, give),
+        in_specs=[VMEM] * 2,
+        out_specs=(VMEM,) * 2,
+        scratch_shapes=[
+            pltpu.VMEM((8, 2, 128, wide // 2), bf16),
+            pltpu.VMEM((8, 2, 128, wide // 2), bf16),
+            pltpu.VMEM((8, 128, wide // 2), bf16),
+            pltpu.VMEM((8, 128, wide // 2), bf16),
+            pltpu.VMEM((8, 128, wide // 2), bf16),
+            pltpu.VMEM((8, 128, wide // 2), bf16),
+            pltpu.VMEM((8, 128, wide), bf16),
+            DMA((8, 2)), DMA((8, 2)), DMA((8, 2)), DMA((8, 2)), DMA((2, 4)), DMA((2, 4)),
+        ],
+        compiler_params=params(),
+        name="scatter_all",
+    )(ga, gm)
+
+
+def mix(a, b, over):
+    return lax.dot_general(a, b, (over, ((), ())), preferred_element_type=f32)
+
+
+def attend(q_t, k_t, v):
+    count = v.shape[0]
+    s = mix(q_t, k_t, ((0,), (0,)))
+    causal = lax.broadcasted_iota(jnp.int32, (count, count), 0) >= lax.broadcasted_iota(
+        jnp.int32, (count, count), 1
+    )
+    scores = jnp.where(causal, 1.0 + s * (0.25 + s * (1.0 / 32.0)), 0.0)
+    weighted = scores.astype(bf16)
+    numer = mix(weighted, v, ((1,), (0,)))
+    denom = jnp.sum(weighted.astype(f32), axis=-1, keepdims=True)
+    return numer / denom, denom
+
+
+def attend_back(q_t, k_t, v, ratio, denom, d_heads):
+    count = v.shape[0]
+    s = mix(q_t, k_t, ((0,), (0,)))
+    causal = lax.broadcasted_iota(jnp.int32, (count, count), 0) >= lax.broadcasted_iota(
+        jnp.int32, (count, count), 1
+    )
+    weighted = jnp.where(causal, 1.0 + s * (0.25 + s * (1.0 / 32.0)), 0.0).astype(bf16)
+    d_numer = (d_heads / denom).astype(bf16)
+    d_denom = -jnp.sum(d_heads * ratio, axis=-1, keepdims=True) / denom
+    d_scores = mix(d_numer, v, ((1,), (1,))) + d_denom
+    d_s = jnp.where(causal, d_scores * (0.25 + s * (1.0 / 16.0)), 0.0).astype(bf16)
+    d_v = mix(weighted, d_numer, ((0,), (0,)))
+    d_q = mix(k_t, d_s, ((1,), (1,)))
+    d_k = mix(q_t, d_s, ((1,), (0,)))
+    return d_q, d_k, d_v
+
+
+def fast(
+    inputs, norm_gain1, w_query, w_key, w_value, w_out, norm_gain2, w_gate, w_up, w_down, cotangent
+):
+    mbs, count, wide = inputs.shape
+    heads = w_query.shape[1] // F
+    units = w_gate.shape[1] // ZED
+    room = -(-units // 128) * 128
+    qk, vv = 2 * heads * F, heads * DV
+    rows = w_query.shape[0]
+    gain1, gain2 = norm_gain1.astype(f32)[:, None], norm_gain2.astype(f32)[:, None]
+
+    def folded(weight, gain):
+        return (weight.astype(f32) * gain).astype(bf16)
+
+    a = jnp.concatenate(
+        [folded(w_query, gain1), folded(w_key, gain1), folded(w_value, gain1), w_out.T], axis=1
+    )
+
+    def cut(weight):
+        pieces = jnp.transpose(weight.reshape(rows, ZED, units), (1, 0, 2))
+        return jnp.pad(pieces, ((0, 0), (0, 0), (0, room - units)))
+
+    m = jnp.concatenate([cut(folded(w_gate, gain2)), cut(folded(w_up, gain2)), cut(w_down.T)], axis=2)
+    wa, wm, gg = gather_all(a, m, cotangent)
+    w_qk, w_v, w_o = wa[:, :qk], wa[:, qk : qk + vv], wa[:, qk + vv :]
+    w_g, w_u, w_d = wm[:, :room], wm[:, room : 2 * room], wm[:, 2 * room :]
+
+    stream = inputs.astype(f32).reshape(mbs * count, wide)
+    r1 = lax.rsqrt(jnp.mean(stream * stream, axis=-1, keepdims=True) + epsilon)
+    xh1 = (stream * r1).astype(bf16)
+    qk_t = mix(w_qk, xh1, ((0,), (1,))).astype(bf16)
+    qk_t = qk_t.reshape(2, heads, F, mbs, count).transpose(3, 1, 0, 2, 4).reshape(16, 2 * F, count)
+    val = mix(xh1, w_v, ((1,), (0,))).astype(bf16)
+    val = val.reshape(mbs, count, heads, DV).transpose(0, 2, 1, 3).reshape(16, count, DV)
+    got = exchange(jnp.concatenate([qk_t, val], axis=1))
+    q_t = got[:, :F].transpose(1, 0, 2).reshape(F, 16 * count)
+    k_t = got[:, F : 2 * F].transpose(1, 0, 2).reshape(F, 16 * count)
+    v = got[:, 2 * F :].reshape(16 * count, DV)
+    ratio, denom = attend(q_t, k_t, v)
+    back = exchange(ratio.astype(bf16).reshape(16, count, DV))
+    heads_out = back.reshape(mbs, heads, count, DV).transpose(0, 2, 1, 3).reshape(mbs * count, vv)
+    part = mix(heads_out, w_o, ((1,), (1,)))
+    middle, near = norm_two(part.reshape(mbs, count, wide), inputs)
+    middle = middle.reshape(mbs * count, wide)
+    many = ZED * mbs * count
+    n2 = near.reshape(many, wide)
+    up_g = gg.reshape(many, wide)
+    gate = mix(n2, w_g, ((1,), (0,)))
+    up = mix(n2, w_u, ((1,), (0,)))
+    d_hidden = mix(up_g, w_d, ((1,), (0,)))
+    sig = jax.nn.sigmoid(gate)
+    silu = gate * sig
+    hidden = (silu * up).astype(bf16)
+    d_gate = (d_hidden * up * sig * (1.0 + gate * (1.0 - sig))).astype(bf16)
+    d_up = (d_hidden * silu).astype(bf16)
+    branch = mix(hidden, w_d, ((1,), (1,))).astype(bf16)
+    d_n2 = (mix(d_gate, w_g, ((1,), (1,))) + mix(d_up, w_u, ((1,), (1,)))).astype(bf16)
+    both = combine(jnp.stack([d_n2, branch]).reshape(2, ZED, mbs, count, wide))
+    e2 = both[0].reshape(mbs * count, wide).astype(f32)
+    outputs = (middle + both[1].reshape(mbs * count, wide).astype(f32)).astype(bf16)
+    r2 = lax.rsqrt(jnp.mean(middle * middle, axis=-1, keepdims=True) + epsilon)
+    xh2 = middle * r2
+    d_middle = cotangent.reshape(mbs * count, wide).astype(f32) + r2 * (
+        e2 - xh2 * jnp.mean(e2 * xh2, axis=-1, keepdims=True)
+    )
+    d_att = d_middle.astype(bf16)
+    d_heads = mix(d_att, w_o, ((1,), (0,))).astype(bf16)
+    d_heads = d_heads.reshape(mbs, count, heads, DV).transpose(0, 2, 1, 3).reshape(16, count, DV)
+    d_heads = exchange(d_heads).reshape(16 * count, DV).astype(f32)
+    d_q, d_k, d_v = attend_back(q_t, k_t, v, ratio, denom, d_heads)
+    d_qk = jnp.concatenate([d_q, d_k], axis=0).astype(bf16)
+    d_qk = d_qk.reshape(2 * F, 16, count).transpose(1, 0, 2)
+    home = exchange(jnp.concatenate([d_qk, d_v.astype(bf16).reshape(16, count, DV)], axis=1))
+    d_qk = home[:, : 2 * F].reshape(mbs, heads, 2, F, count).transpose(0, 4, 2, 1, 3)
+    d_qk = d_qk.reshape(mbs * count, qk)
+    d_val = home[:, 2 * F :].reshape(mbs, heads, count, DV).transpose(0, 2, 1, 3)
+    d_val = d_val.reshape(mbs * count, vv)
+    e1 = pair_sum(mix(d_qk, w_qk, ((1,), (1,))) + mix(d_val, w_v, ((1,), (1,))))
+    xh1f = stream * r1
+    input_grad = (
+        d_middle + r1 * (e1 - xh1f * jnp.mean(e1 * xh1f, axis=-1, keepdims=True))
+    ).astype(bf16)
+    first = ((0,), (0,))
+    ga = jnp.concatenate(
+        [mix(xh1, d_qk, first), mix(xh1, d_val, first), mix(d_att, heads_out, first)], axis=1
+    ).astype(bf16)
+    gm = jnp.concatenate(
+        [mix(n2, d_gate, first), mix(n2, d_up, first), mix(up_g, hidden, first)], axis=1
+    ).astype(bf16)
+    za, zm = scatter_all(ga, gm)
+    za = jnp.sum(za.astype(f32), axis=0)
+    zm = zm.astype(f32)
+
+    def joined(piece):
+        return jnp.transpose(piece[:, :, :units], (1, 0, 2)).reshape(rows, ZED * units)
+
+    g_gate, g_up, g_down = joined(zm[:, :, :room]), joined(zm[:, :, room : 2 * room]), joined(zm[:, :, 2 * room :])
+    s_q, s_k, s_v = za[:, : qk // 2], za[:, qk // 2 : qk], za[:, qk : qk + vv]
+    g_gain1 = (
+        jnp.sum(w_query.astype(f32) * s_q, axis=1)
+        + jnp.sum(w_key.astype(f32) * s_k, axis=1)
+        + jnp.sum(w_value.astype(f32) * s_v, axis=1)
+    )
+    g_gain2 = jnp.sum(w_gate.astype(f32) * g_gate, axis=1) + jnp.sum(w_up.astype(f32) * g_up, axis=1)
+    gains = lax.psum(jnp.stack([g_gain1, g_gain2]), "head")
+    return (
+        outputs.reshape(mbs, count, wide),
+        input_grad.reshape(mbs, count, wide),
+        gains[0],
+        s_q * gain1,
+        s_k * gain1,
+        s_v * gain1,
+        za[:, qk + vv :].T,
+        gains[1],
+        g_gate * gain2,
+        g_up * gain2,
+        g_down.T,
+    )
+
+
 def solution(mesh):
     return jax.shard_map(
-        local,
+        fast if mesh.shape["seq"] == 16 else local,
         mesh=mesh,
         in_specs=(
             P(None, "seq", None),

time: 4340 us -> 1000 us (0.23)
  waiting for transfers between devices: 3450 us -> 0 us
  Pallas kernels: 0 us -> 721 us
  blocking collectives: 490 us -> 2.81 us
  matrix products: 232 us -> 123 us
    reduce_scatter x7 -> x0, waiting for transfers between devices: 1800 us -> none  [the longest x1 483 us: local(): lax.psum_scatter(grad_down, 'seq', scatter_dimension=1, tiled=True)]
    all_gather x9 -> x0, waiting for transfers between devices: 1630 us -> none  [the longest x4 1130 us: entering(): gathered = jax.tree.map(lambda a: lax.all_gather(a, axis), part)]
    pallas_call x0 -> x9, Pallas kernels: none -> 721 us  [the longest x1 232 us: gather_all(): pl.pallas_call(gather_kernel, out_shape=(jax.ShapeDtypeStruct((depth, wid...]
    all_gather x8 -> x0, blocking collectives: 413 us -> none  [the longest x4 217 us: entering(): gathered = jax.tree.map(lambda a: lax.all_gather(a, axis), part)]
    dot_general x70 -> x24, matrix products: 232 us -> 123 us  [mix(): return lax.dot_general(a, b, (over, ((), ())), preferred_element_type=f32)]
    unnamed x1 -> x0, blocking collectives: 77.4 us -> none
  transfers between devices with their start and end apart: 19 -> 0, of which waited for: 16 -> 0; matrix products, arithmetic and copies ran while one was open for 5% -> 0% of each run, Pallas kernels for 0% -> 0%
where the time goes in v1:
time: 1000 us; the launch traced here: 991 us
  Pallas kernels  721 us (72%)
  matrix products  123 us (12%)
  local copies, waits for them, and re-layouts  82.3 us (8%)
  other arithmetic  59.8 us (6%)
    pallas_call x1, Pallas kernels, gather_all(): pl.pallas_call(gather_kernel, out_shape=(jax.ShapeDtypeStruct((depth, wid...  232 us
    pallas_call x1, Pallas kernels, scatter_all(): pl.pallas_call(scatter_kernel, out_shape=(give, give), in_specs=[VMEM] *...  220 us
    dot_general x24, matrix products, mix(): return lax.dot_general(a, b, (over, ((), ())), preferred_element_type=f32)  123 us
    pallas_call x4, Pallas kernels, exchange(): pl.pallas_call(exchange_kernel, out_shape=jax.ShapeDtypeStruct(blocks.sha...  97.7 us
    pallas_call x1, Pallas kernels, combine(): pl.pallas_call(combine_kernel, out_shape=jax.ShapeDtypeStruct((kinds, mbs...  95.9 us
    pallas_call x1, Pallas kernels, norm_two(): pl.pallas_call(norm_kernel, out_shape=(jax.ShapeDtypeStruct(part.shape, f...  55.6 us
    dot_general x5, local copies, waits for them, and re-layouts, mix(): return lax.dot_general(a, b, (over, ((), ())), preferred_element_type=f32)  33.4 us
    pallas_call x1, Pallas kernels, pair_sum(): pl.pallas_call(pair_kernel, out_shape=jax.ShapeDtypeStruct(part.shape, pa...  20.3 us

profile of v1, /device:TPU:0, one launch (start us, length us, event | category | flops | bytes accessed | tf_op | source)
XLA Modules:
  0.0 991.1 jit_solution(16309739716837478774)
XLA Ops:
  14.7 231.5 %gather_all.1 = (bf16[2048,2304]{1,0:T(8,128)(2,1)}, bf16[2048,2304]{1,0:T(8,128)(2,1)}, bf16[4,2,128,2048]{3,2,1,0:T(8,128)(2,1)}) custom-call(bf16[128,2304]{1,0:T(8,128)(2,1)} %pad_maximum_fusion.5.a, bf16[4,128,2304]{2,1,0:T(8,128)(2,1)} %fusion.26.m, bf16[2,128,2048]{2,1,0:T(8,128)(2,1)} %g.1), custom_call_target="tpu_custom_call" | custom-call | tf_op jit(solution)/shard_map/gather_all/pallas_call | solution.py:361
  253.8 19.0 %exchange.4 = bf16[16,160,128]{2,1,0:T(8,128)(2,1)} custom-call(bf16[16,160,128]{2,1,0:T(8,128)(2,1)} %pad_maximum_fusion.3.src), custom_call_target="tpu_custom_call" | custom-call | tf_op jit(solution)/shard_map/exchange/pallas_call | solution.py:397
  273.7 8.1 fusion.77
  281.8 17.6 %copy.51 = f32[2048,2048]{1,0:T(8,128)} copy(f32[2048,2048]{0,1:T(8,128)} %fusion.77) | data formatting | bytes 33554432 | tf_op jit(solution)/shard_map/dot_general | solution.py:661
  299.3 9.3 convert_reduce_fusion
  312.7 20.8 %exchange.5 = bf16[16,128,128]{2,1,0:T(8,128)(2,1)} custom-call(bf16[16,128,128]{2,1,0:T(8,128)(2,1)} %bitcast.270), custom_call_target="tpu_custom_call" | custom-call | tf_op jit(solution)/shard_map/exchange/pallas_call | solution.py:397
  333.5 5.0 fusion.5.part
  338.5 55.6 %norm_two.1 = (f32[2,128,2048]{2,1,0:T(8,128)}, bf16[4,2,128,2048]{3,2,1,0:T(8,128)(2,1)}) custom-call(f32[2,128,2048]{2,1,0:T(8,128)} %fusion.5.part, bf16[2,128,2048]{2,1,0:T(8,128)(2,1)} %xin.1), custom_call_target="tpu_custom_call" | custom-call | tf_op jit(solution)/shard_map/norm_two/pallas_call | solution.py:448
  394.1 6.3 fusion.20
  404.3 5.7 multiply_convert_fusion.1
  410.0 6.4 copy.63
  416.4 8.0 convolution_convert_fusion.5
  424.4 4.8 convolution_convert_fusion.6
  429.2 5.9 fusion.15
  435.1 6.1 add_convert_fusion
  441.2 5.1 convolution_convert_fusion
  446.3 6.2 pad_maximum_fusion.2.t
  452.5 95.9 %combine.1 = bf16[2,2,128,2048]{3,2,1,0:T(8,128)(2,1)} custom-call(bf16[2,4,2,128,2048]{4,3,2,1,0:T(8,128)(2,1)} %pad_maximum_fusion.2.t), custom_call_target="tpu_custom_call" | custom-call | tf_op jit(solution)/shard_map/combine/pallas_call | solution.py:522
  559.1 4.8 convolution_convert_fusion.1
  569.8 36.8 %exchange.6 = bf16[16,128,128]{2,1,0:T(8,128)(2,1)} custom-call(bf16[16,128,128]{2,1,0:T(8,128)(2,1)} %bitcast.260), custom_call_target="tpu_custom_call" | custom-call | tf_op jit(solution)/shard_map/exchange/pallas_call | solution.py:397
  609.8 12.1 %fusion = (bf16[2048,2048]{1,0:T(8,128)(2,1)}, bf16[2048,2048]{0,1:T(8,128)(2,1)}) fusion(f32[2048,2048]{0,1:T(8,128)} %fusion.77, f32[2048]{0:T(1024)S(1)} %negate_divide_fusion, bf16[2048,128]{1,0:T(8,128)(2,1)S(1)} %bitcast.253, bf16[2048,128]{1,0:T(8,128)(2,1)S(1)} %bitcast.252), kind=kOutput, calls=%fused_computation.1 | convolution fusion | flops 1103101952 | bytes 34611200 | tf_op jit(solution)/shard_map/dot_general | solution.py:661
  621.9 12.3 %copy.56 = bf16[2048,2048]{1,0:T(8,128)(2,1)} copy(bf16[2048,2048]{0,1:T(8,128)(2,1)} %get-tuple-element.93) | data formatting | bytes 16777216 | tf_op jit(solution)/shard_map/mul | solution.py:687
  634.2 8.0 select_convert_fusion
  642.3 5.6 convolution_convert_fusion.10
  648.0 5.6 convolution_convert_fusion.9
  653.7 5.8 convolution_convert_fusion.3
  660.4 21.2 %exchange.7 = bf16[16,160,128]{2,1,0:T(8,128)(2,1)} custom-call(bf16[16,160,128]{2,1,0:T(8,128)(2,1)} %pad_maximum_fusion.4.src), custom_call_target="tpu_custom_call" | custom-call | tf_op jit(solution)/shard_map/exchange/pallas_call | solution.py:397
  689.9 6.5 copy.64
  696.3 6.3 convolution_convert_fusion.4
  703.3 6.8 pad_maximum_fusion
  710.1 220.3 %scatter_all.1 = (bf16[4,128,2304]{2,1,0:T(8,128)(2,1)}, bf16[4,128,2304]{2,1,0:T(8,128)(2,1)}) custom-call(bf16[4,2,2,128,2304]{4,3,2,1,0:T(8,128)(2,1)} %get-tuple-element.94.ga, bf16[4,2,2,128,2304]{4,3,2,1,0:T(8,128)(2,1)} %get-tuple-element.95.gm), custom_call_target="tpu_custom_call" | custom-call | tf_op jit(solution)/shard_map/scatter_all/pallas_call | solution.py:640
  966.8 20.3 %pair_sum.1 = f32[256,2048]{1,0:T(8,128)} custom-call(f32[256,2048]{1,0:T(8,128)} %convolution_add_fusion.part), custom_call_target="tpu_custom_call" | custom-call | tf_op jit(solution)/shard_map/pair_sum/pallas_call | solution.py:548
  (178 shorter events, 99.9 us)
Async XLA Ops:
  0.6 6.1 copy-start.30
  0.7 6.5 copy-start.39
  7.1 5.1 copy-start.14
  14.7 231.6 %copy-start = (bf16[2,128,2048]{2,1,0:T(8,128)(2,1)S(1)}, bf16[2,128,2048]{2,1,0:T(8,128)(2,1)}, u32[]{:S(2)}) copy-start(bf16[2,128,2048]{2,1,0:T(8,128)(2,1)} %xin.1) | copy-start | bytes 3145732
  299.3 9.3 copy-start.22
  338.5 61.9 %slice-start.1 = ((s8[9437184]{0:T(1024)(128)(4,1)}), s8[1048576]{0:T(1024)(128)(4,1)S(1)}, s32[]{:S(2)}) async-start(s8[9437184]{0:T(1024)(128)(4,1)} %bitcast.272), calls=%async_computation.1 | async-start | bytes 2097152
  394.1 6.3 copy-start.18
  394.1 6.3 slice-start.2
  394.1 6.8 slice-start.3
  416.4 8.0 copy-start.19
  416.4 12.8 %slice-start.4 = ((s8[9437184]{0:T(1024)(128)(4,1)}), s8[4194304]{0:T(1024)(128)(4,1)S(1)}, s32[]{:S(2)}) async-start(s8[9437184]{0:T(1024)(128)(4,1)} %bitcast.274), calls=%async_computation.4 | async-start | bytes 8388608
  416.4 12.8 %slice-start.5 = ((s8[9437184]{0:T(1024)(128)(4,1)}), s8[4194304]{0:T(1024)(128)(4,1)S(1)}, s32[]{:S(2)}) async-start(s8[9437184]{0:T(1024)(128)(4,1)} %bitcast.274), calls=%async_computation.5 | async-start | bytes 8388608
  424.4 4.8 slice-start.6
  429.2 5.9 copy-start.41
  435.1 6.1 copy-start.40
  452.5 95.9 %copy-start.2 = (f32[2,128,2048]{2,1,0:T(8,128)S(1)}, f32[2,128,2048]{2,1,0:T(8,128)}, u32[]{:S(2)}) copy-start(f32[2,128,2048]{2,1,0:T(8,128)} %get-tuple-element.19) | copy-start | bytes 6291460
  559.1 4.8 copy-start.5
  568.8 39.2 %copy-start.29 = (f32[2048,128]{1,0:T(8,128)S(1)}, f32[2048,128]{1,0:T(8,128)}, u32[]{:S(2)}) copy-start(f32[2048,128]{1,0:T(8,128)} %get-tuple-element.91) | copy-start | bytes 3145732
  568.8 41.0 %copy-start.25 = (bf16[16,128,128]{2,1,0:T(8,128)(2,1)S(1)}, bf16[16,128,128]{2,1,0:T(8,128)(2,1)}, u32[]{:S(2)}) copy-start(bf16[16,128,128]{2,1,0:T(8,128)(2,1)} %copy-done.24) | copy-start | bytes 1572868
  659.5 24.5 %copy-start.1 = (bf16[2,128,2048]{2,1,0:T(8,128)(2,1)S(1)}, bf16[2,128,2048]{2,1,0:T(8,128)(2,1)}, u32[]{:S(2)}) copy-start(bf16[2,128,2048]{2,1,0:T(8,128)(2,1)} %xin.1) | copy-start | bytes 3145732
  685.0 4.3 slice-start
  696.3 6.3 copy-start.6
  696.3 6.3 copy-start.7
  696.3 6.3 copy-start.20
  696.3 7.0 copy-start.21
  937.6 6.1 copy-start.13
  937.6 6.1 copy-start.15
  937.6 6.1 copy-start.38
  947.4 9.2 copy-start.16
  953.7 6.6 copy-start.27
  966.8 20.3 %copy-start.34 = (f32[256]{0:T(256)S(1)}, f32[256]{0:T(256)}, u32[]{:S(2)}) copy-start(f32[256]{0:T(256)} %copy-done.33) | copy-start | bytes 3076
  966.8 22.5 %copy-start.11 = (f32[256,2048]{1,0:T(8,128)S(1)}, f32[256,2048]{1,0:T(8,128)}, u32[]{:S(2)}) copy-start(f32[256,2048]{1,0:T(8,128)} %copy-done.10) | copy-start | bytes 6291460
  (17 other events, 45.1 us)

commit v2 on v1

--- a/solution.py
+++ b/solution.py
@@ -281,100 +281,6 @@
 ORDER = (0, 1, 3, 2)
 
 
-def gather_kernel(a, m, g, wa, wm, gg, ls, zs, zr, ps, pr, ds, dr):
-    x, y, z, h = where_am_i()
-    me = index_of(z, y, x)
-    at_x, at_y = index_of(z, y, 1 - x), index_of(z, 1 - y, x)
-    half = a.shape[1] // 2
-
-    def rows(zz, yy, xx):
-        return pl.ds(pl.multiple_of(index_of(zz, yy, xx) * 128, 128), 128)
-
-    mine = rows(z, y, x)
-    local = [
-        pltpu.make_async_copy(a, wa.at[mine], ls.at[0]),
-        pltpu.make_async_copy(m.at[z], wm.at[mine], ls.at[1]),
-        pltpu.make_async_copy(g, gg.at[z], ls.at[2]),
-    ]
-    for copy in local:
-        copy.start()
-    sends = []
-    for d in (1, 3, 2):
-        there = index_of((z + d) % ZED, y, x)
-        sends.append(remote(a, wa.at[mine], zs.at[0, d], zr.at[0, d], there, h))
-    for d in (1, 3, 2):
-        there = index_of((z + d) % ZED, y, x)
-        sends.append(remote(m.at[(z + d) % ZED], wm.at[mine], zs.at[1, d], zr.at[1, d], there, h))
-    for d in (1, 3, 2):
-        there = index_of((z + d) % ZED, y, x)
-        sends.append(remote(g.at[h], gg.at[z, h], zs.at[2, d], zr.at[2, d], there, h))
-    for copy in sends:
-        copy.start()
-    local[0].wait()
-    local[1].wait()
-    local[2].wait()
-    sets = [(0, wa, d) for d in ORDER] + [(1, wm, d) for d in ORDER]
-    late = []
-    for turn in range(len(sets) + 1):
-        if turn < len(sets):
-            kind, w, d = sets[turn]
-            zz = (z + ZED - d) % ZED
-            block = w.at[rows(zz, y, x)]
-            if d:
-                arrived(block, zs.at[kind, d], zr.at[kind, d], me, h)
-            for side, there in ((0, at_x), (1, at_y)):
-                copy = remote(block, block, ps.at[kind, d, side], pr.at[kind, d, side], there, h)
-                copy.start()
-                late.append(copy)
-        if turn > 0:
-            kind, w, d = sets[turn - 1]
-            zz = (z + ZED - d) % ZED
-            from_x, from_y = rows(zz, y, 1 - x), rows(zz, 1 - y, x)
-            arrived(w.at[from_x], ps.at[kind, d, 0], pr.at[kind, d, 0], me, h)
-            arrived(w.at[from_y], ps.at[kind, d, 1], pr.at[kind, d, 1], me, h)
-            left = w.at[from_y, pl.ds(0, half)]
-            right = w.at[from_x, pl.ds(half, half)]
-            for side, part, there in ((2, left, at_x), (3, right, at_y)):
-                copy = remote(part, part, ps.at[kind, d, side], pr.at[kind, d, side], there, h)
-                copy.start()
-                late.append(copy)
-    for d in (1, 3, 2):
-        zz = (z + ZED - d) % ZED
-        arrived(gg.at[zz, h], zs.at[2, d], zr.at[2, d], me, h)
-        copy = remote(gg.at[zz, h], gg.at[zz, h], ds.at[d], dr.at[d], me, 1 - h)
-        copy.start()
-        late.append(copy)
-    for kind, w, d in sets:
-        zz = (z + ZED - d) % ZED
-        corner = rows(zz, 1 - y, 1 - x)
-        arrived(w.at[corner, pl.ds(0, half)], ps.at[kind, d, 2], pr.at[kind, d, 2], me, h)
-        arrived(w.at[corner, pl.ds(half, half)], ps.at[kind, d, 3], pr.at[kind, d, 3], me, h)
-    for d in (1, 3, 2):
-        zz = (z + ZED - d) % ZED
-        arrived(gg.at[zz, 1 - h], ds.at[d], dr.at[d], me, 1 - h)
-    for copy in sends + late:
-        copy.wait_send()
-
-
-def gather_all(a, m, g):
-    depth, wide = 16 * a.shape[0], a.shape[1]
-    return pl.pallas_call(
-        gather_kernel,
-        out_shape=(
-            jax.ShapeDtypeStruct((depth, wide), bf16),
-            jax.ShapeDtypeStruct((depth, wide), bf16),
-            jax.ShapeDtypeStruct((ZED,) + g.shape, bf16),
-        ),
-        in_specs=[ANY] * 3,
-        out_specs=(ANY,) * 3,
-        scratch_shapes=[
-            DMA((3,)), DMA((3, 4)), DMA((3, 4)), DMA((2, 4, 4)), DMA((2, 4, 4)), DMA((4,)), DMA((4,)),
-        ],
-        compiler_params=params(),
-        name="gather_all",
-    )(a, m, g)
-
-
 def exchange_kernel(src, dst, ls, ss, rs):
     x, y, z, h = where_am_i()
     me = index_of(z, y, x)
@@ -403,62 +309,6 @@
         compiler_params=params(),
         name="exchange",
     )(blocks)
-
-
-def norm_kernel(part, xin, middle, near, other, sem, zs, zr, ds, dr):
-    x, y, z, h = where_am_i()
-    me = index_of(z, y, x)
-    swap = remote(part, other, sem.at[0], sem.at[1], me, 1 - h)
-    swap.start()
-    swap.wait()
-
-    def one(mb):
-        def body(turn, carry):
-            row = pl.ds(pl.multiple_of(turn * 16, 16), 16)
-            mid = xin[mb, row, :].astype(f32) + (part[mb, row, :] + other[mb, row, :])
-            middle[mb, row, :] = mid
-            scale = lax.rsqrt(jnp.mean(mid * mid, axis=-1, keepdims=True) + epsilon)
-            near[z, mb, row, :] = (mid * scale).astype(bf16)
-            return carry
-
-        lax.fori_loop(0, 8, body, 0)
-
-    one(h)
-    copies = []
-    for d in (2, 1, 3):
-        there = index_of((z + d) % ZED, y, x)
-        copies.append(remote(near.at[z, h], near.at[z, h], zs.at[d], zr.at[d], there, h))
-    for copy in copies:
-        copy.start()
-    one(1 - h)
-    for d in (1, 3, 2):
-        zz = (z + ZED - d) % ZED
-        arrived(near.at[zz, h], zs.at[d], zr.at[d], me, h)
-        copy = remote(near.at[zz, h], near.at[zz, h], ds.at[d], dr.at[d], me, 1 - h)
-        copy.start()
-        copies.append(copy)
-    for d in (1, 3, 2):
-        zz = (z + ZED - d) % ZED
-        arrived(near.at[zz, 1 - h], ds.at[d], dr.at[d], me, 1 - h)
-    for copy in copies:
-        copy.wait_send()
-
-
-def norm_two(part, xin):
-    return pl.pallas_call(
-        norm_kernel,
-        out_shape=(
-            jax.ShapeDtypeStruct(part.shape, f32),
-            jax.ShapeDtypeStruct((ZED,) + part.shape, bf16),
-        ),
-        in_specs=[VMEM] * 2,
-        out_specs=(VMEM,) * 2,
-        scratch_shapes=[
-            pltpu.VMEM(part.shape, f32), DMA((2,)), DMA((4,)), DMA((4,)), DMA((4,)), DMA((4,)),
-        ],
-        compiler_params=params(),
-        name="norm_two",
-    )(part, xin)
 
 
 def combine_kernel(t, out, other, summed, landed, sem, zs, zr, ds, dr):
@@ -661,34 +511,356 @@
     return lax.dot_general(a, b, (over, ((), ())), preferred_element_type=f32)
 
 
-def attend(q_t, k_t, v):
-    count = v.shape[0]
-    s = mix(q_t, k_t, ((0,), (0,)))
-    causal = lax.broadcasted_iota(jnp.int32, (count, count), 0) >= lax.broadcasted_iota(
+CHUNK = 512
+COLS = 256
+
+
+def spread(got, q_t, k_t, va):
+    count = got.shape[2]
+    for b in range(got.shape[0]):
+        q_t[:, b * count : (b + 1) * count] = got[b, 0:F, :]
+        k_t[:, b * count : (b + 1) * count] = got[b, F : 2 * F, :]
+        va[b * count : (b + 1) * count, 0:DV] = got[b, 2 * F :, :]
+    va[:, DV:] = jnp.ones((va.shape[0], va.shape[1] - DV), bf16)
+
+
+def lower(count):
+    return lax.broadcasted_iota(jnp.int32, (count, count), 0) >= lax.broadcasted_iota(
         jnp.int32, (count, count), 1
     )
-    scores = jnp.where(causal, 1.0 + s * (0.25 + s * (1.0 / 32.0)), 0.0)
-    weighted = scores.astype(bf16)
-    numer = mix(weighted, v, ((1,), (0,)))
-    denom = jnp.sum(weighted.astype(f32), axis=-1, keepdims=True)
-    return numer / denom, denom
-
-
-def attend_back(q_t, k_t, v, ratio, denom, d_heads):
-    count = v.shape[0]
-    s = mix(q_t, k_t, ((0,), (0,)))
-    causal = lax.broadcasted_iota(jnp.int32, (count, count), 0) >= lax.broadcasted_iota(
-        jnp.int32, (count, count), 1
-    )
-    weighted = jnp.where(causal, 1.0 + s * (0.25 + s * (1.0 / 32.0)), 0.0).astype(bf16)
-    d_numer = (d_heads / denom).astype(bf16)
-    d_denom = -jnp.sum(d_heads * ratio, axis=-1, keepdims=True) / denom
-    d_scores = mix(d_numer, v, ((1,), (1,))) + d_denom
-    d_s = jnp.where(causal, d_scores * (0.25 + s * (1.0 / 16.0)), 0.0).astype(bf16)
-    d_v = mix(weighted, d_numer, ((0,), (0,)))
-    d_q = mix(k_t, d_s, ((1,), (1,)))
-    d_k = mix(q_t, d_s, ((1,), (0,)))
-    return d_q, d_k, d_v
+
+
+def attend_rows(qi, q_t, k_t, va, ratio, den, causal):
+    qs = slice(qi * CHUNK, (qi + 1) * CHUNK)
+    acc = jnp.zeros((CHUNK, va.shape[1]), f32)
+    for kj in range(qi + 1):
+        ks = slice(kj * CHUNK, (kj + 1) * CHUNK)
+        s = mix(q_t[:, qs], k_t[:, ks], ((0,), (0,)))
+        p = 1.0 + s * (0.25 + s * (1.0 / 32.0))
+        if kj == qi:
+            p = jnp.where(causal, p, 0.0)
+        acc = acc + mix(p.astype(bf16), va[ks, :], ((1,), (0,)))
+    ratio[qs, :] = acc[:, :DV] / acc[:, DV:]
+    den[qs, :] = acc[:, DV:]
+
+
+def front_kernel(
+    a1, a2, m, xh, xin,
+    wa1, wa2, wm, got, ratio, den, heads_out, middle, near,
+    w1, w2, pack, q_t, k_t, va, ob, part, other,
+    ls, zs, zr, ps, pr, e1s, e1r, e2s, e2r, ws, wr, ns, nr, ds, dr,
+):
+    x, y, z, h = where_am_i()
+    me = index_of(z, y, x)
+    at_x, at_y = index_of(z, y, 1 - x), index_of(z, 1 - y, x)
+    count = xin.shape[1]
+    heads = 16 // xin.shape[0]
+    late = []
+
+    def go(copy):
+        copy.start()
+        late.append(copy)
+
+    def rows(zz, yy, xx):
+        return pl.ds(pl.multiple_of(index_of(zz, yy, xx) * 128, 128), 128)
+
+    mine = rows(z, y, x)
+    kept = [
+        pltpu.make_async_copy(a1, w1.at[mine], ls.at[0]),
+        pltpu.make_async_copy(a2, w2.at[mine], ls.at[1]),
+        pltpu.make_async_copy(m.at[z], wm.at[mine], ls.at[2]),
+    ]
+    for copy in kept:
+        copy.start()
+    dest = (w1, w2, wm)
+
+    def line(kind):
+        for d in (1, 3, 2):
+            zz = (z + d) % ZED
+            src = (a1, a2, m.at[zz])[kind]
+            go(remote(src, dest[kind].at[mine], zs.at[kind, d], zr.at[kind, d], index_of(zz, y, x), h))
+
+    def plane(kind, d):
+        block = dest[kind].at[rows((z + ZED - d) % ZED, y, x)]
+        if d:
+            arrived(block, zs.at[kind, d], zr.at[kind, d], me, h)
+        else:
+            kept[kind].wait()
+        go(remote(block, block, ps.at[kind, d, 0], pr.at[kind, d, 0], at_x, h))
+        go(remote(block, block, ps.at[kind, d, 1], pr.at[kind, d, 1], at_y, h))
+
+    def onward(kind, d):
+        w = dest[kind]
+        zz = (z + ZED - d) % ZED
+        half = w.shape[1] // 2
+        from_x, from_y = rows(zz, y, 1 - x), rows(zz, 1 - y, x)
+        arrived(w.at[from_x], ps.at[kind, d, 0], pr.at[kind, d, 0], me, h)
+        arrived(w.at[from_y], ps.at[kind, d, 1], pr.at[kind, d, 1], me, h)
+        left = w.at[from_y, pl.ds(0, half)]
+        right = w.at[from_x, pl.ds(half, half)]
+        go(remote(left, left, ps.at[kind, d, 2], pr.at[kind, d, 2], at_x, h))
+        go(remote(right, right, ps.at[kind, d, 3], pr.at[kind, d, 3], at_y, h))
+
+    def corner(kind):
+        w = dest[kind]
+        half = w.shape[1] // 2
+        for d in ORDER:
+            far = rows((z + ZED - d) % ZED, 1 - y, 1 - x)
+            arrived(w.at[far, pl.ds(0, half)], ps.at[kind, d, 2], pr.at[kind, d, 2], me, h)
+            arrived(w.at[far, pl.ds(half, half)], ps.at[kind, d, 3], pr.at[kind, d, 3], me, h)
+
+    line(0)
+    plane(0, 0)
+    plane(0, 1)
+    onward(0, 0)
+    plane(0, 3)
+    line(1)
+    onward(0, 1)
+    plane(0, 2)
+    onward(0, 3)
+    plane(1, 0)
+    onward(0, 2)
+    corner(0)
+    out1 = pltpu.make_async_copy(w1, wa1, ls.at[3])
+    out1.start()
+    kq = mix(xh[...], w1[:, 0 : 2 * heads * F], ((1,), (0,)))
+    qk = jnp.transpose(kq).astype(bf16)
+    for mb in range(16 // heads):
+        for k in range(heads):
+            t = k + heads * mb
+            cols = slice(mb * count, (mb + 1) * count)
+            pack[t, 0:F, :] = qk[k * F : (k + 1) * F, cols]
+            pack[t, F : 2 * F, :] = qk[(heads + k) * F : (heads + k + 1) * F, cols]
+    for c in range(heads * DV // COLS):
+        at = 2 * heads * F + c * COLS
+        val = mix(xh[...], w1[:, at : at + COLS], ((1,), (0,))).astype(bf16)
+        for mb in range(16 // heads):
+            for i in range(COLS // DV):
+                t = c * (COLS // DV) + i + heads * mb
+                pack[t, 2 * F :, :] = val[mb * count : (mb + 1) * count, i * DV : (i + 1) * DV]
+    keep = pltpu.make_async_copy(pack.at[me], got.at[me], ls.at[4])
+    keep.start()
+    for d in range(1, 16):
+        there = (me + d) % 16
+        go(remote(pack.at[there], got.at[me], e1s.at[d], e1r.at[d], there, h))
+    plane(1, 1)
+    onward(1, 0)
+    plane(1, 3)
+    onward(1, 1)
+    plane(1, 2)
+    onward(1, 3)
+    keep.wait()
+    for d in range(1, 16):
+        arrived(got.at[(me + 16 - d) % 16], e1s.at[d], e1r.at[d], me, h)
+    line(2)
+    plane(2, 0)
+    onward(1, 2)
+    spread(got, q_t, k_t, va)
+    causal = lower(CHUNK)
+    for qi in range(va.shape[0] // CHUNK):
+        attend_rows(qi, q_t, k_t, va, ratio, den, causal)
+    for b in range(16):
+        ob[b, :, :] = ratio[b * count : (b + 1) * count, :].astype(bf16)
+
+    def window(source):
+        return heads_out.at[
+            pl.ds(pl.multiple_of((source // heads) * count, count), count),
+            pl.ds(pl.multiple_of((source % heads) * DV, DV), DV),
+        ]
+
+    keep = pltpu.make_async_copy(ob.at[me], window(me), ls.at[4])
+    keep.start()
+    for d in range(1, 16):
+        there = (me + d) % 16
+        go(remote(ob.at[there], window(me), e2s.at[d], e2r.at[d], there, h))
+    onward(2, 0)
+    corner(1)
+    out2 = pltpu.make_async_copy(w2, wa2, ls.at[5])
+    out2.start()
+    keep.wait()
+    for d in range(1, 16):
+        arrived(window((me + 16 - d) % 16), e2s.at[d], e2r.at[d], me, h)
+    wide = part.shape[1]
+    swaps = []
+    for c in range(wide // COLS):
+        cols = pl.ds(c * COLS, COLS)
+        part[:, c * COLS : (c + 1) * COLS] = mix(
+            heads_out[...], w2[c * COLS : (c + 1) * COLS, :], ((1,), (1,))
+        )
+        go(remote(part.at[:, cols], other.at[:, cols], ws.at[c], wr.at[c], me, 1 - h))
+    for c in range(wide // COLS):
+        cols = pl.ds(c * COLS, COLS)
+        arrived(other.at[:, cols], ws.at[c], wr.at[c], me, 1 - h)
+
+    def one(mb):
+        def body(turn, carry):
+            row = pl.ds(pl.multiple_of(turn * 16, 16), 16)
+            flat = pl.ds(pl.multiple_of(mb * count + turn * 16, 16), 16)
+            mid = xin[mb, row, :].astype(f32) + (part[flat, :] + other[flat, :])
+            middle[mb, row, :] = mid
+            scale = lax.rsqrt(jnp.mean(mid * mid, axis=-1, keepdims=True) + epsilon)
+            near[z, mb, row, :] = (mid * scale).astype(bf16)
+            return carry
+
+        lax.fori_loop(0, count // 16, body, 0)
+
+    one(h)
+    for d in (2, 1, 3):
+        there = index_of((z + d) % ZED, y, x)
+        go(remote(near.at[z, h], near.at[z, h], ns.at[d], nr.at[d], there, h))
+    one(1 - h)
+    plane(2, 1)
+    plane(2, 3)
+    onward(2, 1)
+    plane(2, 2)
+    onward(2, 3)
+    for d in (1, 3, 2):
+        zz = (z + ZED - d) % ZED
+        arrived(near.at[zz, h], ns.at[d], nr.at[d], me, h)
+        go(remote(near.at[zz, h], near.at[zz, h], ds.at[d], dr.at[d], me, 1 - h))
+    onward(2, 2)
+    corner(2)
+    for d in (1, 3, 2):
+        zz = (z + ZED - d) % ZED
+        arrived(near.at[zz, 1 - h], ds.at[d], dr.at[d], me, 1 - h)
+    out1.wait()
+    out2.wait()
+    for copy in late:
+        copy.wait_send()
+
+
+def front(a1, a2, m, xh, xin):
+    mbs, count, wide = xin.shape
+    depth = 16 * count
+    wide1, wide2 = a1.shape[1], a2.shape[1]
+    shape = jax.ShapeDtypeStruct
+    return pl.pallas_call(
+        front_kernel,
+        out_shape=(
+            shape((wide, wide1), bf16),
+            shape((wide, wide2), bf16),
+            shape((wide, m.shape[2]), bf16),
+            shape((16, 2 * F + DV, count), bf16),
+            shape((depth, DV), f32),
+            shape((depth, DV), f32),
+            shape((mbs * count, wide2), bf16),
+            shape(xin.shape, f32),
+            shape((ZED,) + xin.shape, bf16),
+        ),
+        in_specs=[ANY] * 3 + [VMEM] * 2,
+        out_specs=(ANY,) * 3 + (VMEM,) * 6,
+        scratch_shapes=[
+            pltpu.VMEM((wide, wide1), bf16),
+            pltpu.VMEM((wide, wide2), bf16),
+            pltpu.VMEM((16, 2 * F + DV, count), bf16),
+            pltpu.VMEM((F, depth), bf16),
+            pltpu.VMEM((F, depth), bf16),
+            pltpu.VMEM((depth, 2 * DV), bf16),
+            pltpu.VMEM((16, count, DV), bf16),
+            pltpu.VMEM((mbs * count, wide), f32),
+            pltpu.VMEM((mbs * count, wide), f32),
+            DMA((6,)), DMA((3, 4)), DMA((3, 4)), DMA((3, 4, 4)), DMA((3, 4, 4)),
+            DMA((16,)), DMA((16,)), DMA((16,)), DMA((16,)),
+            DMA((wide // COLS,)), DMA((wide // COLS,)), DMA((4,)), DMA((4,)), DMA((4,)), DMA((4,)),
+        ],
+        compiler_params=params(),
+        name="front",
+    )(a1, a2, m, xh, xin)
+
+
+def back_rows_kernel(got, ratio, den, d_o, d_qk, d_v, q_t, k_t, va, da, dn_t):
+    attend_back_body(got, ratio, den, d_o, d_qk, d_v, q_t, k_t, va, da, dn_t)
+
+
+def attend_back_body(got, ratio, den, d_o, d_qk, d_v, q_t, k_t, va, da, dn_t):
+    spread(got, q_t, k_t, va)
+    depth = va.shape[0]
+    lane = lax.broadcasted_iota(jnp.int32, (CHUNK, DV), 1)
+    for qi in range(depth // CHUNK):
+        qs = slice(qi * CHUNK, (qi + 1) * CHUNK)
+        dn = d_o[qs, :].astype(f32) / den[qs, :]
+        dd = -jnp.sum(dn * ratio[qs, :], axis=-1, keepdims=True)
+        big = dd.astype(bf16).astype(f32)
+        da[qs, 0:DV] = dn.astype(bf16)
+        da[qs, DV:] = jnp.where(lane == 0, big, jnp.where(lane == 1, dd - big, 0.0)).astype(bf16)
+        dn_t[:, qs] = jnp.transpose(dn).astype(bf16)
+    causal = lower(CHUNK)
+    for kj in range(depth // CHUNK):
+        ks = slice(kj * CHUNK, (kj + 1) * CHUNK)
+        acc_k = jnp.zeros((F, CHUNK), f32)
+        acc_v = jnp.zeros((DV, CHUNK), f32)
+        for qi in range(kj, depth // CHUNK):
+            qs = slice(qi * CHUNK, (qi + 1) * CHUNK)
+            s = mix(q_t[:, qs], k_t[:, ks], ((0,), (0,)))
+            p = 1.0 + s * (0.25 + s * (1.0 / 32.0))
+            d_s = mix(da[qs, :], va[ks, :], ((1,), (1,))) * (0.25 + s * (1.0 / 16.0))
+            if kj == qi:
+                p = jnp.where(causal, p, 0.0)
+                d_s = jnp.where(causal, d_s, 0.0)
+            d_s = d_s.astype(bf16)
+            acc_v = acc_v + mix(dn_t[:, qs], p.astype(bf16), ((1,), (0,)))
+            acc_k = acc_k + mix(q_t[:, qs], d_s, ((1,), (0,)))
+            d_q = mix(k_t[:, ks], d_s, ((1,), (1,)))
+            d_qk[0:F, qs] = d_q if kj == 0 else d_qk[0:F, qs] + d_q
+        d_qk[F : 2 * F, ks] = acc_k
+        d_v[ks, :] = jnp.transpose(acc_v)
+
+
+def attend_back(got, ratio, den, d_o):
+    depth = d_o.shape[0]
+    shape = jax.ShapeDtypeStruct
+    return pl.pallas_call(
+        back_rows_kernel,
+        out_shape=(shape((2 * F, depth), f32), shape((depth, DV), f32)),
+        in_specs=[VMEM] * 4,
+        out_specs=(VMEM,) * 2,
+        scratch_shapes=[
+            pltpu.VMEM((F, depth), bf16),
+            pltpu.VMEM((F, depth), bf16),
+            pltpu.VMEM((depth, 2 * DV), bf16),
+            pltpu.VMEM((depth, 2 * DV), bf16),
+            pltpu.VMEM((DV, depth), bf16),
+        ],
+        compiler_params=pltpu.CompilerParams(vmem_limit_bytes=VMEM_LIMIT),
+        name="attend_back",
+    )(got, ratio, den, d_o)
+
+
+def share_kernel(g, gg, ls, zs, zr, ds, dr):
+    x, y, z, h = where_am_i()
+    me = index_of(z, y, x)
+    local = pltpu.make_async_copy(g, gg.at[z], ls)
+    local.start()
+    copies = []
+    for d in (2, 1, 3):
+        there = index_of((z + d) % ZED, y, x)
+        copies.append(remote(g.at[h], gg.at[z, h], zs.at[d], zr.at[d], there, h))
+    for copy in copies:
+        copy.start()
+    for d in (1, 3, 2):
+        zz = (z + ZED - d) % ZED
+        arrived(gg.at[zz, h], zs.at[d], zr.at[d], me, h)
+        copy = remote(gg.at[zz, h], gg.at[zz, h], ds.at[d], dr.at[d], me, 1 - h)
+        copy.start()
+        copies.append(copy)
+    for d in (1, 3, 2):
+        zz = (z + ZED - d) % ZED
+        arrived(gg.at[zz, 1 - h], ds.at[d], dr.at[d], me, 1 - h)
+    local.wait()
+    for copy in copies:
+        copy.wait_send()
+
+
+def share(g):
+    return pl.pallas_call(
+        share_kernel,
+        out_shape=jax.ShapeDtypeStruct((ZED,) + g.shape, bf16),
+        in_specs=[ANY],
+        out_specs=ANY,
+        scratch_shapes=[DMA, DMA((4,)), DMA((4,)), DMA((4,)), DMA((4,))],
+        compiler_params=params(),
+        name="share",
+    )(g)
 
 
 def fast(
@@ -705,35 +877,20 @@
     def folded(weight, gain):
         return (weight.astype(f32) * gain).astype(bf16)
 
-    a = jnp.concatenate(
-        [folded(w_query, gain1), folded(w_key, gain1), folded(w_value, gain1), w_out.T], axis=1
-    )
+    a1 = jnp.concatenate([folded(w_query, gain1), folded(w_key, gain1), folded(w_value, gain1)], axis=1)
 
     def cut(weight):
         pieces = jnp.transpose(weight.reshape(rows, ZED, units), (1, 0, 2))
         return jnp.pad(pieces, ((0, 0), (0, 0), (0, room - units)))
 
     m = jnp.concatenate([cut(folded(w_gate, gain2)), cut(folded(w_up, gain2)), cut(w_down.T)], axis=2)
-    wa, wm, gg = gather_all(a, m, cotangent)
-    w_qk, w_v, w_o = wa[:, :qk], wa[:, qk : qk + vv], wa[:, qk + vv :]
-    w_g, w_u, w_d = wm[:, :room], wm[:, room : 2 * room], wm[:, 2 * room :]
-
     stream = inputs.astype(f32).reshape(mbs * count, wide)
     r1 = lax.rsqrt(jnp.mean(stream * stream, axis=-1, keepdims=True) + epsilon)
     xh1 = (stream * r1).astype(bf16)
-    qk_t = mix(w_qk, xh1, ((0,), (1,))).astype(bf16)
-    qk_t = qk_t.reshape(2, heads, F, mbs, count).transpose(3, 1, 0, 2, 4).reshape(16, 2 * F, count)
-    val = mix(xh1, w_v, ((1,), (0,))).astype(bf16)
-    val = val.reshape(mbs, count, heads, DV).transpose(0, 2, 1, 3).reshape(16, count, DV)
-    got = exchange(jnp.concatenate([qk_t, val], axis=1))
-    q_t = got[:, :F].transpose(1, 0, 2).reshape(F, 16 * count)
-    k_t = got[:, F : 2 * F].transpose(1, 0, 2).reshape(F, 16 * count)
-    v = got[:, 2 * F :].reshape(16 * count, DV)
-    ratio, denom = attend(q_t, k_t, v)
-    back = exchange(ratio.astype(bf16).reshape(16, count, DV))
-    heads_out = back.reshape(mbs, heads, count, DV).transpose(0, 2, 1, 3).reshape(mbs * count, vv)
-    part = mix(heads_out, w_o, ((1,), (1,)))
-    middle, near = norm_two(part.reshape(mbs, count, wide), inputs)
+    wa1, w_o, wm, got, ratio, den, heads_out, middle, near = front(a1, w_out.T, m, xh1, inputs)
+    gg = share(cotangent)
+    w_qk, w_v = wa1[:, :qk], wa1[:, qk:]
+    w_g, w_u, w_d = wm[:, :room], wm[:, room : 2 * room], wm[:, 2 * room :]
     middle = middle.reshape(mbs * count, wide)
     many = ZED * mbs * count
     n2 = near.reshape(many, wide)
@@ -759,10 +916,9 @@
     d_att = d_middle.astype(bf16)
     d_heads = mix(d_att, w_o, ((1,), (0,))).astype(bf16)
     d_heads = d_heads.reshape(mbs, count, heads, DV).transpose(0, 2, 1, 3).reshape(16, count, DV)
-    d_heads = exchange(d_heads).reshape(16 * count, DV).astype(f32)
-    d_q, d_k, d_v = attend_back(q_t, k_t, v, ratio, denom, d_heads)
-    d_qk = jnp.concatenate([d_q, d_k], axis=0).astype(bf16)
-    d_qk = d_qk.reshape(2 * F, 16, count).transpose(1, 0, 2)
+    d_heads = exchange(d_heads).reshape(16 * count, DV)
+    d_qk, d_v = attend_back(got, ratio, den, d_heads)
+    d_qk = d_qk.astype(bf16).reshape(2 * F, 16, count).transpose(1, 0, 2)
     home = exchange(jnp.concatenate([d_qk, d_v.astype(bf16).reshape(16, count, DV)], axis=1))
     d_qk = home[:, : 2 * F].reshape(mbs, heads, 2, F, count).transpose(0, 4, 2, 1, 3)
     d_qk = d_qk.reshape(mbs * count, qk)

time: 1000 us -> 858 us (0.86)
  Pallas kernels: 721 us -> 670 us
  matrix products: 123 us -> 81.5 us
  local copies, waits for them, and re-layouts: 82.3 us -> 45.4 us
  other arithmetic: 59.8 us -> 49.6 us
    dot_general x24 -> x15, matrix products: 123 us -> 81.5 us  [mix(): return lax.dot_general(a, b, (over, ((), ())), preferred_element_type=f32)]
    pallas_call x4 -> x2, Pallas kernels: 97.7 us -> 58.8 us  [exchange(): pl.pallas_call(exchange_kernel, out_shape=jax.ShapeDtypeStruct(blocks.sha...]
    dot_general x5 -> x4, local copies, waits for them, and re-layouts: 33.4 us -> 15.6 us  [mix(): return lax.dot_general(a, b, (over, ((), ())), preferred_element_type=f32)]
    mul x1 -> x0, local copies, waits for them, and re-layouts: 12.3 us -> none  [attend_back(): d_scores * (0.25 + s * (1.0 / 16.0))]
    pallas_call x2 -> x3, Pallas kernels: 287 us -> 275 us  [the longest x1 223 us: front(): pl.pallas_call(front_kernel, out_shape=(shape((wide, wide1), bf16), shape...]
    reduce_sum x2 -> x0, other arithmetic: 11 us -> none  [the longest x1 9.27 us: attend(): denom = jnp.sum(weighted.astype(f32), axis=-1, keepdims=True)]
where the time goes in v2:
time: 858 us; the launch traced here: 850 us
  Pallas kernels  670 us (78%)
  matrix products  81.5 us (9%)
  other arithmetic  49.6 us (6%)
  local copies, waits for them, and re-layouts  45.4 us (5%)
    pallas_call x1, Pallas kernels, front(): pl.pallas_call(front_kernel, out_shape=(shape((wide, wide1), bf16), shape...  223 us
    pallas_call x1, Pallas kernels, scatter_all(): pl.pallas_call(scatter_kernel, out_shape=(give, give), in_specs=[VMEM] *...  220 us
    pallas_call x1, Pallas kernels, combine(): pl.pallas_call(combine_kernel, out_shape=jax.ShapeDtypeStruct((kinds, mbs...  95.8 us
    dot_general x15, matrix products, mix(): return lax.dot_general(a, b, (over, ((), ())), preferred_element_type=f32)  81.5 us
    pallas_call x2, Pallas kernels, exchange(): pl.pallas_call(exchange_kernel, out_shape=jax.ShapeDtypeStruct(blocks.sha...  58.8 us
    pallas_call x1, Pallas kernels, share(): pl.pallas_call(share_kernel, out_shape=jax.ShapeDtypeStruct((ZED,) + g.sh...  43.7 us
    pallas_call x1, Pallas kernels, pair_sum(): pl.pallas_call(pair_kernel, out_shape=jax.ShapeDtypeStruct(part.shape, pa...  20.3 us

profile of v2, /device:TPU:0, one launch (start us, length us, event | category | flops | bytes accessed | tf_op | source)
XLA Modules:
  0.0 850.5 jit_solution(15785767839130476564)
XLA Ops:
  12.0 2.6 fusion.23.m
  17.0 222.6 %front.1 = (bf16[2048,1280]{1,0:T(8,128)(2,1)}, bf16[2048,1024]{1,0:T(8,128)(2,1)}, bf16[2048,2304]{1,0:T(8,128)(2,1)}, bf16[16,160,128]{2,1,0:T(8,128)(2,1)}, f...) custom-call(bf16[128,1280]{1,0:T(8,128)(2,1)} %pad_maximum_fusion.4., ...), custom_call_target="tpu_custom_call" | custom-call | tf_op jit(solution)/shard_map/front/pallas_call | solution.py:737
  239.6 8.4 fusion.17
  248.0 7.2 fusion.14
  255.2 43.7 %share.1 = bf16[4,2,128,2048]{3,2,1,0:T(8,128)(2,1)} custom-call(bf16[2,128,2048]{2,1,0:T(8,128)(2,1)} %g.1), custom_call_target="tpu_custom_call" | custom-call | tf_op jit(solution)/shard_map/share/pallas_call | solution.py:855
  298.9 9.6 %fusion.9 = (bf16[1024,768]{0,1:T(8,128)(2,1)S(1)}, bf16[1024,768]{0,1:T(8,128)(2,1)S(1)}, bf16[1024,768]{0,1:T(8,128)(2,1)S(1)}) fusion(f32[1024,768]{0,1:T(8,128)} %fusion.14, f32[1024,768]{0,1:T(8,128)} %fusion.17, bf16[1024,2048]{1,0:T(8,128)(2,1)} %bitcast.173, bf16[2048,2304]{1,0:T(8,128)(2,1)} %get-tuple-element.25), kind=kOutput, calls=%fused_computation.22 | convolution fusion | flops 3233021952 | bytes 18350080 | tf_op jit(solution)/shard_map/dot_general | solution.py:511
  308.6 7.1 fusion.12
  315.6 6.0 add_convert_fusion
  321.6 7.0 convolution_convert_fusion
  328.6 6.2 pad_maximum_fusion.2.t
  334.8 95.8 %combine.1 = bf16[2,2,128,2048]{3,2,1,0:T(8,128)(2,1)} custom-call(bf16[2,4,2,128,2048]{4,3,2,1,0:T(8,128)(2,1)} %pad_maximum_fusion.2.t), custom_call_target="tpu_custom_call" | custom-call | tf_op jit(solution)/shard_map/combine/pallas_call | solution.py:372
  437.1 3.0 copy.74
  440.1 4.8 convolution_convert_fusion.2
  447.2 37.2 %exchange.2 = bf16[16,128,128]{2,1,0:T(8,128)(2,1)} custom-call(bf16[16,128,128]{2,1,0:T(8,128)(2,1)} %bitcast.194), custom_call_target="tpu_custom_call" | custom-call | tf_op jit(solution)/shard_map/exchange/pallas_call | solution.py:303
  484.4 8.6 %attend_back.1 = (f32[32,2048]{1,0:T(8,128)}, f32[2048,128]{1,0:T(8,128)}) custom-call(bf16[16,160,128]{2,1,0:T(8,128)(2,1)} %get-tuple-element.27.got, f32[2048,128]{1,0:T(8,128)} %get-tuple-element.28.ratio, f32[2048,128]{1,0:T(8,128)} %get-tuple-element.29.den, bf16[2048,128]{1,0:T(8,128)(2,1)} %bitcast.190), custom_call_target="tpu_custom_call" | custom-call | tf_op jit(solution)/shard_map/attend_back/pallas_call | solution.py:812
  496.2 21.7 %exchange.3 = bf16[16,160,128]{2,1,0:T(8,128)(2,1)} custom-call(bf16[16,160,128]{2,1,0:T(8,128)(2,1)} %pad_maximum_fusion.3.src), custom_call_target="tpu_custom_call" | custom-call | tf_op jit(solution)/shard_map/exchange/pallas_call | solution.py:303
  523.1 4.3 convolution_convert_fusion.3
  527.4 6.4 copy.56
  533.8 7.9 convolution_convert_fusion.4
  541.8 4.9 convolution_convert_fusion.5
  548.3 4.8 fusion.11
  553.2 4.8 copy.59
  557.9 12.1 %pad_maximum_fusion = (bf16[4,2,2,128,2304]{4,3,2,1,0:T(8,128)(2,1)}, bf16[4,2,2,128,2304]{4,3,2,1,0:T(8,128)(2,1)}) fusion(bf16[4,2,2,128,1024]{4,3,2,1,0:T(8,128)(2,1)} %convolution_convert_fusion.2, bf16[4,2,2,128,1024]{4,3,2,1,0:T(8,128)(2,1)} %convolution_convert_fusion.3, bf16[4,2,2,128,256]{4,3,2,1,0:T(8,128)(2,1)S(1)} %copy-done.10, ...), kind=kLoop, calls=%fused_computation | loop fusion | flops 56623104 | bytes 37748736 | tf_op jit(solution)/shard_map/concatenate | solution.py:933
  570.0 220.3 %scatter_all.1 = (bf16[4,128,2304]{2,1,0:T(8,128)(2,1)}, bf16[4,128,2304]{2,1,0:T(8,128)(2,1)}) custom-call(bf16[4,2,2,128,2304]{4,3,2,1,0:T(8,128)(2,1)} %get-tuple-element.94.ga, bf16[4,2,2,128,2304]{4,3,2,1,0:T(8,128)(2,1)} %get-tuple-element.95.gm), custom_call_target="tpu_custom_call" | custom-call | tf_op jit(solution)/shard_map/scatter_all/pallas_call | solution.py:490
  797.3 3.0 copy.60
  800.3 3.0 copy.61
  803.3 3.7 bitcast_multiply_fusion.5
  810.1 2.9 copy.64
  813.0 3.0 copy.65
  819.6 3.5 fusion.4
  823.1 3.1 convolution_add_fusion.part
  826.3 20.3 %pair_sum.1 = f32[256,2048]{1,0:T(8,128)} custom-call(f32[256,2048]{1,0:T(8,128)} %convolution_add_fusion.part), custom_call_target="tpu_custom_call" | custom-call | tf_op jit(solution)/shard_map/pair_sum/pallas_call | solution.py:398
  (111 shorter events, 49.7 us)
Async XLA Ops:
  0.6 4.9 copy-start.19
  0.7 5.2 copy-start.24
  9.6 5.0 copy-start
  12.0 4.2 copy-start.20
  239.6 8.4 copy-start.11
  308.5 7.1 copy-start.25
  308.5 7.1 copy-start.29
  308.5 13.1 %copy-start.27 = (bf16[1024,768]{0,1:T(8,128)(2,1)}, bf16[1024,768]{0,1:T(8,128)(2,1)S(1)}, u32[]{:S(2)}) copy-start(bf16[1024,768]{0,1:T(8,128)(2,1)S(1)} %get-tuple-element.65) | copy-start | bytes 4718596
  430.6 1.9 copy-start.2
  430.6 4.5 copy-start.4
  432.5 3.1 copy-start.8
  437.1 7.8 copy-start.5
  440.1 4.8 copy-start.23
  494.3 26.1 %copy-start.1 = (bf16[2,128,2048]{2,1,0:T(8,128)(2,1)S(1)}, bf16[2,128,2048]{2,1,0:T(8,128)(2,1)}, u32[]{:S(2)}) copy-start(bf16[2,128,2048]{2,1,0:T(8,128)(2,1)} %xin.1) | copy-start | bytes 3145732
  519.3 2.2 copy-start.14
  533.8 8.0 copy-start.12
  533.8 8.0 copy-start.26
  541.8 5.0 slice-start
  541.8 6.6 copy-start.9
  541.8 6.6 copy-start.28
  546.9 1.5 copy-start.16
  553.2 4.8 copy-start.10
  790.4 2.4 copy-start.18
  790.4 3.4 copy-start.21
  790.4 3.4 copy-start.22
  790.4 4.2 copy-start.13
  807.0 9.0 %copy-start.7 = (f32[128,4,704]{2,0,1:T(8,128)S(1)}, f32[128,4,704]{2,0,1:T(8,128)}, u32[]{:S(2)}) copy-start(f32[128,4,704]{2,0,1:T(8,128)} %get-tuple-element.66) | copy-start | bytes 4325380
  813.0 6.6 copy-start.15
  819.6 3.5 copy-start.17
  826.3 22.5 %copy-start.6 = (f32[256,2048]{1,0:T(8,128)S(1)}, f32[256,2048]{1,0:T(8,128)}, u32[]{:S(2)}) copy-start(f32[256,2048]{1,0:T(8,128)} %copy-done.5) | copy-start | bytes 6291460
  846.6 2.2 copy-start.3

commit v3 on v2

--- a/solution.py
+++ b/solution.py
@@ -281,232 +281,6 @@
 ORDER = (0, 1, 3, 2)
 
 
-def exchange_kernel(src, dst, ls, ss, rs):
-    x, y, z, h = where_am_i()
-    me = index_of(z, y, x)
-    local = pltpu.make_async_copy(src.at[me], dst.at[me], ls)
-    local.start()
-    copies = []
-    for d in range(1, 16):
-        there = (me + d) % 16
-        copies.append(remote(src.at[there], dst.at[me], ss.at[d], rs.at[d], there, h))
-    for copy in copies:
-        copy.start()
-    local.wait()
-    for d in range(1, 16):
-        arrived(dst.at[(me + 16 - d) % 16], ss.at[d], rs.at[d], me, h)
-    for copy in copies:
-        copy.wait_send()
-
-
-def exchange(blocks):
-    return pl.pallas_call(
-        exchange_kernel,
-        out_shape=jax.ShapeDtypeStruct(blocks.shape, blocks.dtype),
-        in_specs=[ANY],
-        out_specs=ANY,
-        scratch_shapes=[DMA, DMA((16,)), DMA((16,))],
-        compiler_params=params(),
-        name="exchange",
-    )(blocks)
-
-
-def combine_kernel(t, out, other, summed, landed, sem, zs, zr, ds, dr):
-    x, y, z, h = where_am_i()
-    me = index_of(z, y, x)
-    kinds = t.shape[0]
-    swaps = []
-    for d in (2, 1, 3, 0):
-        zz = (z + d) % ZED
-        for kind in range(kinds):
-            swaps.append(
-                remote(t.at[kind, zz, 1 - h], other.at[kind, zz], sem.at[0, kind, d], sem.at[1, kind, d], me, 1 - h)
-            )
-    for copy in swaps:
-        copy.start()
-    copies = []
-    for d in (2, 1, 3, 0):
-        zz = (z + d) % ZED
-        for kind in range(kinds):
-            arrived(other.at[kind, zz], sem.at[0, kind, d], sem.at[1, kind, d], me, h)
-
-            def add(turn, carry):
-                row = pl.ds(pl.multiple_of(turn * 16, 16), 16)
-                summed[kind, zz, row, :] = (
-                    t[kind, zz, h, row, :].astype(f32) + other[kind, zz, row, :].astype(f32)
-                ).astype(bf16)
-                return carry
-
-            lax.fori_loop(0, 8, add, 0)
-            if d:
-                copy = remote(
-                    summed.at[kind, zz], landed.at[kind, d], zs.at[kind, d], zr.at[kind, d],
-                    index_of(zz, y, x), h,
-                )
-                copy.start()
-                copies.append(copy)
-    for kind in range(kinds):
-        for d in (1, 3, 2):
-            arrived(landed.at[kind, d], zs.at[kind, d], zr.at[kind, d], me, h)
-
-        def total(turn, carry):
-            row = pl.ds(pl.multiple_of(turn * 16, 16), 16)
-            acc = summed[kind, z, row, :].astype(f32)
-            for d in (1, 2, 3):
-                acc = acc + landed[kind, d, row, :].astype(f32)
-            out[kind, h, row, :] = acc.astype(bf16)
-            return carry
-
-        lax.fori_loop(0, 8, total, 0)
-        copy = remote(out.at[kind, h], out.at[kind, h], ds.at[kind], dr.at[kind], me, 1 - h)
-        copy.start()
-        copies.append(copy)
-    for kind in range(kinds):
-        arrived(out.at[kind, 1 - h], ds.at[kind], dr.at[kind], me, 1 - h)
-    for copy in swaps + copies:
-        copy.wait_send()
-
-
-def combine(t):
-    kinds, _, mbs, count, wide = t.shape
-    return pl.pallas_call(
-        combine_kernel,
-        out_shape=jax.ShapeDtypeStruct((kinds, mbs, count, wide), bf16),
-        in_specs=[VMEM],
-        out_specs=VMEM,
-        scratch_shapes=[
-            pltpu.VMEM((kinds, ZED, count, wide), bf16),
-            pltpu.VMEM((kinds, ZED, count, wide), bf16),
-            pltpu.VMEM((kinds, ZED, count, wide), bf16),
-            DMA((2, kinds, 4)), DMA((kinds, 4)), DMA((kinds, 4)), DMA((kinds,)), DMA((kinds,)),
-        ],
-        compiler_params=params(),
-        name="combine",
-    )(t)
-
-
-def pair_kernel(part, out, other, sem):
-    x, y, z, h = where_am_i()
-    me = index_of(z, y, x)
-    swap = remote(part, other, sem.at[0], sem.at[1], me, 1 - h)
-    swap.start()
-    swap.wait()
-    out[...] = part[...] + other[...]
-
-
-def pair_sum(part):
-    return pl.pallas_call(
-        pair_kernel,
-        out_shape=jax.ShapeDtypeStruct(part.shape, part.dtype),
-        in_specs=[VMEM],
-        out_specs=VMEM,
-        scratch_shapes=[pltpu.VMEM(part.shape, part.dtype), DMA((2,))],
-        compiler_params=params(),
-        name="pair_sum",
-    )(part)
-
-
-def scatter_kernel(ga, gm, za, zm, r1x, r1y, r2x, r2y, f1, f2, fin, s1, q1, s2, q2, s3, q3):
-    x, y, z, h = where_am_i()
-    me = index_of(z, y, x)
-    at_x, at_y = index_of(z, y, 1 - x), index_of(z, 1 - y, x)
-    half = ga.shape[-1] // 2
-    low, high = pl.ds(0, half), pl.ds(half, half)
-    sets = [(0, ga, za, d) for d in (2, 1, 3, 0)] + [(1, gm, zm, d) for d in (2, 1, 3, 0)]
-    copies = []
-
-    def start(copy):
-        copy.start()
-        copies.append(copy)
-
-    for n, (kind, g, out, d) in enumerate(sets):
-        zz = (z + d) % ZED
-        start(remote(g.at[zz, :, 1 - x, :, low], r1x.at[n], s1.at[n, 0], q1.at[n, 0], at_x, h))
-        start(remote(g.at[zz, 1 - y, :, :, high], r1y.at[n], s1.at[n, 1], q1.at[n, 1], at_y, h))
-
-    def wide(turns):
-        return pl.ds(pl.multiple_of(turns * 16, 16), 16)
-
-    for turn in range(len(sets) + 1):
-        if turn < len(sets):
-            n = turn
-            kind, g, out, d = sets[n]
-            zz = (z + d) % ZED
-            arrived(r1x.at[n], s1.at[n, 0], q1.at[n, 0], me, h)
-            arrived(r1y.at[n], s1.at[n, 1], q1.at[n, 1], me, h)
-
-            def forward(i, carry):
-                row = wide(i)
-                f1[n, row, :] = (
-                    g[zz, 1 - y, x, row, low].astype(f32) + r1x[n, 1 - y, row, :].astype(f32)
-                ).astype(bf16)
-                f2[n, row, :] = (
-                    g[zz, y, 1 - x, row, high].astype(f32) + r1y[n, 1 - x, row, :].astype(f32)
-                ).astype(bf16)
-                return carry
-
-            lax.fori_loop(0, 8, forward, 0)
-            start(remote(f1.at[n], r2y.at[n], s2.at[n, 0], q2.at[n, 0], at_y, h))
-            start(remote(f2.at[n], r2x.at[n], s2.at[n, 1], q2.at[n, 1], at_x, h))
-        if turn > 0:
-            n = turn - 1
-            kind, g, out, d = sets[n]
-            zz = (z + d) % ZED
-            arrived(r2y.at[n], s2.at[n, 0], q2.at[n, 0], me, h)
-            arrived(r2x.at[n], s2.at[n, 1], q2.at[n, 1], me, h)
-            target = fin.at[n] if d else out.at[z]
-
-            def finish(i, carry):
-                row = wide(i)
-                target[row, low] = (
-                    g[zz, y, x, row, low].astype(f32)
-                    + r1x[n, y, row, :].astype(f32)
-                    + r2y[n, row, :].astype(f32)
-                ).astype(bf16)
-                target[row, high] = (
-                    g[zz, y, x, row, high].astype(f32)
-                    + r1y[n, x, row, :].astype(f32)
-                    + r2x[n, row, :].astype(f32)
-                ).astype(bf16)
-                return carry
-
-            lax.fori_loop(0, 8, finish, 0)
-            if d:
-                start(
-                    remote(fin.at[n], out.at[z], s3.at[kind, d], q3.at[kind, d], index_of(zz, y, x), h)
-                )
-    for kind, g, out, d in sets:
-        if d:
-            arrived(out.at[(z + ZED - d) % ZED], s3.at[kind, d], q3.at[kind, d], me, h)
-    for copy in copies:
-        copy.wait_send()
-
-
-def scatter_all(ga, gm):
-    wide = ga.shape[-1]
-    ga = ga.reshape(ZED, 2, 2, 128, wide)
-    gm = gm.reshape(ZED, 2, 2, 128, wide)
-    give = jax.ShapeDtypeStruct((ZED, 128, wide), bf16)
-    return pl.pallas_call(
-        scatter_kernel,
-        out_shape=(give, give),
-        in_specs=[VMEM] * 2,
-        out_specs=(VMEM,) * 2,
-        scratch_shapes=[
-            pltpu.VMEM((8, 2, 128, wide // 2), bf16),
-            pltpu.VMEM((8, 2, 128, wide // 2), bf16),
-            pltpu.VMEM((8, 128, wide // 2), bf16),
-            pltpu.VMEM((8, 128, wide // 2), bf16),
-            pltpu.VMEM((8, 128, wide // 2), bf16),
-            pltpu.VMEM((8, 128, wide // 2), bf16),
-            pltpu.VMEM((8, 128, wide), bf16),
-            DMA((8, 2)), DMA((8, 2)), DMA((8, 2)), DMA((8, 2)), DMA((2, 4)), DMA((2, 4)),
-        ],
-        compiler_params=params(),
-        name="scatter_all",
-    )(ga, gm)
-
-
 def mix(a, b, over):
     return lax.dot_general(a, b, (over, ((), ())), preferred_element_type=f32)
 
@@ -768,10 +542,6 @@
     )(a1, a2, m, xh, xin)
 
 
-def back_rows_kernel(got, ratio, den, d_o, d_qk, d_v, q_t, k_t, va, da, dn_t):
-    attend_back_body(got, ratio, den, d_o, d_qk, d_v, q_t, k_t, va, da, dn_t)
-
-
 def attend_back_body(got, ratio, den, d_o, d_qk, d_v, q_t, k_t, va, da, dn_t):
     spread(got, q_t, k_t, va)
     depth = va.shape[0]
@@ -806,26 +576,6 @@
         d_v[ks, :] = jnp.transpose(acc_v)
 
 
-def attend_back(got, ratio, den, d_o):
-    depth = d_o.shape[0]
-    shape = jax.ShapeDtypeStruct
-    return pl.pallas_call(
-        back_rows_kernel,
-        out_shape=(shape((2 * F, depth), f32), shape((depth, DV), f32)),
-        in_specs=[VMEM] * 4,
-        out_specs=(VMEM,) * 2,
-        scratch_shapes=[
-            pltpu.VMEM((F, depth), bf16),
-            pltpu.VMEM((F, depth), bf16),
-            pltpu.VMEM((depth, 2 * DV), bf16),
-            pltpu.VMEM((depth, 2 * DV), bf16),
-            pltpu.VMEM((DV, depth), bf16),
-        ],
-        compiler_params=pltpu.CompilerParams(vmem_limit_bytes=VMEM_LIMIT),
-        name="attend_back",
-    )(got, ratio, den, d_o)
-
-
 def share_kernel(g, gg, ls, zs, zr, ds, dr):
     x, y, z, h = where_am_i()
     me = index_of(z, y, x)
@@ -863,6 +613,409 @@
     )(g)
 
 
+FAR = (2, 1, 3, 0)
+
+
+def chunk(turn):
+    return pl.ds(pl.multiple_of(turn * 16, 16), 16)
+
+
+class Scatter:
+    def __init__(self, g, low_acc, high_acc, fin, out, r1x, r1y, r2x, r2y, s, q, go):
+        self.g, self.low_acc, self.high_acc, self.fin, self.out = g, low_acc, high_acc, fin, out
+        self.r1x, self.r1y, self.r2x, self.r2y, self.s, self.q = r1x, r1y, r2x, r2y, s, q
+        self.go = go
+        self.x, self.y, self.z, self.h = where_am_i()
+        self.me = index_of(self.z, self.y, self.x)
+        self.at_x = index_of(self.z, self.y, 1 - self.x)
+        self.at_y = index_of(self.z, 1 - self.y, self.x)
+        self.half = r1x.shape[-1]
+        self.low, self.high = pl.ds(0, self.half), pl.ds(self.half, self.half)
+
+    def first(self, d):
+        zz, x, y, g = (self.z + d) % ZED, self.x, self.y, self.g
+        self.go(remote(g.at[zz, :, 1 - x, :, self.low], self.r1x.at[d], self.s.at[d, 0], self.q.at[d, 0], self.at_x, self.h))
+        self.go(remote(g.at[zz, 1 - y, :, :, self.high], self.r1y.at[d], self.s.at[d, 1], self.q.at[d, 1], self.at_y, self.h))
+
+    def second(self, d):
+        x, y, me, h, r1x, r1y = self.x, self.y, self.me, self.h, self.r1x, self.r1y
+        arrived(r1x.at[d], self.s.at[d, 0], self.q.at[d, 0], me, h)
+        arrived(r1y.at[d], self.s.at[d, 1], self.q.at[d, 1], me, h)
+        low_acc, high_acc = self.low_acc(d), self.high_acc(d)
+
+        def body(i, carry):
+            row = chunk(i)
+            low_acc[row, :] = (
+                low_acc[row, :].astype(f32) + r1x[d, 1 - y, row, :].astype(f32)
+            ).astype(bf16)
+            high_acc[row, :] = (
+                high_acc[row, :].astype(f32) + r1y[d, 1 - x, row, :].astype(f32)
+            ).astype(bf16)
+            return carry
+
+        lax.fori_loop(0, 8, body, 0)
+        self.go(remote(low_acc, self.r2y.at[d], self.s.at[d, 2], self.q.at[d, 2], self.at_y, h))
+        self.go(remote(high_acc, self.r2x.at[d], self.s.at[d, 3], self.q.at[d, 3], self.at_x, h))
+
+    def third(self, d):
+        x, y, me, h, z = self.x, self.y, self.me, self.h, self.z
+        arrived(self.r2y.at[d], self.s.at[d, 2], self.q.at[d, 2], me, h)
+        arrived(self.r2x.at[d], self.s.at[d, 3], self.q.at[d, 3], me, h)
+        fin, low, high = self.fin(d), self.low, self.high
+        target = fin if d else self.out.at[z]
+
+        def body(i, carry):
+            row = chunk(i)
+            target[row, low] = (
+                fin[row, low].astype(f32)
+                + self.r1x[d, y, row, :].astype(f32)
+                + self.r2y[d, row, :].astype(f32)
+            ).astype(bf16)
+            target[row, high] = (
+                fin[row, high].astype(f32)
+                + self.r1y[d, x, row, :].astype(f32)
+                + self.r2x[d, row, :].astype(f32)
+            ).astype(bf16)
+            return carry
+
+        lax.fori_loop(0, 8, body, 0)
+        if d:
+            there = index_of((z + d) % ZED, y, x)
+            self.go(remote(fin, self.out.at[z], self.s.at[d, 4], self.q.at[d, 4], there, h))
+
+    def last(self):
+        for d in (1, 3, 2):
+            arrived(
+                self.out.at[(self.z + ZED - d) % ZED], self.s.at[d, 4], self.q.at[d, 4], self.me, self.h
+            )
+
+
+class Combine:
+    def __init__(self, t, out, other, summed, landed, ls, s, q, go):
+        self.t, self.out, self.other, self.summed, self.landed = t, out, other, summed, landed
+        self.ls, self.s, self.q, self.go = ls, s, q, go
+        self.x, self.y, self.z, self.h = where_am_i()
+        self.me = index_of(self.z, self.y, self.x)
+
+    def begin(self):
+        t, h, other = self.t, self.h, self.other
+        self.own = {}
+        for d in FAR:
+            zz = (self.z + d) % ZED
+            self.own[d] = pltpu.make_async_copy(t.at[zz, h], self.summed.at[d], self.ls.at[d])
+            self.own[d].start()
+            self.go(remote(t.at[zz, 1 - h], other.at[d], self.s.at[d, 0], self.q.at[d, 0], self.me, 1 - h))
+
+    def spread(self):
+        summed, other = self.summed, self.other
+        for d in FAR:
+            zz = (self.z + d) % ZED
+            self.own[d].wait()
+            arrived(other.at[d], self.s.at[d, 0], self.q.at[d, 0], self.me, 1 - self.h)
+
+            def add(turn, carry):
+                row = chunk(turn)
+                summed[d, row, :] = (
+                    summed[d, row, :].astype(f32) + other[d, row, :].astype(f32)
+                ).astype(bf16)
+                return carry
+
+            lax.fori_loop(0, 8, add, 0)
+            if d:
+                there = index_of(zz, self.y, self.x)
+                self.go(remote(summed.at[d], self.landed.at[d], self.s.at[d, 1], self.q.at[d, 1], there, self.h))
+
+    def total(self):
+        summed, landed, out, h = self.summed, self.landed, self.out, self.h
+        for d in (1, 3, 2):
+            arrived(landed.at[d], self.s.at[d, 1], self.q.at[d, 1], self.me, h)
+
+        def body(turn, carry):
+            row = chunk(turn)
+            acc = summed[0, row, :].astype(f32)
+            for d in (1, 2, 3):
+                acc = acc + landed[d, row, :].astype(f32)
+            out[h, row, :] = acc.astype(bf16)
+            return carry
+
+        lax.fori_loop(0, 8, body, 0)
+        self.go(remote(out.at[h], out.at[h], self.s.at[0, 1], self.q.at[0, 1], self.me, 1 - h))
+
+    def done(self):
+        arrived(self.out.at[1 - self.h], self.s.at[0, 1], self.q.at[0, 1], self.me, 1 - self.h)
+
+
+def back_kernel(
+    gm, t, wo, mid, cot, got, ratio, den,
+    zm, d_mid, d_att, home,
+    r1x, r1y, r2x, r2y, f1, f2, fin, e2, other, summed, landed, w2, pack, d_o, d_qk, d_v,
+    q_t, k_t, va, da, dn_t, pack2,
+    ls, fs, gs, gq, cs, cq, e1s, e1r, e2s, e2r,
+):
+    x, y, z, h = where_am_i()
+    me = index_of(z, y, x)
+    count = mid.shape[1]
+    heads = 16 // mid.shape[0]
+    late = []
+
+    def go(copy):
+        copy.start()
+        late.append(copy)
+
+    combine = Combine(t, e2, other, summed, landed, ls, cs, cq, go)
+    scatter = Scatter(
+        gm, lambda d: f1.at[d], lambda d: f2.at[d], lambda d: fin.at[d], zm,
+        r1x, r1y, r2x, r2y, gs, gq, go,
+    )
+    combine.begin()
+    for d in FAR:
+        scatter.first(d)
+    keep = {}
+    for d in FAR:
+        zz = (z + d) % ZED
+        keep[d] = [
+            pltpu.make_async_copy(gm.at[zz, 1 - y, x, :, scatter.low], f1.at[d], fs.at[d, 0]),
+            pltpu.make_async_copy(gm.at[zz, y, 1 - x, :, scatter.high], f2.at[d], fs.at[d, 1]),
+            pltpu.make_async_copy(gm.at[zz, y, x], fin.at[d], fs.at[d, 2]),
+        ]
+        for copy in keep[d]:
+            copy.start()
+    weight = pltpu.make_async_copy(wo, w2, ls.at[4])
+    weight.start()
+    combine.spread()
+    for d in FAR:
+        for copy in keep[d]:
+            copy.wait()
+    weight.wait()
+    scatter.second(2)
+    scatter.second(1)
+    combine.total()
+    combine.done()
+
+    for mb in range(mid.shape[0]):
+
+        def body(turn, carry):
+            row = chunk(turn)
+            m = mid[mb, row, :]
+            scale = lax.rsqrt(jnp.mean(m * m, axis=-1, keepdims=True) + epsilon)
+            hat = m * scale
+            e = e2[mb, row, :].astype(f32)
+            d_m = cot[mb, row, :].astype(f32) + scale * (
+                e - hat * jnp.mean(e * hat, axis=-1, keepdims=True)
+            )
+            d_mid[mb, row, :] = d_m
+            d_att[pl.ds(pl.multiple_of(mb * count + turn * 16, 16), 16), :] = d_m.astype(bf16)
+            return carry
+
+        lax.fori_loop(0, count // 16, body, 0)
+    for c in range(heads * DV // COLS):
+        val = mix(d_att[...], w2[:, c * COLS : (c + 1) * COLS], ((1,), (0,))).astype(bf16)
+        for mb in range(16 // heads):
+            for i in range(COLS // DV):
+                pack[c * (COLS // DV) + i + heads * mb, :, :] = val[
+                    mb * count : (mb + 1) * count, i * DV : (i + 1) * DV
+                ]
+
+    def window(source):
+        return d_o.at[pl.ds(pl.multiple_of(source * count, count), count)]
+
+    own = pltpu.make_async_copy(pack.at[me], window(me), ls.at[5])
+    own.start()
+    for d in range(1, 16):
+        there = (me + d) % 16
+        go(remote(pack.at[there], window(me), e1s.at[d], e1r.at[d], there, h))
+    scatter.second(3)
+    own.wait()
+    for d in range(1, 16):
+        arrived(window((me + 16 - d) % 16), e1s.at[d], e1r.at[d], me, h)
+    scatter.second(0)
+    scatter.third(2)
+    attend_back_body(got, ratio, den, d_o, d_qk, d_v, q_t, k_t, va, da, dn_t)
+    for b in range(16):
+        pack2[b, 0 : 2 * F, :] = d_qk[:, b * count : (b + 1) * count].astype(bf16)
+        pack2[b, 2 * F :, :] = d_v[b * count : (b + 1) * count, :].astype(bf16)
+    own = pltpu.make_async_copy(pack2.at[me], home.at[me], ls.at[5])
+    own.start()
+    for d in range(1, 16):
+        there = (me + d) % 16
+        go(remote(pack2.at[there], home.at[me], e2s.at[d], e2r.at[d], there, h))
+    scatter.third(1)
+    scatter.third(3)
+    scatter.third(0)
+    own.wait()
+    for d in range(1, 16):
+        arrived(home.at[(me + 16 - d) % 16], e2s.at[d], e2r.at[d], me, h)
+    scatter.last()
+    for copy in late:
+        copy.wait_send()
+
+
+def scatter_room(wide):
+    return [
+        pltpu.VMEM((4, 2, 128, wide // 2), bf16),
+        pltpu.VMEM((4, 2, 128, wide // 2), bf16),
+        pltpu.VMEM((4, 128, wide // 2), bf16),
+        pltpu.VMEM((4, 128, wide // 2), bf16),
+    ]
+
+
+def back(gm, t, wo, mid, cot, got, ratio, den):
+    mbs, count, wide = cot.shape
+    depth = 16 * count
+    shape = jax.ShapeDtypeStruct
+    cols = gm.shape[-1]
+    line = pltpu.VMEM((ZED, count, wide), bf16)
+    return pl.pallas_call(
+        back_kernel,
+        out_shape=(
+            shape((ZED, 128, cols), bf16),
+            shape(cot.shape, f32),
+            shape((mbs * count, wide), bf16),
+            shape((16, 2 * F + DV, count), bf16),
+        ),
+        in_specs=[ANY] * 3 + [VMEM] * 5,
+        out_specs=(VMEM,) * 4,
+        scratch_shapes=scatter_room(cols) + [
+            pltpu.VMEM((4, 128, cols // 2), bf16),
+            pltpu.VMEM((4, 128, cols // 2), bf16),
+            pltpu.VMEM((4, 128, cols), bf16),
+            pltpu.VMEM(cot.shape, bf16), line, line, line,
+            pltpu.VMEM(wo.shape, bf16),
+            pltpu.VMEM((16, count, DV), bf16),
+            pltpu.VMEM((depth, DV), bf16),
+            pltpu.VMEM((2 * F, depth), f32),
+            pltpu.VMEM((depth, DV), f32),
+            pltpu.VMEM((F, depth), bf16),
+            pltpu.VMEM((F, depth), bf16),
+            pltpu.VMEM((depth, 2 * DV), bf16),
+            pltpu.VMEM((depth, 2 * DV), bf16),
+            pltpu.VMEM((DV, depth), bf16),
+            pltpu.VMEM((16, 2 * F + DV, count), bf16),
+            DMA((6,)), DMA((4, 3)), DMA((4, 5)), DMA((4, 5)), DMA((4, 2)), DMA((4, 2)),
+            DMA((16,)), DMA((16,)), DMA((16,)), DMA((16,)),
+        ],
+        compiler_params=params(),
+        name="back",
+    )(gm.reshape(ZED, 2, 2, 128, cols), t, wo, mid, cot, got, ratio, den)
+
+
+def end_kernel(
+    t, home, xh, d_att, heads_out, wa1, d_mid, xin, mid,
+    za, d_in, outputs,
+    g, r1x, r1y, r2x, r2y, branch, other, summed, landed, w1, dqk_t, dqkv, part, swap,
+    ls, gs, gq, cs, cq, ws, wr,
+):
+    x, y, z, h = where_am_i()
+    me = index_of(z, y, x)
+    mbs, count, wide = xin.shape
+    heads = 16 // mbs
+    qk, vv = 2 * heads * F, heads * DV
+    late = []
+
+    def go(copy):
+        copy.start()
+        late.append(copy)
+
+    combine = Combine(t, branch, other, summed, landed, ls, cs, cq, go)
+    scatter = Scatter(
+        g,
+        lambda d: g.at[(z + d) % ZED, 1 - y, x, :, pl.ds(0, g.shape[-1] // 2)],
+        lambda d: g.at[(z + d) % ZED, y, 1 - x, :, pl.ds(g.shape[-1] // 2, g.shape[-1] // 2)],
+        lambda d: g.at[(z + d) % ZED, y, x],
+        za, r1x, r1y, r2x, r2y, gs, gq, go,
+    )
+    combine.begin()
+    weight = pltpu.make_async_copy(wa1, w1, ls.at[4])
+    weight.start()
+    for mb in range(mbs):
+        cols = slice(mb * count, (mb + 1) * count)
+        for k in range(heads):
+            block = home.at[k + heads * mb]
+            dqk_t[k * F : (k + 1) * F, cols] = block[0:F, :].astype(f32)
+            dqk_t[(heads + k) * F : (heads + k + 1) * F, cols] = block[F : 2 * F, :].astype(f32)
+            dqkv[cols, qk + k * DV : qk + (k + 1) * DV] = block[2 * F :, :]
+    dqkv[:, 0:qk] = jnp.transpose(dqk_t[...]).astype(bf16)
+    for n, d in enumerate(FAR):
+        zz = (z + d) % ZED
+        for yy in range(2):
+            for xx in range(2):
+                at = pl.ds(pl.multiple_of(index_of(zz, yy, xx) * 128, 128), 128)
+                g[zz, yy, xx, :, 0 : qk + vv] = mix(xh[:, at], dqkv[...], ((0,), (0,))).astype(bf16)
+                g[zz, yy, xx, :, qk + vv :] = mix(d_att[:, at], heads_out[...], ((0,), (0,))).astype(bf16)
+        scatter.first(d)
+        if n == 0:
+            combine.spread()
+    weight.wait()
+    for c in range(wide // COLS):
+        cols = pl.ds(c * COLS, COLS)
+        part[:, c * COLS : (c + 1) * COLS] = mix(dqkv[...], w1[c * COLS : (c + 1) * COLS, :], ((1,), (1,)))
+        go(remote(part.at[:, cols], swap.at[:, cols], ws.at[c], wr.at[c], me, 1 - h))
+    scatter.second(2)
+    for c in range(wide // COLS):
+        cols = pl.ds(c * COLS, COLS)
+        arrived(swap.at[:, cols], ws.at[c], wr.at[c], me, 1 - h)
+    for mb in range(mbs):
+
+        def body(turn, carry):
+            row = chunk(turn)
+            flat = pl.ds(pl.multiple_of(mb * count + turn * 16, 16), 16)
+            v = xin[mb, row, :].astype(f32)
+            scale = lax.rsqrt(jnp.mean(v * v, axis=-1, keepdims=True) + epsilon)
+            hat = v * scale
+            e = part[flat, :] + swap[flat, :]
+            d_in[mb, row, :] = (
+                d_mid[mb, row, :] + scale * (e - hat * jnp.mean(e * hat, axis=-1, keepdims=True))
+            ).astype(bf16)
+            return carry
+
+        lax.fori_loop(0, count // 16, body, 0)
+    scatter.second(1)
+    scatter.third(2)
+    scatter.second(3)
+    scatter.third(1)
+    scatter.second(0)
+    scatter.third(3)
+    combine.total()
+    scatter.third(0)
+    combine.done()
+    for mb in range(mbs):
+
+        def body(turn, carry):
+            row = chunk(turn)
+            outputs[mb, row, :] = (mid[mb, row, :] + branch[mb, row, :].astype(f32)).astype(bf16)
+            return carry
+
+        lax.fori_loop(0, count // 16, body, 0)
+    scatter.last()
+    for copy in late:
+        copy.wait_send()
+
+
+def end(t, home, xh, d_att, heads_out, wa1, d_mid, xin, mid):
+    mbs, count, wide = xin.shape
+    shape = jax.ShapeDtypeStruct
+    cols = wa1.shape[1] + heads_out.shape[1]
+    line = pltpu.VMEM((ZED, count, wide), bf16)
+    return pl.pallas_call(
+        end_kernel,
+        out_shape=(shape((ZED, 128, cols), bf16), shape(xin.shape, bf16), shape(xin.shape, bf16)),
+        in_specs=[ANY] + [VMEM] * 4 + [ANY] + [VMEM] * 3,
+        out_specs=(VMEM,) * 3,
+        scratch_shapes=[pltpu.VMEM((ZED, 2, 2, 128, cols), bf16)] + scatter_room(cols) + [
+            pltpu.VMEM(xin.shape, bf16), line, line, line,
+            pltpu.VMEM(wa1.shape, bf16),
+            pltpu.VMEM((mbs * count, mbs * count), f32),
+            pltpu.VMEM((mbs * count, wa1.shape[1]), bf16),
+            pltpu.VMEM((mbs * count, wide), f32),
+            pltpu.VMEM((mbs * count, wide), f32),
+            DMA((6,)), DMA((4, 5)), DMA((4, 5)), DMA((4, 2)), DMA((4, 2)),
+            DMA((wide // COLS,)), DMA((wide // COLS,)),
+        ],
+        compiler_params=params(),
+        name="end",
+    )(t, home, xh, d_att, heads_out, wa1, d_mid, xin, mid)
+
+
 def fast(
     inputs, norm_gain1, w_query, w_key, w_value, w_out, norm_gain2, w_gate, w_up, w_down, cotangent
 ):
@@ -889,9 +1042,7 @@
     xh1 = (stream * r1).astype(bf16)
     wa1, w_o, wm, got, ratio, den, heads_out, middle, near = front(a1, w_out.T, m, xh1, inputs)
     gg = share(cotangent)
-    w_qk, w_v = wa1[:, :qk], wa1[:, qk:]
     w_g, w_u, w_d = wm[:, :room], wm[:, room : 2 * room], wm[:, 2 * room :]
-    middle = middle.reshape(mbs * count, wide)
     many = ZED * mbs * count
     n2 = near.reshape(many, wide)
     up_g = gg.reshape(many, wide)
@@ -905,38 +1056,17 @@
     d_up = (d_hidden * silu).astype(bf16)
     branch = mix(hidden, w_d, ((1,), (1,))).astype(bf16)
     d_n2 = (mix(d_gate, w_g, ((1,), (1,))) + mix(d_up, w_u, ((1,), (1,)))).astype(bf16)
-    both = combine(jnp.stack([d_n2, branch]).reshape(2, ZED, mbs, count, wide))
-    e2 = both[0].reshape(mbs * count, wide).astype(f32)
-    outputs = (middle + both[1].reshape(mbs * count, wide).astype(f32)).astype(bf16)
-    r2 = lax.rsqrt(jnp.mean(middle * middle, axis=-1, keepdims=True) + epsilon)
-    xh2 = middle * r2
-    d_middle = cotangent.reshape(mbs * count, wide).astype(f32) + r2 * (
-        e2 - xh2 * jnp.mean(e2 * xh2, axis=-1, keepdims=True)
-    )
-    d_att = d_middle.astype(bf16)
-    d_heads = mix(d_att, w_o, ((1,), (0,))).astype(bf16)
-    d_heads = d_heads.reshape(mbs, count, heads, DV).transpose(0, 2, 1, 3).reshape(16, count, DV)
-    d_heads = exchange(d_heads).reshape(16 * count, DV)
-    d_qk, d_v = attend_back(got, ratio, den, d_heads)
-    d_qk = d_qk.astype(bf16).reshape(2 * F, 16, count).transpose(1, 0, 2)
-    home = exchange(jnp.concatenate([d_qk, d_v.astype(bf16).reshape(16, count, DV)], axis=1))
-    d_qk = home[:, : 2 * F].reshape(mbs, heads, 2, F, count).transpose(0, 4, 2, 1, 3)
-    d_qk = d_qk.reshape(mbs * count, qk)
-    d_val = home[:, 2 * F :].reshape(mbs, heads, count, DV).transpose(0, 2, 1, 3)
-    d_val = d_val.reshape(mbs * count, vv)
-    e1 = pair_sum(mix(d_qk, w_qk, ((1,), (1,))) + mix(d_val, w_v, ((1,), (1,))))
-    xh1f = stream * r1
-    input_grad = (
-        d_middle + r1 * (e1 - xh1f * jnp.mean(e1 * xh1f, axis=-1, keepdims=True))
-    ).astype(bf16)
     first = ((0,), (0,))
-    ga = jnp.concatenate(
-        [mix(xh1, d_qk, first), mix(xh1, d_val, first), mix(d_att, heads_out, first)], axis=1
-    ).astype(bf16)
     gm = jnp.concatenate(
         [mix(n2, d_gate, first), mix(n2, d_up, first), mix(up_g, hidden, first)], axis=1
     ).astype(bf16)
-    za, zm = scatter_all(ga, gm)
+    lines = (ZED, mbs, count, wide)
+    zm, d_mid, d_att, home = back(
+        gm, d_n2.reshape(lines), w_o, middle, cotangent, got, ratio, den
+    )
+    za, input_grad, outputs = end(
+        branch.reshape(lines), home, xh1, d_att, heads_out, wa1, d_mid, inputs, middle
+    )
     za = jnp.sum(za.astype(f32), axis=0)
     zm = zm.astype(f32)
 
@@ -953,8 +1083,8 @@
     g_gain2 = jnp.sum(w_gate.astype(f32) * g_gate, axis=1) + jnp.sum(w_up.astype(f32) * g_up, axis=1)
     gains = lax.psum(jnp.stack([g_gain1, g_gain2]), "head")
     return (
-        outputs.reshape(mbs, count, wide),
-        input_grad.reshape(mbs, count, wide),
+        outputs,
+        input_grad,
         gains[0],
         s_q * gain1,
         s_k * gain1,

time: 858 us -> 669 us (0.78)
  Pallas kernels: 670 us -> 547 us
  matrix products: 81.5 us -> 52.8 us
  other arithmetic: 49.6 us -> 25.2 us
  local copies, waits for them, and re-layouts: 45.4 us -> 36.1 us
    pallas_call x6 -> x2, Pallas kernels: 404 us -> 282 us  [the longest x1 149 us: back(): pl.pallas_call(back_kernel, out_shape=(shape((ZED, 128, cols), bf16), sha...]
    dot_general x15 -> x9, matrix products: 81.5 us -> 52.8 us  [mix(): return lax.dot_general(a, b, (over, ((), ())), preferred_element_type=f32)]
where the time goes in v3:
time: 669 us; the launch traced here: 665 us
  Pallas kernels  547 us (82%)
  matrix products  52.8 us (8%)
  local copies, waits for them, and re-layouts  36.1 us (5%)
  other arithmetic  25.2 us (4%)
    pallas_call x1, Pallas kernels, front(): pl.pallas_call(front_kernel, out_shape=(shape((wide, wide1), bf16), shape...  222 us
    pallas_call x1, Pallas kernels, back(): pl.pallas_call(back_kernel, out_shape=(shape((ZED, 128, cols), bf16), sha...  149 us
    pallas_call x1, Pallas kernels, end(): pl.pallas_call(end_kernel, out_shape=(shape((ZED, 128, cols), bf16), shap...  133 us
    dot_general x9, matrix products, mix(): return lax.dot_general(a, b, (over, ((), ())), preferred_element_type=f32)  52.8 us
    pallas_call x1, Pallas kernels, share(): pl.pallas_call(share_kernel, out_shape=jax.ShapeDtypeStruct((ZED,) + g.sh...  43.5 us

profile of v3, /device:TPU:0, one launch (start us, length us, event | category | flops | bytes accessed | tf_op | source)
XLA Modules:
  0.0 665.2 jit_solution(13361879065797866916)
XLA Ops:
  4.1 1.5 copy.28
  7.4 1.4 copy.31
  8.8 2.4 copy.32
  11.1 2.6 fusion.21.m
  14.0 1.2 fusion.22.xh
  16.1 222.3 %front.1 = (bf16[2048,1280]{1,0:T(8,128)(2,1)}, bf16[2048,1024]{1,0:T(8,128)(2,1)}, bf16[2048,2304]{1,0:T(8,128)(2,1)}, bf16[16,160,128]{2,1,0:T(8,128)(2,1)}, f...) custom-call(bf16[128,1280]{1,0:T(8,128)(2,1)} %pad_maximum_fusion.1., ...), custom_call_target="tpu_custom_call" | custom-call | tf_op jit(solution)/shard_map/front/pallas_call | solution.py:511
  238.4 8.3 %fusion.18 = f32[1024,768]{1,0:T(8,128)} fusion(bf16[1024,2048]{1,0:T(8,128)(2,1)} %bitcast.85, bf16[2048,2304]{1,0:T(8,128)(2,1)} %get-tuple-element.28), kind=kOutput, calls=%fused_computation.31 | convolution fusion | flops 3221225472 | bytes 10485760 | tf_op jit(solution)/shard_map/dot_general | solution.py:285
  246.8 43.5 %share.1 = bf16[4,2,128,2048]{3,2,1,0:T(8,128)(2,1)} custom-call(bf16[2,128,2048]{2,1,0:T(8,128)(2,1)} %cot.1), custom_call_target="tpu_custom_call" | custom-call | tf_op jit(solution)/shard_map/share/pallas_call | solution.py:605
  290.3 6.8 %fusion.10 = f32[768,1024]{0,1:T(8,128)S(1)} fusion(bf16[1024,2048]{1,0:T(8,128)(2,1)} %bitcast.83, bf16[2048,2304]{1,0:T(8,128)(2,1)} %get-tuple-element.28), kind=kOutput, calls=%fused_computation.23 | convolution fusion | flops 3221225472 | bytes 10485760 | tf_op jit(solution)/shard_map/dot_general | solution.py:285
  298.0 4.5 fusion.6
  302.5 3.5 fusion.16
  306.0 5.1 add_convert_fusion
  311.1 6.4 copy.33
  317.5 7.9 %convolution_convert_fusion.3 = bf16[4,2,2,128,768]{4,3,2,1,0:T(8,128)(2,1)} fusion(bf16[4,2,2,128,1024]{4,3,2,1,0:T(8,128)(2,1)} %bitcast.88, bf16[1024,768]{1,0:T(8,128)(2,1)} %copy-done.18), kind=kOutput, calls=%fused_computation.36 | convolution fusion | flops 3222798336 | bytes 8912896 | tf_op jit(solution)/shard_map/dot_general | solution.py:285
  325.4 5.0 convolution_convert_fusion.2
  330.3 4.8 fusion.9
  335.2 3.2 copy.35
  338.4 6.7 %pad_maximum_fusion.gm = bf16[4,2,2,128,2304]{4,3,2,1,0:T(8,128)(2,1)} fusion(bf16[4,2,2,128,768]{4,3,2,1,0:T(8,128)(2,1)S(1)} %bitcast.81, bf16[4,2,2,128,768]{4,3,2,1,0:T(8,128)(2,1)} %convolution_convert_fusion.2, bf16[4,2,2,128,768]{4,3,2,1,0:T(8,128)(2,1)} %convolution_convert_fusion.3), kind=kLoop, calls=%fused_computation | loop fusion | flops 28311552 | bytes 18874368 | tf_op jit(solution)/shard_map/concatenate | solution.py:1060
  345.1 148.9 %back.1 = (bf16[4,128,2304]{2,1,0:T(8,128)(2,1)}, f32[2,128,2048]{2,1,0:T(8,128)}, bf16[256,2048]{1,0:T(8,128)(2,1)}, bf16[16,160,128]{2,1,0:T(8,128)(2,1)}) custom-call(bf16[4,2,2,128,2304]{4,3,2,1,0:T(8,128)(2,1)} %pad_maximum_fusion.gm, bf16[4,2,128,2048]{3,2,1,0:T(8,128)(2,1)} %bitcast.90, bf16[2048,1024]{1,0:T(8,128)(2,1)} %get-tuple-element.29.wo, ...), custom_call_target="tpu_custom_call" | custom-call | tf_op jit(solution)/shard_map/back/pallas_call | solution.py:868
  494.0 2.1 convert_element_type.94
  496.1 2.1 slice_bitcast_fusion
  498.2 3.1 copy.36
  501.3 3.0 copy.37
  504.3 3.8 bitcast_multiply_fusion.3
  508.1 6.9 %convolution_convert_fusion = bf16[1024,2048]{1,0:T(8,128)(2,1)} fusion(bf16[1024,768]{1,0:T(8,128)(2,1)S(1)} %copy-done.17, bf16[2048,2304]{1,0:T(8,128)(2,1)} %get-tuple-element.28), kind=kOutput, calls=%fused_computation.11 | convolution fusion | flops 3223322624 | bytes 8912896 | tf_op jit(solution)/shard_map/dot_general | solution.py:285
  515.0 132.7 %end.1 = (bf16[4,128,2304]{2,1,0:T(8,128)(2,1)}, bf16[2,128,2048]{2,1,0:T(8,128)(2,1)}, bf16[2,128,2048]{2,1,0:T(8,128)(2,1)}) custom-call(bf16[4,2,128,2048]{3,2,1,0:T(8,128)(2,1)} %bitcast.82, bf16[16,160,128]{2,1,0:T(8,128)(2,1)} %get-tuple-element.34.home, bf16[256,2048]{1,0:T(8,128)(2,1)} %fusion.22.xh, bf16[256,2048]{1,0:T(8,128)(2,1)} %get-tuple-element.35.d_att, ...), custom_call_target="tpu_custom_call" | custom-call | tf_op jit(solution)/shard_map/end/pallas_call | solution.py:999
  647.7 2.2 convert_reduce_fusion
  651.7 2.5 psum.7
  654.7 2.9 copy.40
  657.6 1.5 copy.41
  659.1 1.6 copy.38
  661.7 2.3 copy.47
  (69 shorter events, 11.5 us)
Async XLA Ops:
  0.6 4.9 copy-start.11
  0.7 5.2 copy-start.15
  5.5 1.8 copy-start.1
  5.9 1.5 copy-start.3
  8.8 5.0 copy-start
  11.1 4.1 copy-start.12
  246.8 50.4 %slice-start = ((s8[9437184]{0:T(1024)(128)(4,1)}), s8[1048576]{0:T(1024)(128)(4,1)S(1)}, s32[]{:S(2)}) async-start(s8[9437184]{0:T(1024)(128)(4,1)} %bitcast.99), calls=%async_computation | async-start | bytes 2097152
  290.3 6.9 %copy-start.7 = (bf16[4,2,128,2048]{3,2,1,0:T(8,128)(2,1)S(1)}, bf16[4,2,128,2048]{3,2,1,0:T(8,128)(2,1)}, u32[]{:S(2)}) copy-start(bf16[4,2,128,2048]{3,2,1,0:T(8,128)(2,1)} %get-tuple-element.27) | copy-start | bytes 12582916
  290.3 6.9 %slice-start.1 = ((s8[9437184]{0:T(1024)(128)(4,1)}), s8[4194304]{0:T(1024)(128)(4,1)S(1)}, s32[]{:S(2)}) async-start(s8[9437184]{0:T(1024)(128)(4,1)} %bitcast.99), calls=%async_computation.1 | async-start | bytes 8388608
  290.3 6.9 %slice-start.2 = ((s8[9437184]{0:T(1024)(128)(4,1)}), s8[4194304]{0:T(1024)(128)(4,1)S(1)}, s32[]{:S(2)}) async-start(s8[9437184]{0:T(1024)(128)(4,1)} %bitcast.99), calls=%async_computation.2 | async-start | bytes 8388608
  290.3 7.7 %copy-start.19 = (f32[1024,768]{1,0:T(8,128)S(1)}, f32[1024,768]{1,0:T(8,128)}, u32[]{:S(2)}) copy-start(f32[1024,768]{1,0:T(8,128)} %fusion.18) | copy-start | bytes 9437188
  302.5 3.5 copy-start.18
  302.5 3.5 copy-start.20
  302.5 27.8 %copy-start.16 = (bf16[1024,768]{1,0:T(8,128)(2,1)}, bf16[1024,768]{1,0:T(8,128)(2,1)S(1)}, u32[]{:S(2)}) copy-start(bf16[1024,768]{1,0:T(8,128)(2,1)S(1)} %get-tuple-element.69) | copy-start | bytes 4718596
  317.5 7.9 %copy-start.8 = (bf16[2048,1024]{1,0:T(8,128)(2,1)S(1)}, bf16[2048,1024]{1,0:T(8,128)(2,1)}, u32[]{:S(2)}) copy-start(bf16[2048,1024]{1,0:T(8,128)(2,1)} %copy.33) | copy-start | bytes 12582916
  317.5 7.9 %copy-start.21 = (bf16[1024,768]{1,0:T(8,128)(2,1)S(1)}, bf16[1024,768]{1,0:T(8,128)(2,1)}, u32[]{:S(2)}) copy-start(bf16[1024,768]{1,0:T(8,128)(2,1)} %copy-done.20) | copy-start | bytes 4718596
  325.4 5.0 copy-start.6
  498.2 6.1 copy-start.2
  498.2 6.1 copy-start.4
  504.2 3.8 copy-start.17
  647.7 2.2 copy-start.9
  647.7 3.1 copy-start.13
  647.7 3.1 copy-start.14
  649.9 7.7 %copy-start.5 = (f32[128,2816]{0,1:T(8,128)S(1)}, f32[128,2816]{0,1:T(8,128)}, u32[]{:S(2)}) copy-start(f32[128,2816]{0,1:T(8,128)} %get-tuple-element.73) | copy-start | bytes 4325380
  659.1 4.9 copy-start.10

commit v4 on v3

--- a/solution.py
+++ b/solution.py
@@ -319,10 +319,10 @@
 
 
 def front_kernel(
-    a1, a2, m, xh, xin,
-    wa1, wa2, wm, got, ratio, den, heads_out, middle, near,
+    a1, a2, m, cot, xh, xin,
+    wa1, wa2, wm, gg, got, ratio, den, heads_out, middle, near,
     w1, w2, pack, q_t, k_t, va, ob, part, other,
-    ls, zs, zr, ps, pr, e1s, e1r, e2s, e2r, ws, wr, ns, nr, ds, dr,
+    ls, zs, zr, us, ur, ps, pr, e1s, e1r, e2s, e2r, ws, wr, ds, dr,
 ):
     x, y, z, h = where_am_i()
     me = index_of(z, y, x)
@@ -331,9 +331,15 @@
     heads = 16 // xin.shape[0]
     late = []
 
-    def go(copy):
-        copy.start()
-        late.append(copy)
+    def when(true, do):
+        if true is None:
+            do()
+        else:
+            pl.when(true)(do)
+
+    def go(copy, true=None):
+        when(true, copy.start)
+        late.append((true, copy))
 
     def rows(zz, yy, xx):
         return pl.ds(pl.multiple_of(index_of(zz, yy, xx) * 128, 128), 128)
@@ -343,57 +349,145 @@
         pltpu.make_async_copy(a1, w1.at[mine], ls.at[0]),
         pltpu.make_async_copy(a2, w2.at[mine], ls.at[1]),
         pltpu.make_async_copy(m.at[z], wm.at[mine], ls.at[2]),
+        pltpu.make_async_copy(cot, gg.at[z], ls.at[6]),
     ]
     for copy in kept:
         copy.start()
     dest = (w1, w2, wm)
-
-    def line(kind):
+    UP, DOWN = 0, 1
+    COT, NEAR = 2, 3
+
+    def held(kind, zz):
+        return (lambda: w1.at[rows(zz, y, x)], lambda: w2.at[rows(zz, y, x)],
+                lambda: gg.at[zz, h], lambda: near.at[zz, h])[kind]()
+
+    def origin(way, step):
+        return (z + ZED - step) % ZED if way == UP else (z + step) % ZED
+
+    def valid(way, step):
+        return z >= step if way == UP else z <= ZED - 1 - step
+
+    def pass_on(kind, way, step, src, true):
+        there = index_of((z + 1) % ZED if way == UP else (z + ZED - 1) % ZED, y, x)
+        block = held(kind, origin(way, step))
+        go(remote(block if src is None else src, block, us.at[kind, way, step], ur.at[kind, way, step + 1], there, h), true)
+
+    def offer(kind, src=None):
+        pass_on(kind, UP, 0, src, z < ZED - 1)
+        pass_on(kind, DOWN, 0, src, z > 0)
+
+    def hop(kind, way, step):
+        block = held(kind, origin(way, step))
+        when(
+            valid(way, step),
+            lambda: arrived(block, us.at[kind, way, step], ur.at[kind, way, step], me, h),
+        )
+        if step < ZED - 1:
+            more = z < ZED - 1 if way == UP else z > 0
+            pass_on(kind, way, step, None, valid(way, step) & more)
+
+    def across(kind, way, step):
+        zz = origin(way, step)
+        block = held(kind, zz)
+        go(remote(block, block, ds.at[kind, way, step], dr.at[kind, way, step], me, 1 - h), valid(way, step))
+
+    def across_done(kind, way, step):
+        zz = origin(way, step)
+        block = (gg if kind == COT else near).at[zz, 1 - h]
+        when(
+            valid(way, step),
+            lambda: arrived(block, ds.at[kind, way, step], dr.at[kind, way, step], me, 1 - h),
+        )
+
+    def both(do, kind, step):
+        do(kind, UP, step)
+        do(kind, DOWN, step)
+
+    def line():
         for d in (1, 3, 2):
             zz = (z + d) % ZED
-            src = (a1, a2, m.at[zz])[kind]
-            go(remote(src, dest[kind].at[mine], zs.at[kind, d], zr.at[kind, d], index_of(zz, y, x), h))
-
-    def plane(kind, d):
-        block = dest[kind].at[rows((z + ZED - d) % ZED, y, x)]
-        if d:
-            arrived(block, zs.at[kind, d], zr.at[kind, d], me, h)
-        else:
-            kept[kind].wait()
-        go(remote(block, block, ps.at[kind, d, 0], pr.at[kind, d, 0], at_x, h))
-        go(remote(block, block, ps.at[kind, d, 1], pr.at[kind, d, 1], at_y, h))
-
-    def onward(kind, d):
+            go(remote(m.at[zz], wm.at[mine], zs.at[d], zr.at[d], index_of(zz, y, x), h))
+
+    def slot_of(way, step):
+        return step if way == UP else 3 + step if step else 0
+
+    def plane_set(kind, slot, zz, true):
+        block = dest[kind].at[rows(zz, y, x)]
+        go(remote(block, block, ps.at[kind, slot, 0], pr.at[kind, slot, 0], at_x, h), true)
+        go(remote(block, block, ps.at[kind, slot, 1], pr.at[kind, slot, 1], at_y, h), true)
+
+    def onward_set(kind, slot, zz, true):
         w = dest[kind]
-        zz = (z + ZED - d) % ZED
         half = w.shape[1] // 2
         from_x, from_y = rows(zz, y, 1 - x), rows(zz, 1 - y, x)
-        arrived(w.at[from_x], ps.at[kind, d, 0], pr.at[kind, d, 0], me, h)
-        arrived(w.at[from_y], ps.at[kind, d, 1], pr.at[kind, d, 1], me, h)
+
+        def wait():
+            arrived(w.at[from_x], ps.at[kind, slot, 0], pr.at[kind, slot, 0], me, h)
+            arrived(w.at[from_y], ps.at[kind, slot, 1], pr.at[kind, slot, 1], me, h)
+
+        when(true, wait)
         left = w.at[from_y, pl.ds(0, half)]
         right = w.at[from_x, pl.ds(half, half)]
-        go(remote(left, left, ps.at[kind, d, 2], pr.at[kind, d, 2], at_x, h))
-        go(remote(right, right, ps.at[kind, d, 3], pr.at[kind, d, 3], at_y, h))
-
-    def corner(kind):
+        go(remote(left, left, ps.at[kind, slot, 2], pr.at[kind, slot, 2], at_x, h), true)
+        go(remote(right, right, ps.at[kind, slot, 3], pr.at[kind, slot, 3], at_y, h), true)
+
+    def corner_set(kind, slot, zz, true):
         w = dest[kind]
         half = w.shape[1] // 2
-        for d in ORDER:
-            far = rows((z + ZED - d) % ZED, 1 - y, 1 - x)
-            arrived(w.at[far, pl.ds(0, half)], ps.at[kind, d, 2], pr.at[kind, d, 2], me, h)
-            arrived(w.at[far, pl.ds(half, half)], ps.at[kind, d, 3], pr.at[kind, d, 3], me, h)
-
-    line(0)
-    plane(0, 0)
-    plane(0, 1)
-    onward(0, 0)
-    plane(0, 3)
-    line(1)
-    onward(0, 1)
-    plane(0, 2)
-    onward(0, 3)
-    plane(1, 0)
-    onward(0, 2)
+        far = rows(zz, 1 - y, 1 - x)
+
+        def wait():
+            arrived(w.at[far, pl.ds(0, half)], ps.at[kind, slot, 2], pr.at[kind, slot, 2], me, h)
+            arrived(w.at[far, pl.ds(half, half)], ps.at[kind, slot, 3], pr.at[kind, slot, 3], me, h)
+
+        when(true, wait)
+
+    def plane(kind, way, step):
+        if step == 0:
+            kept[kind].wait()
+        plane_set(kind, slot_of(way, step), origin(way, step), valid(way, step) if step else None)
+
+    def onward(kind, way, step):
+        onward_set(kind, slot_of(way, step), origin(way, step), valid(way, step) if step else None)
+
+    def corner(kind):
+        corner_set(kind, 0, z, None)
+        for step in (1, 2, 3):
+            for way in (UP, DOWN):
+                corner_set(kind, slot_of(way, step), origin(way, step), valid(way, step))
+
+    def m_plane(d):
+        zz = (z + ZED - d) % ZED
+        if d:
+            arrived(wm.at[rows(zz, y, x)], zs.at[d], zr.at[d], me, h)
+        else:
+            kept[2].wait()
+        plane_set(2, d, zz, None)
+
+    def m_onward(d):
+        onward_set(2, d, (z + ZED - d) % ZED, None)
+
+    offer(0, a1)
+    plane(0, UP, 0)
+    for way in (UP, DOWN):
+        hop(0, way, 1)
+        plane(0, way, 1)
+    offer(1, a2)
+    onward(0, UP, 0)
+    for way in (UP, DOWN):
+        hop(0, way, 2)
+        plane(0, way, 2)
+    both(onward, 0, 1)
+    both(hop, 1, 1)
+    for way in (UP, DOWN):
+        hop(0, way, 3)
+        plane(0, way, 3)
+    both(onward, 0, 2)
+    both(hop, 1, 2)
+    plane(1, UP, 0)
+    both(onward, 0, 3)
+    both(hop, 1, 3)
+    both(plane, 1, 1)
     corner(0)
     out1 = pltpu.make_async_copy(w1, wa1, ls.at[3])
     out1.start()
@@ -417,18 +511,17 @@
     for d in range(1, 16):
         there = (me + d) % 16
         go(remote(pack.at[there], got.at[me], e1s.at[d], e1r.at[d], there, h))
-    plane(1, 1)
-    onward(1, 0)
-    plane(1, 3)
-    onward(1, 1)
-    plane(1, 2)
-    onward(1, 3)
+    line()
+    onward(1, UP, 0)
+    both(plane, 1, 2)
+    both(onward, 1, 1)
+    both(plane, 1, 3)
+    both(onward, 1, 2)
     keep.wait()
     for d in range(1, 16):
         arrived(got.at[(me + 16 - d) % 16], e1s.at[d], e1r.at[d], me, h)
-    line(2)
-    plane(2, 0)
-    onward(1, 2)
+    m_plane(0)
+    both(onward, 1, 3)
     spread(got, q_t, k_t, va)
     causal = lower(CHUNK)
     for qi in range(va.shape[0] // CHUNK):
@@ -447,7 +540,7 @@
     for d in range(1, 16):
         there = (me + d) % 16
         go(remote(ob.at[there], window(me), e2s.at[d], e2r.at[d], there, h))
-    onward(2, 0)
+    m_onward(0)
     corner(1)
     out2 = pltpu.make_async_copy(w2, wa2, ls.at[5])
     out2.start()
@@ -455,13 +548,14 @@
     for d in range(1, 16):
         arrived(window((me + 16 - d) % 16), e2s.at[d], e2r.at[d], me, h)
     wide = part.shape[1]
-    swaps = []
     for c in range(wide // COLS):
         cols = pl.ds(c * COLS, COLS)
         part[:, c * COLS : (c + 1) * COLS] = mix(
             heads_out[...], w2[c * COLS : (c + 1) * COLS, :], ((1,), (1,))
         )
         go(remote(part.at[:, cols], other.at[:, cols], ws.at[c], wr.at[c], me, 1 - h))
+    m_plane(1)
+    m_plane(3)
     for c in range(wide // COLS):
         cols = pl.ds(c * COLS, COLS)
         arrived(other.at[:, cols], ws.at[c], wr.at[c], me, 1 - h)
@@ -479,31 +573,38 @@
         lax.fori_loop(0, count // 16, body, 0)
 
     one(h)
-    for d in (2, 1, 3):
-        there = index_of((z + d) % ZED, y, x)
-        go(remote(near.at[z, h], near.at[z, h], ns.at[d], nr.at[d], there, h))
+    offer(NEAR)
+    offer(COT, cot.at[h])
     one(1 - h)
-    plane(2, 1)
-    plane(2, 3)
-    onward(2, 1)
-    plane(2, 2)
-    onward(2, 3)
-    for d in (1, 3, 2):
-        zz = (z + ZED - d) % ZED
-        arrived(near.at[zz, h], ns.at[d], nr.at[d], me, h)
-        go(remote(near.at[zz, h], near.at[zz, h], ds.at[d], dr.at[d], me, 1 - h))
-    onward(2, 2)
-    corner(2)
-    for d in (1, 3, 2):
-        zz = (z + ZED - d) % ZED
-        arrived(near.at[zz, 1 - h], ds.at[d], dr.at[d], me, 1 - h)
+    kept[3].wait()
+    m_onward(1)
+    m_onward(3)
+    both(hop, NEAR, 1)
+    both(across, NEAR, 1)
+    both(hop, COT, 1)
+    both(across, COT, 1)
+    m_plane(2)
+    both(hop, NEAR, 2)
+    both(across, NEAR, 2)
+    both(hop, COT, 2)
+    both(across, COT, 2)
+    m_onward(2)
+    both(hop, NEAR, 3)
+    both(across, NEAR, 3)
+    both(hop, COT, 3)
+    both(across, COT, 3)
+    for d in ORDER:
+        corner_set(2, d, (z + ZED - d) % ZED, None)
+    for kind in (NEAR, COT):
+        for step in (1, 2, 3):
+            both(across_done, kind, step)
     out1.wait()
     out2.wait()
-    for copy in late:
-        copy.wait_send()
-
-
-def front(a1, a2, m, xh, xin):
+    for true, copy in late:
+        when(true, copy.wait_send)
+
+
+def front(a1, a2, m, cot, xh, xin):
     mbs, count, wide = xin.shape
     depth = 16 * count
     wide1, wide2 = a1.shape[1], a2.shape[1]
@@ -514,6 +615,7 @@
             shape((wide, wide1), bf16),
             shape((wide, wide2), bf16),
             shape((wide, m.shape[2]), bf16),
+            shape((ZED,) + cot.shape, bf16),
             shape((16, 2 * F + DV, count), bf16),
             shape((depth, DV), f32),
             shape((depth, DV), f32),
@@ -521,8 +623,8 @@
             shape(xin.shape, f32),
             shape((ZED,) + xin.shape, bf16),
         ),
-        in_specs=[ANY] * 3 + [VMEM] * 2,
-        out_specs=(ANY,) * 3 + (VMEM,) * 6,
+        in_specs=[ANY] * 4 + [VMEM] * 2,
+        out_specs=(ANY,) * 4 + (VMEM,) * 6,
         scratch_shapes=[
             pltpu.VMEM((wide, wide1), bf16),
             pltpu.VMEM((wide, wide2), bf16),
@@ -533,13 +635,13 @@
             pltpu.VMEM((16, count, DV), bf16),
             pltpu.VMEM((mbs * count, wide), f32),
             pltpu.VMEM((mbs * count, wide), f32),
-            DMA((6,)), DMA((3, 4)), DMA((3, 4)), DMA((3, 4, 4)), DMA((3, 4, 4)),
+            DMA((7,)), DMA((4,)), DMA((4,)), DMA((4, 2, 4)), DMA((4, 2, 4)), DMA((3, 7, 4)), DMA((3, 7, 4)),
             DMA((16,)), DMA((16,)), DMA((16,)), DMA((16,)),
-            DMA((wide // COLS,)), DMA((wide // COLS,)), DMA((4,)), DMA((4,)), DMA((4,)), DMA((4,)),
+            DMA((wide // COLS,)), DMA((wide // COLS,)), DMA((4, 2, 4)), DMA((4, 2, 4)),
         ],
         compiler_params=params(),
         name="front",
-    )(a1, a2, m, xh, xin)
+    )(a1, a2, m, cot, xh, xin)
 
 
 def attend_back_body(got, ratio, den, d_o, d_qk, d_v, q_t, k_t, va, da, dn_t):
@@ -574,43 +676,6 @@
             d_qk[0:F, qs] = d_q if kj == 0 else d_qk[0:F, qs] + d_q
         d_qk[F : 2 * F, ks] = acc_k
         d_v[ks, :] = jnp.transpose(acc_v)
-
-
-def share_kernel(g, gg, ls, zs, zr, ds, dr):
-    x, y, z, h = where_am_i()
-    me = index_of(z, y, x)
-    local = pltpu.make_async_copy(g, gg.at[z], ls)
-    local.start()
-    copies = []
-    for d in (2, 1, 3):
-        there = index_of((z + d) % ZED, y, x)
-        copies.append(remote(g.at[h], gg.at[z, h], zs.at[d], zr.at[d], there, h))
-    for copy in copies:
-        copy.start()
-    for d in (1, 3, 2):
-        zz = (z + ZED - d) % ZED
-        arrived(gg.at[zz, h], zs.at[d], zr.at[d], me, h)
-        copy = remote(gg.at[zz, h], gg.at[zz, h], ds.at[d], dr.at[d], me, 1 - h)
-        copy.start()
-        copies.append(copy)
-    for d in (1, 3, 2):
-        zz = (z + ZED - d) % ZED
-        arrived(gg.at[zz, 1 - h], ds.at[d], dr.at[d], me, 1 - h)
-    local.wait()
-    for copy in copies:
-        copy.wait_send()
-
-
-def share(g):
-    return pl.pallas_call(
-        share_kernel,
-        out_shape=jax.ShapeDtypeStruct((ZED,) + g.shape, bf16),
-        in_specs=[ANY],
-        out_specs=ANY,
-        scratch_shapes=[DMA, DMA((4,)), DMA((4,)), DMA((4,)), DMA((4,))],
-        compiler_params=params(),
-        name="share",
-    )(g)
 
 
 FAR = (2, 1, 3, 0)
@@ -1040,8 +1105,9 @@
     stream = inputs.astype(f32).reshape(mbs * count, wide)
     r1 = lax.rsqrt(jnp.mean(stream * stream, axis=-1, keepdims=True) + epsilon)
     xh1 = (stream * r1).astype(bf16)
-    wa1, w_o, wm, got, ratio, den, heads_out, middle, near = front(a1, w_out.T, m, xh1, inputs)
-    gg = share(cotangent)
+    wa1, w_o, wm, gg, got, ratio, den, heads_out, middle, near = front(
+        a1, w_out.T, m, cotangent, xh1, inputs
+    )
     w_g, w_u, w_d = wm[:, :room], wm[:, room : 2 * room], wm[:, 2 * room :]
     many = ZED * mbs * count
     n2 = near.reshape(many, wide)

time: 669 us -> 612 us (0.915)
  Pallas kernels: 547 us -> 488 us
    pallas_call x1 -> x0, Pallas kernels: 43.5 us -> none  [share(): pl.pallas_call(share_kernel, out_shape=jax.ShapeDtypeStruct((ZED,) + g.sh...]
    pallas_call x1, Pallas kernels: 149 us -> 137 us  [back(): pl.pallas_call(back_kernel, out_shape=(shape((ZED, 128, cols), bf16), sha...]
    unnamed x58 -> x46, local copies, waits for them, and re-layouts: 12.3 us -> 13.6 us
where the time goes in v4:
time: 612 us; the launch traced here: 608 us
  Pallas kernels  488 us (80%)
  matrix products  53.7 us (9%)
  local copies, waits for them, and re-layouts  40.2 us (7%)
  other arithmetic  22.5 us (4%)
    pallas_call x1, Pallas kernels, front(): pl.pallas_call(front_kernel, out_shape=(shape((wide, wide1), bf16), shape...  219 us
    pallas_call x1, Pallas kernels, back(): pl.pallas_call(back_kernel, out_shape=(shape((ZED, 128, cols), bf16), sha...  137 us
    pallas_call x1, Pallas kernels, end(): pl.pallas_call(end_kernel, out_shape=(shape((ZED, 128, cols), bf16), shap...  133 us
    dot_general x9, matrix products, mix(): return lax.dot_general(a, b, (over, ((), ())), preferred_element_type=f32)  53.7 us
    unnamed x46, local copies, waits for them, and re-layouts  13.6 us
    dot_general x2, local copies, waits for them, and re-layouts, mix(): return lax.dot_general(a, b, (over, ((), ())), preferred_element_type=f32)  13 us

profile of v4, /device:TPU:0, one launch (start us, length us, event | category | flops | bytes accessed | tf_op | source)
XLA Modules:
  0.0 608.3 jit_solution(10980873612485982175)
XLA Ops:
  4.1 1.5 copy.27
  7.0 1.4 copy.28
  8.4 1.2 copy.30
  9.6 2.4 copy.31
  12.0 2.6 fusion.16.m
  14.9 1.2 fusion.17.xh
  16.9 218.6 %front.1 = (bf16[2048,1280]{1,0:T(8,128)(2,1)}, bf16[2048,1024]{1,0:T(8,128)(2,1)}, bf16[2048,2304]{1,0:T(8,128)(2,1)}, bf16[4,2,128,2048]{3,2,1,0:T(8,128)(2,1)...) custom-call(bf16[128,1280]{1,0:T(8,128)(2,1)} %pad_maximum_fusion.1., ...), custom_call_target="tpu_custom_call" | custom-call | tf_op jit(solution)/shard_map/front/pallas_call | solution.py:612
  235.5 6.3 %fusion.9 = f32[1024,768]{1,0:T(8,128)S(1)} fusion(bf16[1024,2048]{1,0:T(8,128)(2,1)} %bitcast.77, bf16[2048,2304]{1,0:T(8,128)(2,1)} %get-tuple-element.29), kind=kOutput, calls=%fused_computation.21 | convolution fusion | flops 3221225472 | bytes 10485760 | tf_op jit(solution)/shard_map/dot_general | solution.py:285
  242.7 3.4 fusion.5
  246.1 6.1 multiply_convert_fusion.1
  252.2 5.7 fusion.11
  257.9 7.3 %add_convert_fusion = bf16[1024,2048]{1,0:T(8,128)(2,1)} fusion(f32[1024,2048]{1,0:T(8,128)} %fusion.11, bf16[1024,768]{1,0:T(8,128)(2,1)S(1)} %get-tuple-element.70, bf16[2048,2304]{1,0:T(8,128)(2,1)S(1)} %copy-done.13), kind=kOutput, calls=%fused_computation.1 | convolution fusion | flops 3225419776 | bytes 17301504 | tf_op jit(solution)/shard_map/dot_general | solution.py:285
  265.2 6.5 %copy.32 = bf16[2048,1024]{1,0:T(8,128)(2,1)} copy(bf16[2048,1024]{0,1:T(8,128)(2,1)} %bitcast.78) | data formatting | bytes 8388608 | tf_op jit(solution)/shard_map/dot_general | solution.py:285
  271.7 7.5 %convolution_convert_fusion.3 = bf16[4,2,2,128,768]{4,3,2,1,0:T(8,128)(2,1)} fusion(bf16[4,2,2,128,1024]{4,3,2,1,0:T(8,128)(2,1)} %bitcast.80, bf16[1024,768]{1,0:T(8,128)(2,1)S(1)} %get-tuple-element.69), kind=kOutput, calls=%fused_computation.31 | convolution fusion | flops 3222798336 | bytes 8912896 | tf_op jit(solution)/shard_map/dot_general | solution.py:285
  279.2 4.8 convolution_convert_fusion.2
  283.9 6.5 %copy.33 = bf16[2048,1024]{1,0:T(8,128)(2,1)} copy(bf16[2048,1024]{0,1:T(8,128)(2,1)} %bitcast.75) | data formatting | bytes 8388608 | tf_op jit(solution)/shard_map/dot_general | solution.py:285
  290.4 5.8 convolution_convert_fusion.1
  296.2 4.0 pad_maximum_fusion.gm
  300.2 136.9 %back.1 = (bf16[4,128,2304]{2,1,0:T(8,128)(2,1)}, f32[2,128,2048]{2,1,0:T(8,128)}, bf16[256,2048]{1,0:T(8,128)(2,1)}, bf16[16,160,128]{2,1,0:T(8,128)(2,1)}) custom-call(bf16[4,2,2,128,2304]{4,3,2,1,0:T(8,128)(2,1)} %pad_maximum_fusion.gm, bf16[4,2,128,2048]{3,2,1,0:T(8,128)(2,1)} %bitcast.83, bf16[2048,1024]{1,0:T(8,128)(2,1)} %get-tuple-element.31.wo, ...), custom_call_target="tpu_custom_call" | custom-call | tf_op jit(solution)/shard_map/back/pallas_call | solution.py:933
  437.1 2.1 convert_element_type.94
  439.2 2.1 slice_bitcast_fusion
  441.3 3.0 copy.34
  444.3 1.6 copy.35
  445.9 3.9 bitcast_multiply_fusion.1
  449.7 6.9 %convolution_convert_fusion = bf16[1024,2048]{1,0:T(8,128)(2,1)} fusion(bf16[1024,768]{1,0:T(8,128)(2,1)S(1)} %copy-done.16, bf16[2048,2304]{1,0:T(8,128)(2,1)} %get-tuple-element.29), kind=kOutput, calls=%fused_computation.11 | convolution fusion | flops 3223322624 | bytes 8912896 | tf_op jit(solution)/shard_map/dot_general | solution.py:285
  456.6 132.8 %end.1 = (bf16[4,128,2304]{2,1,0:T(8,128)(2,1)}, bf16[2,128,2048]{2,1,0:T(8,128)(2,1)}, bf16[2,128,2048]{2,1,0:T(8,128)(2,1)}) custom-call(bf16[4,2,128,2048]{3,2,1,0:T(8,128)(2,1)} %bitcast.74, bf16[16,160,128]{2,1,0:T(8,128)(2,1)} %get-tuple-element.36.home, bf16[256,2048]{1,0:T(8,128)(2,1)} %fusion.17.xh, bf16[256,2048]{1,0:T(8,128)(2,1)} %get-tuple-element.37.d_att, ...), custom_call_target="tpu_custom_call" | custom-call | tf_op jit(solution)/shard_map/end/pallas_call | solution.py:1064
  589.5 2.2 convert_reduce_fusion
  593.4 2.5 psum.7
  596.4 2.9 copy.38
  599.3 2.9 copy.39
  602.2 1.6 copy.36
  604.8 2.3 copy.45
  (55 shorter events, 11.2 us)
Async XLA Ops:
  0.6 4.9 copy-start.9
  0.7 5.2 copy-start.14
  9.6 5.0 copy-start
  12.0 4.1 copy-start.10
  235.5 6.3 %copy-start.2 = (bf16[4,2,128,2048]{3,2,1,0:T(8,128)(2,1)S(1)}, bf16[4,2,128,2048]{3,2,1,0:T(8,128)(2,1)}, u32[]{:S(2)}) copy-start(bf16[4,2,128,2048]{3,2,1,0:T(8,128)(2,1)} %get-tuple-element.30) | copy-start | bytes 12582916
  235.5 7.1 %copy-start.13 = (bf16[2048,2304]{1,0:T(8,128)(2,1)S(1)}, bf16[2048,2304]{1,0:T(8,128)(2,1)}, u32[]{:S(2)}) copy-start(bf16[2048,2304]{1,0:T(8,128)(2,1)} %get-tuple-element.29) | copy-start | bytes 28311556
  242.7 3.4 copy-start.3
  252.2 5.7 copy-start.17
  271.7 7.5 %copy-start.4 = (bf16[2048,1024]{1,0:T(8,128)(2,1)S(1)}, bf16[2048,1024]{1,0:T(8,128)(2,1)}, u32[]{:S(2)}) copy-start(bf16[2048,1024]{1,0:T(8,128)(2,1)} %copy.32) | copy-start | bytes 12582916
  271.7 7.5 %copy-start.18 = (bf16[1024,768]{1,0:T(8,128)(2,1)S(1)}, bf16[1024,768]{1,0:T(8,128)(2,1)}, u32[]{:S(2)}) copy-start(bf16[1024,768]{1,0:T(8,128)(2,1)} %copy-done.17) | copy-start | bytes 4718596
  283.9 6.5 %copy-start.15 = (bf16[1024,768]{1,0:T(8,128)(2,1)S(1)}, bf16[1024,768]{1,0:T(8,128)(2,1)}, u32[]{:S(2)}) copy-start(bf16[1024,768]{1,0:T(8,128)(2,1)} %get-tuple-element.71) | copy-start | bytes 4718596
  290.4 5.8 copy-start.5
  290.4 5.8 copy-start.6
  445.9 3.9 copy-start.16
  589.5 2.2 copy-start.7
  589.5 3.1 copy-start.11
  589.5 3.1 copy-start.12
  592.6 9.6 %copy-start.1 = (f32[128,4,704]{2,0,1:T(8,128)S(1)}, f32[128,4,704]{2,0,1:T(8,128)}, u32[]{:S(2)}) copy-start(f32[128,4,704]{2,0,1:T(8,128)} %get-tuple-element.72) | copy-start | bytes 4325380
  602.2 4.9 copy-start.8

commit v5 on v4

--- a/solution.py
+++ b/solution.py
@@ -403,10 +403,11 @@
         do(kind, UP, step)
         do(kind, DOWN, step)
 
-    def line():
-        for d in (1, 3, 2):
-            zz = (z + d) % ZED
-            go(remote(m.at[zz], wm.at[mine], zs.at[d], zr.at[d], index_of(zz, y, x), h))
+    partner = (z, z + 1 - 2 * (z % 2), ZED - 1 - z, (z + 2) % ZED)
+
+    def line(d):
+        zz = partner[d]
+        go(remote(m.at[zz], wm.at[mine], zs.at[d], zr.at[d], index_of(zz, y, x), h))
 
     def slot_of(way, step):
         return step if way == UP else 3 + step if step else 0
@@ -457,7 +458,7 @@
                 corner_set(kind, slot_of(way, step), origin(way, step), valid(way, step))
 
     def m_plane(d):
-        zz = (z + ZED - d) % ZED
+        zz = partner[d]
         if d:
             arrived(wm.at[rows(zz, y, x)], zs.at[d], zr.at[d], me, h)
         else:
@@ -465,29 +466,31 @@
         plane_set(2, d, zz, None)
 
     def m_onward(d):
-        onward_set(2, d, (z + ZED - d) % ZED, None)
+        onward_set(2, d, partner[d], None)
 
     offer(0, a1)
     plane(0, UP, 0)
     for way in (UP, DOWN):
         hop(0, way, 1)
         plane(0, way, 1)
-    offer(1, a2)
     onward(0, UP, 0)
     for way in (UP, DOWN):
         hop(0, way, 2)
         plane(0, way, 2)
+    offer(1, a2)
     both(onward, 0, 1)
-    both(hop, 1, 1)
     for way in (UP, DOWN):
         hop(0, way, 3)
         plane(0, way, 3)
     both(onward, 0, 2)
-    both(hop, 1, 2)
+    both(hop, 1, 1)
     plane(1, UP, 0)
     both(onward, 0, 3)
+    both(hop, 1, 2)
+    both(plane, 1, 1)
     both(hop, 1, 3)
-    both(plane, 1, 1)
+    line(1)
+    line(2)
     corner(0)
     out1 = pltpu.make_async_copy(w1, wa1, ls.at[3])
     out1.start()
@@ -511,7 +514,6 @@
     for d in range(1, 16):
         there = (me + d) % 16
         go(remote(pack.at[there], got.at[me], e1s.at[d], e1r.at[d], there, h))
-    line()
     onward(1, UP, 0)
     both(plane, 1, 2)
     both(onward, 1, 1)
@@ -520,7 +522,7 @@
     keep.wait()
     for d in range(1, 16):
         arrived(got.at[(me + 16 - d) % 16], e1s.at[d], e1r.at[d], me, h)
-    m_plane(0)
+    line(3)
     both(onward, 1, 3)
     spread(got, q_t, k_t, va)
     causal = lower(CHUNK)
@@ -540,7 +542,7 @@
     for d in range(1, 16):
         there = (me + d) % 16
         go(remote(ob.at[there], window(me), e2s.at[d], e2r.at[d], there, h))
-    m_onward(0)
+    m_plane(0)
     corner(1)
     out2 = pltpu.make_async_copy(w2, wa2, ls.at[5])
     out2.start()
@@ -554,8 +556,8 @@
             heads_out[...], w2[c * COLS : (c + 1) * COLS, :], ((1,), (1,))
         )
         go(remote(part.at[:, cols], other.at[:, cols], ws.at[c], wr.at[c], me, 1 - h))
+    m_onward(0)
     m_plane(1)
-    m_plane(3)
     for c in range(wide // COLS):
         cols = pl.ds(c * COLS, COLS)
         arrived(other.at[:, cols], ws.at[c], wr.at[c], me, 1 - h)
@@ -574,27 +576,28 @@
 
     one(h)
     offer(NEAR)
-    offer(COT, cot.at[h])
     one(1 - h)
-    kept[3].wait()
     m_onward(1)
-    m_onward(3)
+    m_plane(2)
     both(hop, NEAR, 1)
     both(across, NEAR, 1)
+    both(hop, NEAR, 2)
+    both(across, NEAR, 2)
+    offer(COT, cot.at[h])
+    kept[3].wait()
+    m_onward(2)
+    m_plane(3)
+    both(hop, NEAR, 3)
+    both(across, NEAR, 3)
     both(hop, COT, 1)
     both(across, COT, 1)
-    m_plane(2)
-    both(hop, NEAR, 2)
-    both(across, NEAR, 2)
+    m_onward(3)
     both(hop, COT, 2)
     both(across, COT, 2)
-    m_onward(2)
-    both(hop, NEAR, 3)
-    both(across, NEAR, 3)
     both(hop, COT, 3)
     both(across, COT, 3)
-    for d in ORDER:
-        corner_set(2, d, (z + ZED - d) % ZED, None)
+    for d in range(4):
+        corner_set(2, d, partner[d], None)
     for kind in (NEAR, COT):
         for step in (1, 2, 3):
             both(across_done, kind, step)
@@ -697,10 +700,16 @@
         self.half = r1x.shape[-1]
         self.low, self.high = pl.ds(0, self.half), pl.ds(self.half, self.half)
 
+    def first_copies(self, d):
+        zz, x, y, g = (self.z + d) % ZED, self.x, self.y, self.g
+        return (
+            remote(g.at[zz, :, 1 - x, :, self.low], self.r1x.at[d], self.s.at[d, 0], self.q.at[d, 0], self.at_x, self.h),
+            remote(g.at[zz, 1 - y, :, :, self.high], self.r1y.at[d], self.s.at[d, 1], self.q.at[d, 1], self.at_y, self.h),
+        )
+
     def first(self, d):
-        zz, x, y, g = (self.z + d) % ZED, self.x, self.y, self.g
-        self.go(remote(g.at[zz, :, 1 - x, :, self.low], self.r1x.at[d], self.s.at[d, 0], self.q.at[d, 0], self.at_x, self.h))
-        self.go(remote(g.at[zz, 1 - y, :, :, self.high], self.r1y.at[d], self.s.at[d, 1], self.q.at[d, 1], self.at_y, self.h))
+        for copy in self.first_copies(d):
+            self.go(copy)
 
     def second(self, d):
         x, y, me, h, r1x, r1y = self.x, self.y, self.me, self.h, self.r1x, self.r1y
@@ -811,49 +820,79 @@
 
 
 def back_kernel(
-    gm, t, wo, mid, cot, got, ratio, den,
+    near, gg, dg, du, hid, t, wo, mid, cot, got, ratio, den,
     zm, d_mid, d_att, home,
-    r1x, r1y, r2x, r2y, f1, f2, fin, e2, other, summed, landed, w2, pack, d_o, d_qk, d_v,
-    q_t, k_t, va, da, dn_t, pack2,
+    g, r1x, r1y, r2x, r2y, e2, other, summed, landed, w2, pack, d_o, d_qk, d_v,
+    q_t, k_t, va, da, dn_t, pack2, nbuf, gbuf, turned,
     ls, fs, gs, gq, cs, cq, e1s, e1r, e2s, e2r,
 ):
     x, y, z, h = where_am_i()
     me = index_of(z, y, x)
     count = mid.shape[1]
     heads = 16 // mid.shape[0]
+    room = dg.shape[1]
     late = []
 
     def go(copy):
         copy.start()
         late.append(copy)
 
+    def fetch(i):
+        cols = pl.ds(pl.multiple_of(((z + ZED - 1 - i) % ZED) * 512, 512), 512)
+        return (
+            pltpu.make_async_copy(near.at[:, cols], nbuf.at[i % 2], fs.at[i % 2, 0]),
+            pltpu.make_async_copy(gg.at[:, cols], gbuf.at[i % 2], fs.at[i % 2, 1]),
+        )
+
+    for copy in fetch(0):
+        copy.start()
     combine = Combine(t, e2, other, summed, landed, ls, cs, cq, go)
     scatter = Scatter(
-        gm, lambda d: f1.at[d], lambda d: f2.at[d], lambda d: fin.at[d], zm,
-        r1x, r1y, r2x, r2y, gs, gq, go,
+        g,
+        lambda d: g.at[(z + d) % ZED, 1 - y, x, :, pl.ds(0, g.shape[-1] // 2)],
+        lambda d: g.at[(z + d) % ZED, y, 1 - x, :, pl.ds(g.shape[-1] // 2, g.shape[-1] // 2)],
+        lambda d: g.at[(z + d) % ZED, y, x],
+        zm, r1x, r1y, r2x, r2y, gs, gq, go,
     )
     combine.begin()
-    for d in FAR:
-        scatter.first(d)
-    keep = {}
-    for d in FAR:
-        zz = (z + d) % ZED
-        keep[d] = [
-            pltpu.make_async_copy(gm.at[zz, 1 - y, x, :, scatter.low], f1.at[d], fs.at[d, 0]),
-            pltpu.make_async_copy(gm.at[zz, y, 1 - x, :, scatter.high], f2.at[d], fs.at[d, 1]),
-            pltpu.make_async_copy(gm.at[zz, y, x], fin.at[d], fs.at[d, 2]),
-        ]
-        for copy in keep[d]:
-            copy.start()
     weight = pltpu.make_async_copy(wo, w2, ls.at[4])
     weight.start()
     combine.spread()
-    for d in FAR:
-        for copy in keep[d]:
+
+    def block(i, carry):
+        d = ZED - 1 - i
+        zz = (z + d) % ZED
+
+        @pl.when(i < ZED - 1)
+        def _():
+            for copy in fetch(i + 1):
+                copy.start()
+
+        for copy in fetch(i):
             copy.wait()
+        for buf, terms in ((nbuf, (dg, du)), (gbuf, (hid,))):
+            turned[...] = jnp.transpose(buf[i % 2])
+            for term in terms:
+                base = {id(dg): 0, id(du): room, id(hid): 2 * room}[id(term)]
+
+                def piece(c, carry):
+                    src = pl.ds(pl.multiple_of(c * COLS, COLS), COLS)
+                    dst = pl.ds(pl.multiple_of(base + c * COLS, COLS), COLS)
+                    res = mix(turned[...], term[:, src], ((1,), (0,))).astype(bf16)
+                    for n in range(4):
+                        g[zz, n // 2, n % 2, :, dst] = res[n * 128 : (n + 1) * 128, :]
+                    return carry
+
+                lax.fori_loop(0, room // COLS, piece, 0)
+        for copy in scatter.first_copies(d):
+            copy.start()
+        return carry
+
+    lax.fori_loop(0, ZED, block, 0)
+    for d in range(ZED):
+        late.extend(scatter.first_copies(d))
     weight.wait()
-    scatter.second(2)
-    scatter.second(1)
+    scatter.second(3)
     combine.total()
     combine.done()
 
@@ -889,12 +928,12 @@
     for d in range(1, 16):
         there = (me + d) % 16
         go(remote(pack.at[there], window(me), e1s.at[d], e1r.at[d], there, h))
-    scatter.second(3)
+    scatter.second(2)
     own.wait()
     for d in range(1, 16):
         arrived(window((me + 16 - d) % 16), e1s.at[d], e1r.at[d], me, h)
-    scatter.second(0)
-    scatter.third(2)
+    scatter.third(3)
+    scatter.second(1)
     attend_back_body(got, ratio, den, d_o, d_qk, d_v, q_t, k_t, va, da, dn_t)
     for b in range(16):
         pack2[b, 0 : 2 * F, :] = d_qk[:, b * count : (b + 1) * count].astype(bf16)
@@ -904,8 +943,9 @@
     for d in range(1, 16):
         there = (me + d) % 16
         go(remote(pack2.at[there], home.at[me], e2s.at[d], e2r.at[d], there, h))
+    scatter.third(2)
+    scatter.second(0)
     scatter.third(1)
-    scatter.third(3)
     scatter.third(0)
     own.wait()
     for d in range(1, 16):
@@ -924,11 +964,11 @@
     ]
 
 
-def back(gm, t, wo, mid, cot, got, ratio, den):
+def back(near, gg, dg, du, hid, t, wo, mid, cot, got, ratio, den):
     mbs, count, wide = cot.shape
     depth = 16 * count
     shape = jax.ShapeDtypeStruct
-    cols = gm.shape[-1]
+    cols = 3 * dg.shape[1]
     line = pltpu.VMEM((ZED, count, wide), bf16)
     return pl.pallas_call(
         back_kernel,
@@ -938,12 +978,9 @@
             shape((mbs * count, wide), bf16),
             shape((16, 2 * F + DV, count), bf16),
         ),
-        in_specs=[ANY] * 3 + [VMEM] * 5,
+        in_specs=[ANY] * 2 + [VMEM] * 3 + [ANY] * 2 + [VMEM] * 5,
         out_specs=(VMEM,) * 4,
-        scratch_shapes=scatter_room(cols) + [
-            pltpu.VMEM((4, 128, cols // 2), bf16),
-            pltpu.VMEM((4, 128, cols // 2), bf16),
-            pltpu.VMEM((4, 128, cols), bf16),
+        scratch_shapes=[pltpu.VMEM((ZED, 2, 2, 128, cols), bf16)] + scatter_room(cols) + [
             pltpu.VMEM(cot.shape, bf16), line, line, line,
             pltpu.VMEM(wo.shape, bf16),
             pltpu.VMEM((16, count, DV), bf16),
@@ -956,12 +993,15 @@
             pltpu.VMEM((depth, 2 * DV), bf16),
             pltpu.VMEM((DV, depth), bf16),
             pltpu.VMEM((16, 2 * F + DV, count), bf16),
-            DMA((6,)), DMA((4, 3)), DMA((4, 5)), DMA((4, 5)), DMA((4, 2)), DMA((4, 2)),
+            pltpu.VMEM((2, near.shape[0], 512), bf16),
+            pltpu.VMEM((2, near.shape[0], 512), bf16),
+            pltpu.VMEM((512, near.shape[0]), bf16),
+            DMA((6,)), DMA((2, 2)), DMA((4, 5)), DMA((4, 5)), DMA((4, 2)), DMA((4, 2)),
             DMA((16,)), DMA((16,)), DMA((16,)), DMA((16,)),
         ],
         compiler_params=params(),
         name="back",
-    )(gm.reshape(ZED, 2, 2, 128, cols), t, wo, mid, cot, got, ratio, den)
+    )(near, gg, dg, du, hid, t, wo, mid, cot, got, ratio, den)
 
 
 def end_kernel(
@@ -1081,6 +1121,78 @@
     )(t, home, xh, d_att, heads_out, wa1, d_mid, xin, mid)
 
 
+def finish_kernel(
+    zm, za, wq, wk, wv, wg, wu, g1, g2, o_q, o_k, o_v, o_out, o_g, o_u, o_d, gains
+):
+    units = wg.shape[1] // ZED
+    room = zm.shape[2] // 3
+    nq, nv = wq.shape[1], wv.shape[1]
+    lanes = g1.shape[1]
+
+    def fold(prod):
+        acc = prod[:, 0:lanes]
+        for c in range(1, prod.shape[1] // lanes):
+            acc = acc + prod[:, c * lanes : (c + 1) * lanes]
+        return acc
+
+    def total(cols):
+        acc = za[0, :, cols].astype(f32)
+        for n in range(1, ZED):
+            acc = acc + za[n, :, cols].astype(f32)
+        return acc
+
+    first = jnp.zeros((zm.shape[1], lanes), f32)
+    at = 0
+    for w, out in ((wq, o_q), (wk, o_k), (wv, o_v)):
+        for c in range(w.shape[1] // lanes):
+            cols = slice(c * lanes, (c + 1) * lanes)
+            value = total(slice(at + c * lanes, at + (c + 1) * lanes))
+            out[:, cols] = value * g1[...]
+            first = first + value * w[:, cols].astype(f32)
+        at += w.shape[1]
+    for c in range(nv // lanes):
+        o_out[c * lanes : (c + 1) * lanes, :] = jnp.transpose(
+            total(slice(at + c * lanes, at + (c + 1) * lanes))
+        )
+    second = jnp.zeros((zm.shape[1], lanes), f32)
+    whole = units // lanes * lanes
+    for n in range(ZED):
+        for base, w, out in ((0, wg, o_g), (room, wu, o_u)):
+            for c in range(0, units, lanes):
+                size = min(lanes, units - c)
+                cols = slice(n * units + c, n * units + c + size)
+                value = zm[n, :, base + c : base + c + size].astype(f32)
+                out[:, cols] = value * g2[:, 0:size]
+                prod = value * w[:, cols].astype(f32)
+                if size == lanes:
+                    second = second + prod
+                else:
+                    second = second + jnp.concatenate(
+                        [prod, jnp.zeros((prod.shape[0], lanes - size), f32)], axis=1
+                    )
+        for c in range(0, units, lanes):
+            size = min(lanes, units - c)
+            value = jnp.transpose(zm[n, :, 2 * room + c : 2 * room + c + lanes].astype(f32))
+            o_d[n * units + c : n * units + c + size, :] = value[0:size, :]
+    gains[0:1, :] = jnp.sum(jnp.transpose(first), axis=0, keepdims=True)
+    gains[1:2, :] = jnp.sum(jnp.transpose(second), axis=0, keepdims=True)
+
+
+def finish(zm, za, wq, wk, wv, wg, wu, g1, g2, w_out, w_down):
+    shape = lambda w: jax.ShapeDtypeStruct(w.shape, f32)
+    return pl.pallas_call(
+        finish_kernel,
+        out_shape=(
+            shape(wq), shape(wk), shape(wv), shape(w_out), shape(wg), shape(wu), shape(w_down),
+            jax.ShapeDtypeStruct((2, 128), f32),
+        ),
+        in_specs=[VMEM] * 9,
+        out_specs=(VMEM,) * 8,
+        compiler_params=pltpu.CompilerParams(vmem_limit_bytes=VMEM_LIMIT),
+        name="finish",
+    )(zm, za, wq, wk, wv, wg, wu, g1, g2)
+
+
 def fast(
     inputs, norm_gain1, w_query, w_key, w_value, w_out, norm_gain2, w_gate, w_up, w_down, cotangent
 ):
@@ -1122,45 +1234,20 @@
     d_up = (d_hidden * silu).astype(bf16)
     branch = mix(hidden, w_d, ((1,), (1,))).astype(bf16)
     d_n2 = (mix(d_gate, w_g, ((1,), (1,))) + mix(d_up, w_u, ((1,), (1,)))).astype(bf16)
-    first = ((0,), (0,))
-    gm = jnp.concatenate(
-        [mix(n2, d_gate, first), mix(n2, d_up, first), mix(up_g, hidden, first)], axis=1
-    ).astype(bf16)
     lines = (ZED, mbs, count, wide)
     zm, d_mid, d_att, home = back(
-        gm, d_n2.reshape(lines), w_o, middle, cotangent, got, ratio, den
+        n2, up_g, d_gate, d_up, hidden, d_n2.reshape(lines), w_o, middle, cotangent, got, ratio, den
     )
     za, input_grad, outputs = end(
         branch.reshape(lines), home, xh1, d_att, heads_out, wa1, d_mid, inputs, middle
     )
-    za = jnp.sum(za.astype(f32), axis=0)
-    zm = zm.astype(f32)
-
-    def joined(piece):
-        return jnp.transpose(piece[:, :, :units], (1, 0, 2)).reshape(rows, ZED * units)
-
-    g_gate, g_up, g_down = joined(zm[:, :, :room]), joined(zm[:, :, room : 2 * room]), joined(zm[:, :, 2 * room :])
-    s_q, s_k, s_v = za[:, : qk // 2], za[:, qk // 2 : qk], za[:, qk : qk + vv]
-    g_gain1 = (
-        jnp.sum(w_query.astype(f32) * s_q, axis=1)
-        + jnp.sum(w_key.astype(f32) * s_k, axis=1)
-        + jnp.sum(w_value.astype(f32) * s_v, axis=1)
-    )
-    g_gain2 = jnp.sum(w_gate.astype(f32) * g_gate, axis=1) + jnp.sum(w_up.astype(f32) * g_up, axis=1)
-    gains = lax.psum(jnp.stack([g_gain1, g_gain2]), "head")
-    return (
-        outputs,
-        input_grad,
-        gains[0],
-        s_q * gain1,
-        s_k * gain1,
-        s_v * gain1,
-        za[:, qk + vv :].T,
-        gains[1],
-        g_gate * gain2,
-        g_up * gain2,
-        g_down.T,
-    )
+    full = (rows, 128)
+    o_q, o_k, o_v, o_out, o_g, o_u, o_d, gains = finish(
+        zm, za, w_query, w_key, w_value, w_gate, w_up,
+        jnp.broadcast_to(gain1, full), jnp.broadcast_to(gain2, full), w_out, w_down,
+    )
+    gains = lax.psum(gains, "head")
+    return (outputs, input_grad, gains[0], o_q, o_k, o_v, o_out, gains[1], o_g, o_u, o_d)
 
 
 def solution(mesh):

time: 612 us -> 555 us (0.907)
  local copies, waits for them, and re-layouts: 40.2 us -> 9.44 us
  matrix products: 53.7 us -> 30.9 us
  other arithmetic: 22.5 us -> 6.74 us
  Pallas kernels: 488 us -> 496 us
    dot_general x9 -> x6, matrix products: 53.7 us -> 30.9 us  [mix(): return lax.dot_general(a, b, (over, ((), ())), preferred_element_type=f32)]
    pallas_call x1, Pallas kernels: 137 us -> 153 us  [back(): pl.pallas_call(back_kernel, out_shape=(shape((ZED, 128, cols), bf16), sha...]
    dot_general x2 -> x0, local copies, waits for them, and re-layouts: 13 us -> none  [mix(): return lax.dot_general(a, b, (over, ((), ())), preferred_element_type=f32)]
    pallas_call x1, Pallas kernels: 133 us -> 120 us  [end(): pl.pallas_call(end_kernel, out_shape=(shape((ZED, 128, cols), bf16), shap...]
    transpose x4 -> x0, local copies, waits for them, and re-layouts: 8.23 us -> none  [joined(): jnp.transpose(piece[:, :, :units], (1, 0, 2)).reshape(rows, ZED * units)]
    unnamed x46 -> x31, local copies, waits for them, and re-layouts: 13.6 us -> 5.46 us
    pallas_call x0 -> x1, Pallas kernels: none -> 6.78 us  [finish(): pl.pallas_call(finish_kernel, out_shape=(shape(wq), shape(wk), shape(wv),...]
where the time goes in v5:
time: 555 us; the launch traced here: 547 us
  Pallas kernels  496 us (89%)
  matrix products  30.9 us (6%)
  local copies, waits for them, and re-layouts  9.44 us (2%)
  other arithmetic  6.74 us (1%)
    pallas_call x1, Pallas kernels, front(): pl.pallas_call(front_kernel, out_shape=(shape((wide, wide1), bf16), shape...  216 us
    pallas_call x1, Pallas kernels, back(): pl.pallas_call(back_kernel, out_shape=(shape((ZED, 128, cols), bf16), sha...  153 us
    pallas_call x1, Pallas kernels, end(): pl.pallas_call(end_kernel, out_shape=(shape((ZED, 128, cols), bf16), shap...  120 us
    dot_general x6, matrix products, mix(): return lax.dot_general(a, b, (over, ((), ())), preferred_element_type=f32)  30.9 us

profile of v5, /device:TPU:0, one launch (start us, length us, event | category | flops | bytes accessed | tf_op | source)
XLA Modules:
  0.0 546.8 jit_solution(14239423851049609164)
XLA Ops:
  0.6 0.0 copy-start.3
  0.7 0.7 convert_element_type.62
  1.4 0.9 multiply_convert_fusion.7
  2.3 1.1 multiply_convert_fusion.5
  3.3 0.8 pad_maximum_fusion.a1
  4.1 1.5 copy.24
  5.5 0.3 copy.26
  5.9 0.3 multiply_convert_fusion.4
  6.2 0.3 copy.25
  6.5 0.3 copy.27
  6.8 1.5 copy.28
  8.3 1.6 fusion.16.m
  9.8 0.3 multiply_reduce_fusion
  10.1 1.2 fusion.17.xh
  11.3 0.8 copy.23
  12.2 216.3 %front.1 = (bf16[2048,1280]{1,0:T(8,128)(2,1)}, bf16[2048,1024]{1,0:T(8,128)(2,1)}, bf16[2048,2304]{1,0:T(8,128)(2,1)}, bf16[4,2,128,2048]{3,2,1,0:T(8,128)(2,1)...) custom-call(bf16[128,1280]{1,0:T(8,128)(2,1)} %pad_maximum_fusion.a1, ...), custom_call_target="tpu_custom_call" | custom-call | tf_op jit(solution)/shard_map/front/pallas_call | solution.py:615
  228.5 6.3 %fusion.9 = f32[1024,768]{1,0:T(8,128)S(1)} fusion(bf16[1024,2048]{1,0:T(8,128)(2,1)} %bitcast.32, bf16[2048,2304]{1,0:T(8,128)(2,1)} %get-tuple-element.37), kind=kOutput, calls=%fused_computation.19 | convolution fusion | flops 3221225472 | bytes 10485760 | tf_op jit(solution)/shard_map/dot_general | solution.py:285
  234.8 0.8 copy-done.12
  235.6 3.4 fusion.13
  239.0 5.7 %multiply_convert_fusion = (bf16[1024,768]{1,0:T(8,128)(2,1)S(1)}, bf16[1024,768]{1,0:T(8,128)(2,1)S(1)}, bf16[1024,768]{1,0:T(8,128)(2,1)}) fusion(f32[1024,768]{1,0:T(8,128)S(1)} %fusion.13, f32[1024,768]{1,0:T(8,128)S(1)} %fusion.9, bf16[1024,2048]{1,0:T(8,128)(2,1)S(1)} %bitcast.31, bf16[2048,2304]{1,0:T(8,128)(2,1)S(1)} %copy-done.12), kind=kOutput, calls=%fused_computation.10 | convolution fusion | flops 3233021952 | bytes 18350080 | tf_op jit(solution)/shard_map/dot_general | solution.py:285
  244.7 3.5 fusion.11
  248.2 5.1 add_convert_fusion
  253.3 152.9 %back.1 = (bf16[4,128,2304]{2,1,0:T(8,128)(2,1)}, f32[2,128,2048]{2,1,0:T(8,128)}, bf16[256,2048]{1,0:T(8,128)(2,1)}, bf16[16,160,128]{2,1,0:T(8,128)(2,1)}) custom-call(bf16[1024,2048]{1,0:T(8,128)(2,1)} %bitcast.33, bf16[1024,2048]{1,0:T(8,128)(2,1)} %bitcast.30, bf16[1024,768]{1,0:T(8,128)(2,1)} %copy-done.6, bf16[1024,768]{1,0:T(8,128)(2,1)} %copy-done.5, ...), custom_call_target="tpu_custom_call" | custom-call | tf_op jit(solution)/shard_map/back/pallas_call | solution.py:973
  406.3 6.9 %convolution_convert_fusion = bf16[1024,2048]{1,0:T(8,128)(2,1)} fusion(bf16[1024,768]{1,0:T(8,128)(2,1)S(1)} %copy-done.4, bf16[2048,2304]{1,0:T(8,128)(2,1)} %get-tuple-element.37), kind=kOutput, calls=%fused_computation.9 | convolution fusion | flops 3223322624 | bytes 8912896 | tf_op jit(solution)/shard_map/dot_general | solution.py:285
  413.2 120.1 %end.1 = (bf16[4,128,2304]{2,1,0:T(8,128)(2,1)}, bf16[2,128,2048]{2,1,0:T(8,128)(2,1)}, bf16[2,128,2048]{2,1,0:T(8,128)(2,1)}) custom-call(bf16[4,2,128,2048]{3,2,1,0:T(8,128)(2,1)} %bitcast.29, bf16[16,160,128]{2,1,0:T(8,128)(2,1)} %get-tuple-element.44.home, bf16[256,2048]{1,0:T(8,128)(2,1)} %fusion.17.xh, bf16[256,2048]{1,0:T(8,128)(2,1)} %get-tuple-element.45.d_att, ...), custom_call_target="tpu_custom_call" | custom-call | tf_op jit(solution)/shard_map/end/pallas_call | solution.py:1104
  533.2 0.7 broadcast_in_dim.2.g2
  534.0 0.7 mul.69.g1
  534.7 6.8 %finish.1 = (f32[128,128]{1,0:T(8,128)}, f32[128,128]{1,0:T(8,128)}, f32[128,1024]{1,0:T(8,128)}, f32[1024,128]{1,0:T(8,128)}, f32[128,2816]{1,0:T(8,128)}, /*in...) custom-call(bf16[4,128,2304]{2,1,0:T(8,128)(2,1)} %get-tuple-element.51.zm, ...), custom_call_target="tpu_custom_call" | custom-call | tf_op jit(solution)/shard_map/finish/pallas_call | solution.py:1183
  541.5 2.4 psum.7
  543.9 0.5 slice_bitcast_fusion
  544.4 1.0 copy.31
  545.4 1.0 copy.32
  (26 shorter events, 0.1 us)
Async XLA Ops:
  0.6 4.9 copy-start.3
  0.7 5.2 copy-start.10
  6.8 3.0 copy-start
  9.8 1.5 copy-start.9
  228.5 6.3 %copy-start.2 = (bf16[4,2,128,2048]{3,2,1,0:T(8,128)(2,1)S(1)}, bf16[4,2,128,2048]{3,2,1,0:T(8,128)(2,1)}, u32[]{:S(2)}) copy-start(bf16[4,2,128,2048]{3,2,1,0:T(8,128)(2,1)} %get-tuple-element.36) | copy-start | bytes 12582916
  228.5 7.1 %copy-start.12 = (bf16[2048,2304]{1,0:T(8,128)(2,1)S(1)}, bf16[2048,2304]{1,0:T(8,128)(2,1)}, u32[]{:S(2)}) copy-start(bf16[2048,2304]{1,0:T(8,128)(2,1)} %get-tuple-element.37) | copy-start | bytes 28311556
  235.6 3.4 copy-start.1
  244.7 3.5 copy-start.6
  244.7 3.5 copy-start.5
  253.3 152.9 %copy-start.4 = (bf16[1024,768]{1,0:T(8,128)(2,1)S(1)}, bf16[1024,768]{1,0:T(8,128)(2,1)}, u32[]{:S(2)}) copy-start(bf16[1024,768]{1,0:T(8,128)(2,1)} %get-tuple-element.63.hid) | copy-start | bytes 4718596
  413.2 120.8 %copy-start.11 = (bf16[128]{0:T(256)(128)(2,1)S(1)}, bf16[128]{0:T(256)(128)(2,1)}, u32[]{:S(2)}) copy-start(bf16[128]{0:T(256)(128)(2,1)} %param.12) | copy-start | bytes 772
  534.7 9.8 %copy-start.8 = (bf16[2,128,2048]{2,1,0:T(8,128)(2,1)S(1)}, bf16[2,128,2048]{2,1,0:T(8,128)(2,1)}, u32[]{:S(2)}) copy-start(bf16[2,128,2048]{2,1,0:T(8,128)(2,1)} %get-tuple-element.81) | copy-start | bytes 3145732
  534.7 10.7 %copy-start.7 = (bf16[2,128,2048]{2,1,0:T(8,128)(2,1)S(1)}, bf16[2,128,2048]{2,1,0:T(8,128)(2,1)}, u32[]{:S(2)}) copy-start(bf16[2,128,2048]{2,1,0:T(8,128)(2,1)} %get-tuple-element.82) | copy-start | bytes 3145732

commit v6 on v5

--- a/solution.py
+++ b/solution.py
@@ -318,10 +318,15 @@
     den[qs, :] = acc[:, DV:]
 
 
+def column(gain):
+    count = gain.shape[1]
+    return jnp.transpose(jnp.broadcast_to(gain[...].astype(f32), (count, count)))
+
+
 def front_kernel(
-    a1, a2, m, cot, xh, xin,
-    wa1, wa2, wm, gg, got, ratio, den, heads_out, middle, near,
-    w1, w2, pack, q_t, k_t, va, ob, part, other,
+    wq, wk, wv, w_out, wg, wu, wd, g1, g2, cot, xin,
+    wa1, wa2, wm, gg, got, ratio, den, heads_out, middle, near, xh,
+    a1, a2, m, w1, w2, pack, q_t, k_t, va, ob, part, other,
     ls, zs, zr, us, ur, ps, pr, e1s, e1r, e2s, e2r, ws, wr, ds, dr,
 ):
     x, y, z, h = where_am_i()
@@ -351,8 +356,15 @@
         pltpu.make_async_copy(m.at[z], wm.at[mine], ls.at[2]),
         pltpu.make_async_copy(cot, gg.at[z], ls.at[6]),
     ]
-    for copy in kept:
-        copy.start()
+    lanes = g1.shape[1]
+    scale = column(g1)
+    at = 0
+    for w in (wq, wk, wv):
+        for c in range(0, w.shape[1], lanes):
+            a1[:, at + c : at + c + lanes] = (w[:, c : c + lanes].astype(f32) * scale).astype(bf16)
+        at += w.shape[1]
+    kept[0].start()
+    kept[3].start()
     dest = (w1, w2, wm)
     UP, DOWN = 0, 1
     COT, NEAR = 2, 3
@@ -405,9 +417,13 @@
 
     partner = (z, z + 1 - 2 * (z % 2), ZED - 1 - z, (z + 2) % ZED)
 
-    def line(d):
+    inner = (z > 0) & (z < ZED - 1)
+    outer = (z == 0) | (z == ZED - 1)
+
+    def line(d, true=None):
         zz = partner[d]
-        go(remote(m.at[zz], wm.at[mine], zs.at[d], zr.at[d], index_of(zz, y, x), h))
+        copy = remote(m.at[zz], wm.at[mine], zs.at[d], zr.at[d], index_of(zz, y, x), h)
+        go(copy, true)
 
     def slot_of(way, step):
         return step if way == UP else 3 + step if step else 0
@@ -470,9 +486,30 @@
 
     offer(0, a1)
     plane(0, UP, 0)
+    for c in range(0, w_out.shape[0], lanes):
+        a2[:, c : c + lanes] = jnp.transpose(w_out[c : c + lanes, :].astype(f32)).astype(bf16)
+    kept[1].start()
     for way in (UP, DOWN):
         hop(0, way, 1)
         plane(0, way, 1)
+    units = wg.shape[1] // ZED
+    room = m.shape[2] // 3
+    scale = column(g2)
+    for n in range(ZED):
+        for part_at, w in ((0, wg), (room, wu)):
+            for c in range(0, units, lanes):
+                size = min(lanes, units - c)
+                m[n, :, part_at + c : part_at + c + size] = (
+                    w[:, n * units + c : n * units + c + size].astype(f32) * scale[:, 0:size]
+                ).astype(bf16)
+        for c in range(0, units, lanes):
+            size = min(lanes, units - c)
+            m[n, :, 2 * room + c : 2 * room + c + size] = jnp.transpose(
+                wd[n * units + c : n * units + c + size, :].astype(f32)
+            ).astype(bf16)
+        for part_at in (0, room, 2 * room):
+            m[n, :, part_at + units : part_at + room] = jnp.zeros((lanes, room - units), bf16)
+    kept[2].start()
     onward(0, UP, 0)
     for way in (UP, DOWN):
         hop(0, way, 2)
@@ -485,12 +522,21 @@
     both(onward, 0, 2)
     both(hop, 1, 1)
     plane(1, UP, 0)
+    for mb in range(xin.shape[0]):
+
+        def normed(turn, carry):
+            row = pl.ds(pl.multiple_of(turn * 16, 16), 16)
+            v = xin[mb, row, :].astype(f32)
+            r = lax.rsqrt(jnp.mean(v * v, axis=-1, keepdims=True) + epsilon)
+            xh[pl.ds(pl.multiple_of(mb * count + turn * 16, 16), 16), :] = (v * r).astype(bf16)
+            return carry
+
+        lax.fori_loop(0, count // 16, normed, 0)
     both(onward, 0, 3)
     both(hop, 1, 2)
-    both(plane, 1, 1)
     both(hop, 1, 3)
     line(1)
-    line(2)
+    line(2, inner)
     corner(0)
     out1 = pltpu.make_async_copy(w1, wa1, ls.at[3])
     out1.start()
@@ -514,6 +560,9 @@
     for d in range(1, 16):
         there = (me + d) % 16
         go(remote(pack.at[there], got.at[me], e1s.at[d], e1r.at[d], there, h))
+    line(2, outer)
+    line(3, inner)
+    both(plane, 1, 1)
     onward(1, UP, 0)
     both(plane, 1, 2)
     both(onward, 1, 1)
@@ -522,7 +571,6 @@
     keep.wait()
     for d in range(1, 16):
         arrived(got.at[(me + 16 - d) % 16], e1s.at[d], e1r.at[d], me, h)
-    line(3)
     both(onward, 1, 3)
     spread(got, q_t, k_t, va)
     causal = lower(CHUNK)
@@ -542,7 +590,10 @@
     for d in range(1, 16):
         there = (me + d) % 16
         go(remote(ob.at[there], window(me), e2s.at[d], e2r.at[d], there, h))
+    line(3, outer)
+    offer(COT, cot.at[h])
     m_plane(0)
+    m_plane(1)
     corner(1)
     out2 = pltpu.make_async_copy(w2, wa2, ls.at[5])
     out2.start()
@@ -557,7 +608,8 @@
         )
         go(remote(part.at[:, cols], other.at[:, cols], ws.at[c], wr.at[c], me, 1 - h))
     m_onward(0)
-    m_plane(1)
+    both(hop, COT, 1)
+    m_plane(2)
     for c in range(wide // COLS):
         cols = pl.ds(c * COLS, COLS)
         arrived(other.at[:, cols], ws.at[c], wr.at[c], me, 1 - h)
@@ -578,24 +630,21 @@
     offer(NEAR)
     one(1 - h)
     m_onward(1)
-    m_plane(2)
+    both(hop, COT, 2)
+    m_plane(3)
+    kept[3].wait()
+    both(across, COT, 1)
+    both(across, COT, 2)
     both(hop, NEAR, 1)
     both(across, NEAR, 1)
+    m_onward(2)
+    both(hop, COT, 3)
+    both(across, COT, 3)
     both(hop, NEAR, 2)
     both(across, NEAR, 2)
-    offer(COT, cot.at[h])
-    kept[3].wait()
-    m_onward(2)
-    m_plane(3)
+    m_onward(3)
     both(hop, NEAR, 3)
     both(across, NEAR, 3)
-    both(hop, COT, 1)
-    both(across, COT, 1)
-    m_onward(3)
-    both(hop, COT, 2)
-    both(across, COT, 2)
-    both(hop, COT, 3)
-    both(across, COT, 3)
     for d in range(4):
         corner_set(2, d, partner[d], None)
     for kind in (NEAR, COT):
@@ -607,17 +656,18 @@
         when(true, copy.wait_send)
 
 
-def front(a1, a2, m, cot, xh, xin):
+def front(wq, wk, wv, w_out, wg, wu, wd, g1, g2, cot, xin):
     mbs, count, wide = xin.shape
     depth = 16 * count
-    wide1, wide2 = a1.shape[1], a2.shape[1]
+    wide1, wide2 = wq.shape[1] + wk.shape[1] + wv.shape[1], w_out.shape[0]
+    wide3 = 3 * (-(-wg.shape[1] // ZED // 256) * 256)
     shape = jax.ShapeDtypeStruct
     return pl.pallas_call(
         front_kernel,
         out_shape=(
             shape((wide, wide1), bf16),
             shape((wide, wide2), bf16),
-            shape((wide, m.shape[2]), bf16),
+            shape((wide, wide3), bf16),
             shape((ZED,) + cot.shape, bf16),
             shape((16, 2 * F + DV, count), bf16),
             shape((depth, DV), f32),
@@ -625,10 +675,14 @@
             shape((mbs * count, wide2), bf16),
             shape(xin.shape, f32),
             shape((ZED,) + xin.shape, bf16),
+            shape((mbs * count, wide), bf16),
         ),
-        in_specs=[ANY] * 4 + [VMEM] * 2,
-        out_specs=(ANY,) * 4 + (VMEM,) * 6,
+        in_specs=[VMEM] * 9 + [ANY] + [VMEM],
+        out_specs=(ANY,) * 4 + (VMEM,) * 7,
         scratch_shapes=[
+            pltpu.VMEM((wq.shape[0], wide1), bf16),
+            pltpu.VMEM((wq.shape[0], wide2), bf16),
+            pltpu.VMEM((ZED, wq.shape[0], wide3), bf16),
             pltpu.VMEM((wide, wide1), bf16),
             pltpu.VMEM((wide, wide2), bf16),
             pltpu.VMEM((16, 2 * F + DV, count), bf16),
@@ -644,7 +698,7 @@
         ],
         compiler_params=params(),
         name="front",
-    )(a1, a2, m, cot, xh, xin)
+    )(wq, wk, wv, w_out, wg, wu, wd, g1, g2, cot, xin)
 
 
 def attend_back_body(got, ratio, den, d_o, d_qk, d_v, q_t, k_t, va, da, dn_t):
@@ -711,7 +765,13 @@
         for copy in self.first_copies(d):
             self.go(copy)
 
-    def second(self, d):
+    def second_copies(self, d):
+        return (
+            remote(self.low_acc(d), self.r2y.at[d], self.s.at[d, 2], self.q.at[d, 2], self.at_y, self.h),
+            remote(self.high_acc(d), self.r2x.at[d], self.s.at[d, 3], self.q.at[d, 3], self.at_x, self.h),
+        )
+
+    def second_sum(self, d):
         x, y, me, h, r1x, r1y = self.x, self.y, self.me, self.h, self.r1x, self.r1y
         arrived(r1x.at[d], self.s.at[d, 0], self.q.at[d, 0], me, h)
         arrived(r1y.at[d], self.s.at[d, 1], self.q.at[d, 1], me, h)
@@ -728,8 +788,11 @@
             return carry
 
         lax.fori_loop(0, 8, body, 0)
-        self.go(remote(low_acc, self.r2y.at[d], self.s.at[d, 2], self.q.at[d, 2], self.at_y, h))
-        self.go(remote(high_acc, self.r2x.at[d], self.s.at[d, 3], self.q.at[d, 3], self.at_x, h))
+
+    def second(self, d):
+        self.second_sum(d)
+        for copy in self.second_copies(d):
+            self.go(copy)
 
     def third(self, d):
         x, y, me, h, z = self.x, self.y, self.me, self.h, self.z
@@ -820,11 +883,11 @@
 
 
 def back_kernel(
-    near, gg, dg, du, hid, t, wo, mid, cot, got, ratio, den,
-    zm, d_mid, d_att, home,
+    near, gg, dg, du, hid, t, wo, wm, mid, cot, got, ratio, den,
+    zm, d_mid, d_att, home, tb,
     g, r1x, r1y, r2x, r2y, e2, other, summed, landed, w2, pack, d_o, d_qk, d_v,
-    q_t, k_t, va, da, dn_t, pack2, nbuf, gbuf, turned,
-    ls, fs, gs, gq, cs, cq, e1s, e1r, e2s, e2r,
+    q_t, k_t, va, da, dn_t, pack2, nbuf, gbuf, turned, stage,
+    ls, fs, bs, gs, gq, cs, cq, e1s, e1r, e2s, e2r,
 ):
     x, y, z, h = where_am_i()
     me = index_of(z, y, x)
@@ -884,15 +947,42 @@
                     return carry
 
                 lax.fori_loop(0, room // COLS, piece, 0)
-        for copy in scatter.first_copies(d):
+        @pl.when(i < ZED - 1)
+        def _():
+            for copy in scatter.first_copies(d):
+                copy.start()
+
+        @pl.when((i > 0) & (i < ZED - 1))
+        def _():
+            scatter.second_sum(d + 1)
+            for copy in scatter.second_copies(d + 1):
+                copy.start()
+
+        return carry
+
+    lax.fori_loop(0, ZED, block, 0)
+    for d in (1, 2, 3):
+        late.extend(scatter.first_copies(d))
+    for d in (2, 3):
+        late.extend(scatter.second_copies(d))
+    half = near.shape[1] // 2
+    shards = []
+    for r in range(2):
+        at = pl.ds(r * half, half)
+        shards.append(
+            (
+                pltpu.make_async_copy(wm.at[at, pl.ds(2 * room, 512)], nbuf.at[r], fs.at[r, 0]),
+                pltpu.make_async_copy(
+                    wm.at[at, pl.ds(2 * room + 512, room - 512)],
+                    gbuf.at[r, :, pl.ds(0, room - 512)],
+                    fs.at[r, 1],
+                ),
+            )
+        )
+        for copy in shards[r]:
             copy.start()
-        return carry
-
-    lax.fori_loop(0, ZED, block, 0)
-    for d in range(ZED):
-        late.extend(scatter.first_copies(d))
     weight.wait()
-    scatter.second(3)
+    scatter.third(3)
     combine.total()
     combine.done()
 
@@ -928,12 +1018,29 @@
     for d in range(1, 16):
         there = (me + d) % 16
         go(remote(pack.at[there], window(me), e1s.at[d], e1r.at[d], there, h))
-    scatter.second(2)
+    scatter.second(1)
+    scatter.first(0)
+    scatter.third(2)
+    stored = {}
+    for n in range(2 * half // COLS):
+        r, c = n // (half // COLS), n % (half // COLS)
+        if c == 0:
+            for copy in shards[r]:
+                copy.wait()
+        if n > 1:
+            stored[n - 2].wait()
+        at = slice(c * COLS, (c + 1) * COLS)
+        stage[n % 2, :, :] = (
+            mix(hid[:, 0:512], nbuf[r, at, :], ((1,), (1,)))
+            + mix(hid[:, 512:room], gbuf[r, at, 0 : room - 512], ((1,), (1,)))
+        ).astype(bf16)
+        stored[n] = pltpu.make_async_copy(
+            stage.at[n % 2], tb.at[:, pl.ds(n * COLS, COLS)], bs.at[n % 2]
+        )
+        stored[n].start()
     own.wait()
     for d in range(1, 16):
         arrived(window((me + 16 - d) % 16), e1s.at[d], e1r.at[d], me, h)
-    scatter.third(3)
-    scatter.second(1)
     attend_back_body(got, ratio, den, d_o, d_qk, d_v, q_t, k_t, va, da, dn_t)
     for b in range(16):
         pack2[b, 0 : 2 * F, :] = d_qk[:, b * count : (b + 1) * count].astype(bf16)
@@ -943,9 +1050,10 @@
     for d in range(1, 16):
         there = (me + d) % 16
         go(remote(pack2.at[there], home.at[me], e2s.at[d], e2r.at[d], there, h))
-    scatter.third(2)
+    stored[2 * half // COLS - 2].wait()
+    stored[2 * half // COLS - 1].wait()
+    scatter.third(1)
     scatter.second(0)
-    scatter.third(1)
     scatter.third(0)
     own.wait()
     for d in range(1, 16):
@@ -964,7 +1072,7 @@
     ]
 
 
-def back(near, gg, dg, du, hid, t, wo, mid, cot, got, ratio, den):
+def back(near, gg, dg, du, hid, t, wo, wm, mid, cot, got, ratio, den):
     mbs, count, wide = cot.shape
     depth = 16 * count
     shape = jax.ShapeDtypeStruct
@@ -977,9 +1085,10 @@
             shape(cot.shape, f32),
             shape((mbs * count, wide), bf16),
             shape((16, 2 * F + DV, count), bf16),
+            shape(near.shape, bf16),
         ),
-        in_specs=[ANY] * 2 + [VMEM] * 3 + [ANY] * 2 + [VMEM] * 5,
-        out_specs=(VMEM,) * 4,
+        in_specs=[ANY] * 2 + [VMEM] * 3 + [ANY] * 3 + [VMEM] * 5,
+        out_specs=(VMEM,) * 4 + (ANY,),
         scratch_shapes=[pltpu.VMEM((ZED, 2, 2, 128, cols), bf16)] + scatter_room(cols) + [
             pltpu.VMEM(cot.shape, bf16), line, line, line,
             pltpu.VMEM(wo.shape, bf16),
@@ -996,12 +1105,13 @@
             pltpu.VMEM((2, near.shape[0], 512), bf16),
             pltpu.VMEM((2, near.shape[0], 512), bf16),
             pltpu.VMEM((512, near.shape[0]), bf16),
-            DMA((6,)), DMA((2, 2)), DMA((4, 5)), DMA((4, 5)), DMA((4, 2)), DMA((4, 2)),
+            pltpu.VMEM((2, near.shape[0], COLS), bf16),
+            DMA((6,)), DMA((2, 2)), DMA((2,)), DMA((4, 5)), DMA((4, 5)), DMA((4, 2)), DMA((4, 2)),
             DMA((16,)), DMA((16,)), DMA((16,)), DMA((16,)),
         ],
         compiler_params=params(),
         name="back",
-    )(near, gg, dg, du, hid, t, wo, mid, cot, got, ratio, den)
+    )(near, gg, dg, du, hid, t, wo, wm, mid, cot, got, ratio, den)
 
 
 def end_kernel(
@@ -1128,12 +1238,7 @@
     room = zm.shape[2] // 3
     nq, nv = wq.shape[1], wv.shape[1]
     lanes = g1.shape[1]
-
-    def fold(prod):
-        acc = prod[:, 0:lanes]
-        for c in range(1, prod.shape[1] // lanes):
-            acc = acc + prod[:, c * lanes : (c + 1) * lanes]
-        return acc
+    scale1, scale2 = column(g1), column(g2)
 
     def total(cols):
         acc = za[0, :, cols].astype(f32)
@@ -1147,7 +1252,7 @@
         for c in range(w.shape[1] // lanes):
             cols = slice(c * lanes, (c + 1) * lanes)
             value = total(slice(at + c * lanes, at + (c + 1) * lanes))
-            out[:, cols] = value * g1[...]
+            out[:, cols] = value * scale1
             first = first + value * w[:, cols].astype(f32)
         at += w.shape[1]
     for c in range(nv // lanes):
@@ -1155,14 +1260,13 @@
             total(slice(at + c * lanes, at + (c + 1) * lanes))
         )
     second = jnp.zeros((zm.shape[1], lanes), f32)
-    whole = units // lanes * lanes
     for n in range(ZED):
         for base, w, out in ((0, wg, o_g), (room, wu, o_u)):
             for c in range(0, units, lanes):
                 size = min(lanes, units - c)
                 cols = slice(n * units + c, n * units + c + size)
                 value = zm[n, :, base + c : base + c + size].astype(f32)
-                out[:, cols] = value * g2[:, 0:size]
+                out[:, cols] = value * scale2[:, 0:size]
                 prod = value * w[:, cols].astype(f32)
                 if size == lanes:
                     second = second + prod
@@ -1197,29 +1301,12 @@
     inputs, norm_gain1, w_query, w_key, w_value, w_out, norm_gain2, w_gate, w_up, w_down, cotangent
 ):
     mbs, count, wide = inputs.shape
-    heads = w_query.shape[1] // F
-    units = w_gate.shape[1] // ZED
-    room = -(-units // 128) * 128
-    qk, vv = 2 * heads * F, heads * DV
     rows = w_query.shape[0]
-    gain1, gain2 = norm_gain1.astype(f32)[:, None], norm_gain2.astype(f32)[:, None]
-
-    def folded(weight, gain):
-        return (weight.astype(f32) * gain).astype(bf16)
-
-    a1 = jnp.concatenate([folded(w_query, gain1), folded(w_key, gain1), folded(w_value, gain1)], axis=1)
-
-    def cut(weight):
-        pieces = jnp.transpose(weight.reshape(rows, ZED, units), (1, 0, 2))
-        return jnp.pad(pieces, ((0, 0), (0, 0), (0, room - units)))
-
-    m = jnp.concatenate([cut(folded(w_gate, gain2)), cut(folded(w_up, gain2)), cut(w_down.T)], axis=2)
-    stream = inputs.astype(f32).reshape(mbs * count, wide)
-    r1 = lax.rsqrt(jnp.mean(stream * stream, axis=-1, keepdims=True) + epsilon)
-    xh1 = (stream * r1).astype(bf16)
-    wa1, w_o, wm, gg, got, ratio, den, heads_out, middle, near = front(
-        a1, w_out.T, m, cotangent, xh1, inputs
-    )
+    gain1, gain2 = norm_gain1.reshape(1, rows), norm_gain2.reshape(1, rows)
+    wa1, w_o, wm, gg, got, ratio, den, heads_out, middle, near, xh1 = front(
+        w_query, w_key, w_value, w_out, w_gate, w_up, w_down, gain1, gain2, cotangent, inputs
+    )
+    room = wm.shape[1] // 3
     w_g, w_u, w_d = wm[:, :room], wm[:, room : 2 * room], wm[:, 2 * room :]
     many = ZED * mbs * count
     n2 = near.reshape(many, wide)
@@ -1232,19 +1319,17 @@
     hidden = (silu * up).astype(bf16)
     d_gate = (d_hidden * up * sig * (1.0 + gate * (1.0 - sig))).astype(bf16)
     d_up = (d_hidden * silu).astype(bf16)
-    branch = mix(hidden, w_d, ((1,), (1,))).astype(bf16)
     d_n2 = (mix(d_gate, w_g, ((1,), (1,))) + mix(d_up, w_u, ((1,), (1,)))).astype(bf16)
     lines = (ZED, mbs, count, wide)
-    zm, d_mid, d_att, home = back(
-        n2, up_g, d_gate, d_up, hidden, d_n2.reshape(lines), w_o, middle, cotangent, got, ratio, den
+    zm, d_mid, d_att, home, branch = back(
+        n2, up_g, d_gate, d_up, hidden, d_n2.reshape(lines), w_o, wm, middle, cotangent, got, ratio, den
     )
     za, input_grad, outputs = end(
         branch.reshape(lines), home, xh1, d_att, heads_out, wa1, d_mid, inputs, middle
     )
-    full = (rows, 128)
     o_q, o_k, o_v, o_out, o_g, o_u, o_d, gains = finish(
         zm, za, w_query, w_key, w_value, w_gate, w_up,
-        jnp.broadcast_to(gain1, full), jnp.broadcast_to(gain2, full), w_out, w_down,
+        gain1, gain2, w_out, w_down,
     )
     gains = lax.psum(gains, "head")
     return (outputs, input_grad, gains[0], o_q, o_k, o_v, o_out, gains[1], o_g, o_u, o_d)

time: 555 us -> 517 us (0.932)
  Pallas kernels: 496 us -> 478 us
  matrix products: 30.9 us -> 24 us
  other arithmetic: 6.74 us -> 0 us
  local copies, waits for them, and re-layouts: 9.44 us -> 3.04 us
    pallas_call x1, Pallas kernels: 216 us -> 205 us  [front(): pl.pallas_call(front_kernel, out_shape=(shape((wide, wide1), bf16), shape...]
    pallas_call x1, Pallas kernels: 153 us -> 144 us  [back(): pl.pallas_call(back_kernel, out_shape=(shape((ZED, 128, cols), bf16), sha...]
    dot_general x6 -> x5, matrix products: 30.9 us -> 24 us  [mix(): return lax.dot_general(a, b, (over, ((), ())), preferred_element_type=f32)]
where the time goes in v6:
time: 517 us; the launch traced here: 509 us
  Pallas kernels  478 us (92%)
  matrix products  24 us (5%)
    pallas_call x1, Pallas kernels, front(): pl.pallas_call(front_kernel, out_shape=(shape((wide, wide1), bf16), shape...  205 us
    pallas_call x1, Pallas kernels, back(): pl.pallas_call(back_kernel, out_shape=(shape((ZED, 128, cols), bf16), sha...  144 us
    pallas_call x1, Pallas kernels, end(): pl.pallas_call(end_kernel, out_shape=(shape((ZED, 128, cols), bf16), shap...  123 us
    dot_general x5, matrix products, mix(): return lax.dot_general(a, b, (over, ((), ())), preferred_element_type=f32)  24 us

profile of v6, /device:TPU:0, one launch (start us, length us, event | category | flops | bytes accessed | tf_op | source)
XLA Modules:
  0.0 509.0 jit_solution(9895385758757989875)
XLA Ops:
  0.6 204.6 %front.1 = (bf16[2048,1280]{1,0:T(8,128)(2,1)}, bf16[2048,1024]{1,0:T(8,128)(2,1)}, bf16[2048,2304]{1,0:T(8,128)(2,1)}, bf16[4,2,128,2048]{3,2,1,0:T(8,128)(2,1)...) custom-call(bf16[128,128]{1,0:T(8,128)(2,1)} %wq.3, ...), custom_call_target="tpu_custom_call" | custom-call | tf_op jit(solution)/shard_map/front/pallas_call | solution.py:665
  205.2 0.0 copy-start
  205.2 0.0 copy-start.1
  205.2 6.5 %fusion.1 = f32[1024,768]{1,0:T(8,128)S(1)} fusion(bf16[1024,2048]{1,0:T(8,128)(2,1)} %bitcast.15, bf16[2048,2304]{1,0:T(8,128)(2,1)} %get-tuple-element.40.wm), kind=kOutput, calls=%fused_computation.6 | convolution fusion | flops 3221225472 | bytes 10485760 | tf_op jit(solution)/shard_map/dot_general | solution.py:285
  211.7 0.0 copy-done
  211.7 0.6 copy-done.1
  212.3 3.4 fusion.5
  215.7 5.5 %multiply_convert_fusion = (bf16[1024,768]{1,0:T(8,128)(2,1)}, bf16[1024,768]{1,0:T(8,128)(2,1)S(1)}, bf16[1024,768]{1,0:T(8,128)(2,1)S(1)}) fusion(f32[1024,768]{1,0:T(8,128)S(1)} %fusion.5, f32[1024,768]{1,0:T(8,128)S(1)} %fusion.1, bf16[1024,2048]{1,0:T(8,128)(2,1)S(1)} %bitcast.19, bf16[2048,2304]{1,0:T(8,128)(2,1)S(1)} %copy-done), kind=kOutput, calls=%fused_computation.1 | convolution fusion | flops 3233021952 | bytes 18350080 | tf_op jit(solution)/shard_map/dot_general | solution.py:285
  221.2 0.0 copy-start.2
  221.2 0.0 copy-start.3
  221.2 3.5 fusion.3
  224.7 0.0 copy-done.2
  224.7 0.0 copy-done.3
  224.7 5.1 %add_convert_fusion = bf16[1024,2048]{1,0:T(8,128)(2,1)} fusion(f32[1024,2048]{1,0:T(8,128)S(1)} %fusion.3, bf16[1024,768]{1,0:T(8,128)(2,1)S(1)} %get-tuple-element.67.du, bf16[2048,2304]{1,0:T(8,128)(2,1)S(1)} %copy-done), kind=kOutput, calls=%fused_computation | convolution fusion | flops 3225419776 | bytes 17301504 | tf_op jit(solution)/shard_map/dot_general | solution.py:285
  229.8 144.0 %back.1 = (bf16[4,128,2304]{2,1,0:T(8,128)(2,1)}, f32[2,128,2048]{2,1,0:T(8,128)}, bf16[256,2048]{1,0:T(8,128)(2,1)}, bf16[16,160,128]{2,1,0:T(8,128)(2,1)}, bf16[1024,2048]{1,0:T(8,128)(2,1)}) custom-call(bf16[1024,2048]{1,0:T(8,128)(2,1)} %bitcast.17, bf16[1024,2048]{1,0:T(8,128)(2,1)} %bitcast.16, bf16[1024,768]{1,0:T(8,128)(2,1)} %copy-done.2, ...), custom_call_target="tpu_custom_call" | custom-call | tf_op jit(solution)/shard_map/back/pallas_call | solution.py:1081
  373.8 122.9 %end.1 = (bf16[4,128,2304]{2,1,0:T(8,128)(2,1)}, bf16[2,128,2048]{2,1,0:T(8,128)(2,1)}, bf16[2,128,2048]{2,1,0:T(8,128)(2,1)}) custom-call(bf16[4,2,128,2048]{3,2,1,0:T(8,128)(2,1)} %bitcast.20, bf16[16,160,128]{2,1,0:T(8,128)(2,1)} %get-tuple-element.47.home, bf16[256,2048]{1,0:T(8,128)(2,1)} %get-tuple-element.48.xh, ...), custom_call_target="tpu_custom_call" | custom-call | tf_op jit(solution)/shard_map/end/pallas_call | solution.py:1214
  496.8 0.0 copy-start.5
  496.8 0.0 copy-start.4
  496.8 6.7 %finish.1 = (f32[128,128]{1,0:T(8,128)}, f32[128,128]{1,0:T(8,128)}, f32[128,1024]{1,0:T(8,128)}, f32[1024,128]{1,0:T(8,128)}, f32[128,2816]{1,0:T(8,128)}, /*in...) custom-call(bf16[4,128,2304]{2,1,0:T(8,128)(2,1)} %get-tuple-element.55.zm, ...), custom_call_target="tpu_custom_call" | custom-call | tf_op jit(solution)/shard_map/finish/pallas_call | solution.py:1287
  503.5 2.6 psum.7
  506.1 0.5 slice_bitcast_fusion
  506.6 0.0 copy-done.5
  506.6 1.0 copy.24
  507.6 0.0 copy-done.4
  507.6 1.0 copy.25
Async XLA Ops:
  205.2 6.5 %copy-start = (bf16[2048,2304]{1,0:T(8,128)(2,1)S(1)}, bf16[2048,2304]{1,0:T(8,128)(2,1)}, u32[]{:S(2)}) copy-start(bf16[2048,2304]{1,0:T(8,128)(2,1)} %get-tuple-element.40.wm) | copy-start | bytes 28311556
  205.2 7.0 %copy-start.1 = (bf16[4,2,128,2048]{3,2,1,0:T(8,128)(2,1)S(1)}, bf16[4,2,128,2048]{3,2,1,0:T(8,128)(2,1)}, u32[]{:S(2)}) copy-start(bf16[4,2,128,2048]{3,2,1,0:T(8,128)(2,1)} %get-tuple-element.38) | copy-start | bytes 12582916
  221.2 3.5 copy-start.2
  221.2 3.5 copy-start.3
  496.8 9.9 %copy-start.5 = (bf16[2,128,2048]{2,1,0:T(8,128)(2,1)S(1)}, bf16[2,128,2048]{2,1,0:T(8,128)(2,1)}, u32[]{:S(2)}) copy-start(bf16[2,128,2048]{2,1,0:T(8,128)(2,1)} %get-tuple-element.81) | copy-start | bytes 3145732
  496.8 10.8 %copy-start.4 = (bf16[2,128,2048]{2,1,0:T(8,128)(2,1)S(1)}, bf16[2,128,2048]{2,1,0:T(8,128)(2,1)}, u32[]{:S(2)}) copy-start(bf16[2,128,2048]{2,1,0:T(8,128)(2,1)} %get-tuple-element.82) | copy-start | bytes 3145732

commit v7 on v6

--- a/solution.py
+++ b/solution.py
@@ -743,7 +743,8 @@
 
 
 class Scatter:
-    def __init__(self, g, low_acc, high_acc, fin, out, r1x, r1y, r2x, r2y, s, q, go):
+    def __init__(self, g, low_acc, high_acc, fin, out, r1x, r1y, r2x, r2y, s, q, go, planes=None, relay=None):
+        self.planes, self.relay = planes, relay
         self.g, self.low_acc, self.high_acc, self.fin, self.out = g, low_acc, high_acc, fin, out
         self.r1x, self.r1y, self.r2x, self.r2y, self.s, self.q = r1x, r1y, r2x, r2y, s, q
         self.go = go
@@ -754,8 +755,11 @@
         self.half = r1x.shape[-1]
         self.low, self.high = pl.ds(0, self.half), pl.ds(self.half, self.half)
 
+    def plane(self, d):
+        return (self.z + d) % ZED if self.planes is None else self.planes[d]
+
     def first_copies(self, d):
-        zz, x, y, g = (self.z + d) % ZED, self.x, self.y, self.g
+        zz, x, y, g = self.plane(d), self.x, self.y, self.g
         return (
             remote(g.at[zz, :, 1 - x, :, self.low], self.r1x.at[d], self.s.at[d, 0], self.q.at[d, 0], self.at_x, self.h),
             remote(g.at[zz, 1 - y, :, :, self.high], self.r1y.at[d], self.s.at[d, 1], self.q.at[d, 1], self.at_y, self.h),
@@ -794,12 +798,11 @@
         for copy in self.second_copies(d):
             self.go(copy)
 
-    def third(self, d):
-        x, y, me, h, z = self.x, self.y, self.me, self.h, self.z
+    def third_sum(self, d, target):
+        x, y, me, h = self.x, self.y, self.me, self.h
         arrived(self.r2y.at[d], self.s.at[d, 2], self.q.at[d, 2], me, h)
         arrived(self.r2x.at[d], self.s.at[d, 3], self.q.at[d, 3], me, h)
         fin, low, high = self.fin(d), self.low, self.high
-        target = fin if d else self.out.at[z]
 
         def body(i, carry):
             row = chunk(i)
@@ -816,15 +819,52 @@
             return carry
 
         lax.fori_loop(0, 8, body, 0)
+
+    def third(self, d):
+        fin, z = self.fin(d), self.z
+        self.third_sum(d, fin if d else self.out.at[z])
         if d:
-            there = index_of((z + d) % ZED, y, x)
-            self.go(remote(fin, self.out.at[z], self.s.at[d, 4], self.q.at[d, 4], there, h))
+            there = index_of((z + d) % ZED, self.y, self.x)
+            self.go(remote(fin, self.out.at[z], self.s.at[d, 4], self.q.at[d, 4], there, self.h))
 
     def last(self):
         for d in (1, 3, 2):
             arrived(
                 self.out.at[(self.z + ZED - d) % ZED], self.s.at[d, 4], self.q.at[d, 4], self.me, self.h
             )
+
+    def third_join(self, k):
+        fin = self.fin(k)
+        self.third_sum(k, fin if k else self.out.at[0])
+        near = index_of(self.planes[1], self.y, self.x)
+        if k == 1:
+            self.go(remote(fin, self.out.at[1], self.s.at[1, 4], self.q.at[1, 4], near, self.h))
+        if k > 1:
+            outer = (self.z == 0) | (self.z == ZED - 1)
+            copy = remote(fin, self.relay.at[3 - k], self.s.at[k, 4], self.q.at[5 - k, 4], near, self.h)
+            self.go(copy, outer)
+
+    def join(self, k):
+        fin, relay, s, q = self.fin(k), self.relay, self.s, self.q
+        inner = (self.z > 0) & (self.z < ZED - 1)
+
+        @pl.when(inner)
+        def _():
+            arrived(relay.at[k - 2], s.at[k, 4], q.at[k, 4], self.me, self.h)
+
+            def body(i, carry):
+                row = chunk(i)
+                fin[row, :] = (fin[row, :].astype(f32) + relay[k - 2, row, :].astype(f32)).astype(bf16)
+                return carry
+
+            lax.fori_loop(0, 8, body, 0)
+
+        far = index_of(self.planes[k], self.y, self.x)
+        self.go(remote(fin, self.out.at[2], s.at[k, 4], q.at[0, 4], far, self.h), inner)
+
+    def joined(self):
+        arrived(self.out.at[1], self.s.at[1, 4], self.q.at[1, 4], self.me, self.h)
+        arrived(self.out.at[2], self.s.at[0, 4], self.q.at[0, 4], self.me, self.h)
 
 
 class Combine:
@@ -880,6 +920,82 @@
 
     def done(self):
         arrived(self.out.at[1 - self.h], self.s.at[0, 1], self.q.at[0, 1], self.me, 1 - self.h)
+
+
+class Join:
+    def __init__(self, t, out, other, summed, landed, relay, ls, s, q, go, planes):
+        self.t, self.out, self.other, self.summed, self.landed = t, out, other, summed, landed
+        self.relay, self.ls, self.s, self.q, self.go, self.planes = relay, ls, s, q, go, planes
+        self.x, self.y, self.z, self.h = where_am_i()
+        self.me = index_of(self.z, self.y, self.x)
+        self.inner = (self.z > 0) & (self.z < ZED - 1)
+        self.outer = (self.z == 0) | (self.z == ZED - 1)
+
+    def begin(self):
+        self.own = {}
+        for k in (2, 3, 1, 0):
+            zz = self.planes[k]
+            self.own[k] = pltpu.make_async_copy(self.t.at[zz, self.h], self.summed.at[k], self.ls.at[k])
+            self.own[k].start()
+            self.go(
+                remote(self.t.at[zz, 1 - self.h], self.other.at[k], self.s.at[k, 0], self.q.at[k, 0], self.me, 1 - self.h)
+            )
+
+    def add(self, k, ref, index):
+        summed = self.summed
+
+        def body(turn, carry):
+            row = chunk(turn)
+            summed[k, row, :] = (
+                summed[k, row, :].astype(f32) + ref[index, row, :].astype(f32)
+            ).astype(bf16)
+            return carry
+
+        lax.fori_loop(0, 8, body, 0)
+
+    def spread(self):
+        near = index_of(self.planes[1], self.y, self.x)
+        for k in (2, 3, 1, 0):
+            self.own[k].wait()
+            arrived(self.other.at[k], self.s.at[k, 0], self.q.at[k, 0], self.me, 1 - self.h)
+            self.add(k, self.other, k)
+            if k == 1:
+                self.go(remote(self.summed.at[1], self.landed.at[0], self.s.at[1, 1], self.q.at[1, 1], near, self.h))
+            if k > 1:
+                copy = remote(
+                    self.summed.at[k], self.relay.at[3 - k], self.s.at[k, 1], self.q.at[5 - k, 1], near, self.h
+                )
+                self.go(copy, self.outer)
+
+    def join(self, k):
+        @pl.when(self.inner)
+        def _():
+            arrived(self.relay.at[k - 2], self.s.at[k, 1], self.q.at[k, 1], self.me, self.h)
+            self.add(k, self.relay, k - 2)
+
+        far = index_of(self.planes[k], self.y, self.x)
+        copy = remote(self.summed.at[k], self.landed.at[1], self.s.at[k, 1], self.q.at[0, 1], far, self.h)
+        self.go(copy, self.inner)
+
+    def total(self):
+        summed, landed, out, h = self.summed, self.landed, self.out, self.h
+        arrived(landed.at[0], self.s.at[1, 1], self.q.at[1, 1], self.me, h)
+        arrived(landed.at[1], self.s.at[0, 1], self.q.at[0, 1], self.me, h)
+
+        def body(turn, carry):
+            row = chunk(turn)
+            out[h, row, :] = (
+                summed[0, row, :].astype(f32)
+                + landed[0, row, :].astype(f32)
+                + landed[1, row, :].astype(f32)
+            ).astype(bf16)
+            return carry
+
+        lax.fori_loop(0, 8, body, 0)
+        self.go(remote(out.at[h], out.at[h], self.s.at[4, 0], self.q.at[4, 0], self.me, 1 - h))
+
+    def done(self):
+        arrived(self.out.at[1 - self.h], self.s.at[4, 0], self.q.at[4, 0], self.me, 1 - self.h)
 
 
 def back_kernel(
@@ -1117,7 +1233,7 @@
 def end_kernel(
     t, home, xh, d_att, heads_out, wa1, d_mid, xin, mid,
     za, d_in, outputs,
-    g, r1x, r1y, r2x, r2y, branch, other, summed, landed, w1, dqk_t, dqkv, part, swap,
+    g, r1x, r1y, r2x, r2y, relay, branch, other, summed, landed, relayed, w1, dqk_t, dqkv, part, swap,
     ls, gs, gq, cs, cq, ws, wr,
 ):
     x, y, z, h = where_am_i()
@@ -1127,17 +1243,21 @@
     qk, vv = 2 * heads * F, heads * DV
     late = []
 
-    def go(copy):
-        copy.start()
-        late.append(copy)
-
-    combine = Combine(t, branch, other, summed, landed, ls, cs, cq, go)
+    def go(copy, true=None):
+        if true is None:
+            copy.start()
+        else:
+            pl.when(true)(copy.start)
+        late.append((true, copy))
+
+    planes = (z, z + 1 - 2 * (z % 2), ZED - 1 - z, (z + 2) % ZED)
+    combine = Join(t, branch, other, summed, landed, relayed, ls, cs, cq, go, planes)
     scatter = Scatter(
         g,
-        lambda d: g.at[(z + d) % ZED, 1 - y, x, :, pl.ds(0, g.shape[-1] // 2)],
-        lambda d: g.at[(z + d) % ZED, y, 1 - x, :, pl.ds(g.shape[-1] // 2, g.shape[-1] // 2)],
-        lambda d: g.at[(z + d) % ZED, y, x],
-        za, r1x, r1y, r2x, r2y, gs, gq, go,
+        lambda k: g.at[planes[k], 1 - y, x, :, pl.ds(0, g.shape[-1] // 2)],
+        lambda k: g.at[planes[k], y, 1 - x, :, pl.ds(g.shape[-1] // 2, g.shape[-1] // 2)],
+        lambda k: g.at[planes[k], y, x],
+        za, r1x, r1y, r2x, r2y, gs, gq, go, planes, relay,
     )
     combine.begin()
     weight = pltpu.make_async_copy(wa1, w1, ls.at[4])
@@ -1150,22 +1270,36 @@
             dqk_t[(heads + k) * F : (heads + k + 1) * F, cols] = block[F : 2 * F, :].astype(f32)
             dqkv[cols, qk + k * DV : qk + (k + 1) * DV] = block[2 * F :, :]
     dqkv[:, 0:qk] = jnp.transpose(dqk_t[...]).astype(bf16)
-    for n, d in enumerate(FAR):
-        zz = (z + d) % ZED
-        for yy in range(2):
-            for xx in range(2):
-                at = pl.ds(pl.multiple_of(index_of(zz, yy, xx) * 128, 128), 128)
-                g[zz, yy, xx, :, 0 : qk + vv] = mix(xh[:, at], dqkv[...], ((0,), (0,))).astype(bf16)
-                g[zz, yy, xx, :, qk + vv :] = mix(d_att[:, at], heads_out[...], ((0,), (0,))).astype(bf16)
-        scatter.first(d)
-        if n == 0:
-            combine.spread()
+
+    def terms(k):
+        zz = planes[k]
+
+        def body(n, carry):
+            at = pl.ds(pl.multiple_of((zz * 4 + n) * 128, 128), 128)
+            g[zz, n // 2, n % 2, :, 0 : qk + vv] = mix(xh[:, at], dqkv[...], ((0,), (0,))).astype(bf16)
+            g[zz, n // 2, n % 2, :, qk + vv :] = mix(d_att[:, at], heads_out[...], ((0,), (0,))).astype(bf16)
+            return carry
+
+        lax.fori_loop(0, 4, body, 0)
+
+    terms(2)
+    scatter.first(2)
+    combine.spread()
+    terms(3)
+    scatter.first(3)
+    scatter.second(2)
+    terms(1)
+    scatter.first(1)
     weight.wait()
     for c in range(wide // COLS):
         cols = pl.ds(c * COLS, COLS)
         part[:, c * COLS : (c + 1) * COLS] = mix(dqkv[...], w1[c * COLS : (c + 1) * COLS, :], ((1,), (1,)))
         go(remote(part.at[:, cols], swap.at[:, cols], ws.at[c], wr.at[c], me, 1 - h))
-    scatter.second(2)
+    scatter.second(3)
+    combine.join(3)
+    terms(0)
+    scatter.third_join(2)
+    combine.join(2)
     for c in range(wide // COLS):
         cols = pl.ds(c * COLS, COLS)
         arrived(swap.at[:, cols], ws.at[c], wr.at[c], me, 1 - h)
@@ -1185,13 +1319,13 @@
 
         lax.fori_loop(0, count // 16, body, 0)
     scatter.second(1)
-    scatter.third(2)
-    scatter.second(3)
-    scatter.third(1)
+    scatter.first(0)
+    scatter.third_join(3)
+    scatter.join(3)
+    scatter.third_join(1)
+    scatter.join(2)
+    combine.total()
     scatter.second(0)
-    scatter.third(3)
-    combine.total()
-    scatter.third(0)
     combine.done()
     for mb in range(mbs):
 
@@ -1201,9 +1335,13 @@
             return carry
 
         lax.fori_loop(0, count // 16, body, 0)
-    scatter.last()
-    for copy in late:
-        copy.wait_send()
+    scatter.third_join(0)
+    scatter.joined()
+    for true, copy in late:
+        if true is None:
+            copy.wait_send()
+        else:
+            pl.when(true)(copy.wait_send)
 
 
 def end(t, home, xh, d_att, heads_out, wa1, d_mid, xin, mid):
@@ -1213,17 +1351,20 @@
     line = pltpu.VMEM((ZED, count, wide), bf16)
     return pl.pallas_call(
         end_kernel,
-        out_shape=(shape((ZED, 128, cols), bf16), shape(xin.shape, bf16), shape(xin.shape, bf16)),
+        out_shape=(shape((3, 128, cols), bf16), shape(xin.shape, bf16), shape(xin.shape, bf16)),
         in_specs=[ANY] + [VMEM] * 4 + [ANY] + [VMEM] * 3,
         out_specs=(VMEM,) * 3,
         scratch_shapes=[pltpu.VMEM((ZED, 2, 2, 128, cols), bf16)] + scatter_room(cols) + [
-            pltpu.VMEM(xin.shape, bf16), line, line, line,
+            pltpu.VMEM((2, 128, cols), bf16),
+            pltpu.VMEM(xin.shape, bf16), line, line,
+            pltpu.VMEM((2, count, wide), bf16),
+            pltpu.VMEM((2, count, wide), bf16),
             pltpu.VMEM(wa1.shape, bf16),
             pltpu.VMEM((mbs * count, mbs * count), f32),
             pltpu.VMEM((mbs * count, wa1.shape[1]), bf16),
             pltpu.VMEM((mbs * count, wide), f32),
             pltpu.VMEM((mbs * count, wide), f32),
-            DMA((6,)), DMA((4, 5)), DMA((4, 5)), DMA((4, 2)), DMA((4, 2)),
+            DMA((6,)), DMA((4, 5)), DMA((4, 5)), DMA((5, 2)), DMA((5, 2)),
             DMA((wide // COLS,)), DMA((wide // COLS,)),
         ],
         compiler_params=params(),
@@ -1242,7 +1383,7 @@
 
     def total(cols):
         acc = za[0, :, cols].astype(f32)
-        for n in range(1, ZED):
+        for n in range(1, za.shape[0]):
             acc = acc + za[n, :, cols].astype(f32)
         return acc
 

time: 517 us -> 488 us (0.944)
  Pallas kernels: 478 us -> 449 us
    pallas_call x1, Pallas kernels: 123 us -> 94.1 us  [end(): pl.pallas_call(end_kernel, out_shape=(shape((3, 128, cols), bf16), shape(...]
where the time goes in v7:
time: 488 us; the launch traced here: 480 us
  Pallas kernels  449 us (92%)
  matrix products  24 us (5%)
    pallas_call x1, Pallas kernels, front(): pl.pallas_call(front_kernel, out_shape=(shape((wide, wide1), bf16), shape...  205 us
    pallas_call x1, Pallas kernels, back(): pl.pallas_call(back_kernel, out_shape=(shape((ZED, 128, cols), bf16), sha...  144 us
    pallas_call x1, Pallas kernels, end(): pl.pallas_call(end_kernel, out_shape=(shape((3, 128, cols), bf16), shape(...  94.1 us
    dot_general x5, matrix products, mix(): return lax.dot_general(a, b, (over, ((), ())), preferred_element_type=f32)  24 us

profile of v7, /device:TPU:0, one launch (start us, length us, event | category | flops | bytes accessed | tf_op | source)
XLA Modules:
  0.0 480.0 jit_solution(1045789334024143953)
XLA Ops:
  0.6 204.6 %front.1 = (bf16[2048,1280]{1,0:T(8,128)(2,1)}, bf16[2048,1024]{1,0:T(8,128)(2,1)}, bf16[2048,2304]{1,0:T(8,128)(2,1)}, bf16[4,2,128,2048]{3,2,1,0:T(8,128)(2,1)...) custom-call(bf16[128,128]{1,0:T(8,128)(2,1)} %wq.3, ...), custom_call_target="tpu_custom_call" | custom-call | tf_op jit(solution)/shard_map/front/pallas_call | solution.py:665
  205.2 0.0 copy-start
  205.2 0.0 copy-start.1
  205.2 6.5 %fusion.1 = f32[1024,768]{1,0:T(8,128)S(1)} fusion(bf16[1024,2048]{1,0:T(8,128)(2,1)} %bitcast.15, bf16[2048,2304]{1,0:T(8,128)(2,1)} %get-tuple-element.40.wm), kind=kOutput, calls=%fused_computation.6 | convolution fusion | flops 3221225472 | bytes 10485760 | tf_op jit(solution)/shard_map/dot_general | solution.py:285
  211.7 0.0 copy-done
  211.7 0.6 copy-done.1
  212.3 3.4 fusion.5
  215.7 5.5 %multiply_convert_fusion = (bf16[1024,768]{1,0:T(8,128)(2,1)}, bf16[1024,768]{1,0:T(8,128)(2,1)S(1)}, bf16[1024,768]{1,0:T(8,128)(2,1)S(1)}) fusion(f32[1024,768]{1,0:T(8,128)S(1)} %fusion.5, f32[1024,768]{1,0:T(8,128)S(1)} %fusion.1, bf16[1024,2048]{1,0:T(8,128)(2,1)S(1)} %bitcast.19, bf16[2048,2304]{1,0:T(8,128)(2,1)S(1)} %copy-done), kind=kOutput, calls=%fused_computation.1 | convolution fusion | flops 3233021952 | bytes 18350080 | tf_op jit(solution)/shard_map/dot_general | solution.py:285
  221.2 0.0 copy-start.2
  221.2 0.0 copy-start.3
  221.2 3.5 fusion.3
  224.7 0.0 copy-done.2
  224.7 0.0 copy-done.3
  224.7 5.1 %add_convert_fusion = bf16[1024,2048]{1,0:T(8,128)(2,1)} fusion(f32[1024,2048]{1,0:T(8,128)S(1)} %fusion.3, bf16[1024,768]{1,0:T(8,128)(2,1)S(1)} %get-tuple-element.67.du, bf16[2048,2304]{1,0:T(8,128)(2,1)S(1)} %copy-done), kind=kOutput, calls=%fused_computation | convolution fusion | flops 3225419776 | bytes 17301504 | tf_op jit(solution)/shard_map/dot_general | solution.py:285
  229.8 144.0 %back.1 = (bf16[4,128,2304]{2,1,0:T(8,128)(2,1)}, f32[2,128,2048]{2,1,0:T(8,128)}, bf16[256,2048]{1,0:T(8,128)(2,1)}, bf16[16,160,128]{2,1,0:T(8,128)(2,1)}, bf16[1024,2048]{1,0:T(8,128)(2,1)}) custom-call(bf16[1024,2048]{1,0:T(8,128)(2,1)} %bitcast.17, bf16[1024,2048]{1,0:T(8,128)(2,1)} %bitcast.16, bf16[1024,768]{1,0:T(8,128)(2,1)} %copy-done.2, ...), custom_call_target="tpu_custom_call" | custom-call | tf_op jit(solution)/shard_map/back/pallas_call | solution.py:1197
  373.8 94.1 %end.1 = (bf16[3,128,2304]{2,1,0:T(8,128)(2,1)}, bf16[2,128,2048]{2,1,0:T(8,128)(2,1)}, bf16[2,128,2048]{2,1,0:T(8,128)(2,1)}) custom-call(bf16[4,2,128,2048]{3,2,1,0:T(8,128)(2,1)} %bitcast.20, bf16[16,160,128]{2,1,0:T(8,128)(2,1)} %get-tuple-element.47.home, bf16[256,2048]{1,0:T(8,128)(2,1)} %get-tuple-element.48.xh, ...), custom_call_target="tpu_custom_call" | custom-call | tf_op jit(solution)/shard_map/end/pallas_call | solution.py:1352
  468.0 0.0 copy-start.5
  468.0 0.0 copy-start.4
  468.0 6.6 %finish.1 = (f32[128,128]{1,0:T(8,128)}, f32[128,128]{1,0:T(8,128)}, f32[128,1024]{1,0:T(8,128)}, f32[1024,128]{1,0:T(8,128)}, f32[128,2816]{1,0:T(8,128)}, /*in...) custom-call(bf16[4,128,2304]{2,1,0:T(8,128)(2,1)} %get-tuple-element.55.zm, ...), custom_call_target="tpu_custom_call" | custom-call | tf_op jit(solution)/shard_map/finish/pallas_call | solution.py:1428
  474.5 2.6 psum.7
  477.1 0.5 slice_bitcast_fusion
  477.6 0.0 copy-done.5
  477.6 1.0 copy.24
  478.6 0.0 copy-done.4
  478.6 1.0 copy.25
Async XLA Ops:
  205.2 6.5 %copy-start = (bf16[2048,2304]{1,0:T(8,128)(2,1)S(1)}, bf16[2048,2304]{1,0:T(8,128)(2,1)}, u32[]{:S(2)}) copy-start(bf16[2048,2304]{1,0:T(8,128)(2,1)} %get-tuple-element.40.wm) | copy-start | bytes 28311556
  205.2 7.0 %copy-start.1 = (bf16[4,2,128,2048]{3,2,1,0:T(8,128)(2,1)S(1)}, bf16[4,2,128,2048]{3,2,1,0:T(8,128)(2,1)}, u32[]{:S(2)}) copy-start(bf16[4,2,128,2048]{3,2,1,0:T(8,128)(2,1)} %get-tuple-element.38) | copy-start | bytes 12582916
  221.2 3.5 copy-start.2
  221.2 3.5 copy-start.3
  468.0 9.7 %copy-start.5 = (bf16[2,128,2048]{2,1,0:T(8,128)(2,1)S(1)}, bf16[2,128,2048]{2,1,0:T(8,128)(2,1)}, u32[]{:S(2)}) copy-start(bf16[2,128,2048]{2,1,0:T(8,128)(2,1)} %get-tuple-element.81) | copy-start | bytes 3145732
  468.0 10.6 %copy-start.4 = (bf16[2,128,2048]{2,1,0:T(8,128)(2,1)S(1)}, bf16[2,128,2048]{2,1,0:T(8,128)(2,1)}, u32[]{:S(2)}) copy-start(bf16[2,128,2048]{2,1,0:T(8,128)(2,1)} %get-tuple-element.82) | copy-start | bytes 3145732

commit v8 on v7

--- a/solution.py
+++ b/solution.py
@@ -325,9 +325,9 @@
 
 def front_kernel(
     wq, wk, wv, w_out, wg, wu, wd, g1, g2, cot, xin,
-    wa1, wa2, wm, gg, got, ratio, den, heads_out, middle, near, xh,
-    a1, a2, m, w1, w2, pack, q_t, k_t, va, ob, part, other,
-    ls, zs, zr, us, ur, ps, pr, e1s, e1r, e2s, e2r, ws, wr, ds, dr,
+    wa1, wa2, wm, gg, got_out, ratio_out, den_out, heads_store, middle_out, near, xh_out,
+    got, ratio, den, heads_out, middle, xh, fresh, a1, a2, m, w1, w2, pack, q_t, k_t, va, ob, part, other,
+    os, ls, zs, zr, us, ur, ps, pr, e1s, e1r, e2s, e2r, ws, wr, ds, dr,
 ):
     x, y, z, h = where_am_i()
     me = index_of(z, y, x)
@@ -335,6 +335,12 @@
     count = xin.shape[1]
     heads = 16 // xin.shape[0]
     late = []
+    stored = []
+
+    def store(src, dst):
+        copy = pltpu.make_async_copy(src, dst, os.at[len(stored)])
+        copy.start()
+        stored.append(copy)
 
     def when(true, do):
         if true is None:
@@ -532,6 +538,7 @@
             return carry
 
         lax.fori_loop(0, count // 16, normed, 0)
+    store(xh, xh_out)
     both(onward, 0, 3)
     both(hop, 1, 2)
     both(hop, 1, 3)
@@ -572,12 +579,16 @@
     for d in range(1, 16):
         arrived(got.at[(me + 16 - d) % 16], e1s.at[d], e1r.at[d], me, h)
     both(onward, 1, 3)
+    store(got, got_out)
     spread(got, q_t, k_t, va)
     causal = lower(CHUNK)
     for qi in range(va.shape[0] // CHUNK):
         attend_rows(qi, q_t, k_t, va, ratio, den, causal)
     for b in range(16):
         ob[b, :, :] = ratio[b * count : (b + 1) * count, :].astype(bf16)
+
+    store(ratio, ratio_out)
+    store(den, den_out)
 
     def window(source):
         return heads_out.at[
@@ -600,6 +611,7 @@
     keep.wait()
     for d in range(1, 16):
         arrived(window((me + 16 - d) % 16), e2s.at[d], e2r.at[d], me, h)
+    store(heads_out, heads_store)
     wide = part.shape[1]
     for c in range(wide // COLS):
         cols = pl.ds(c * COLS, COLS)
@@ -621,14 +633,16 @@
             mid = xin[mb, row, :].astype(f32) + (part[flat, :] + other[flat, :])
             middle[mb, row, :] = mid
             scale = lax.rsqrt(jnp.mean(mid * mid, axis=-1, keepdims=True) + epsilon)
-            near[z, mb, row, :] = (mid * scale).astype(bf16)
+            fresh[mb, row, :] = (mid * scale).astype(bf16)
             return carry
 
         lax.fori_loop(0, count // 16, body, 0)
 
     one(h)
-    offer(NEAR)
+    offer(NEAR, fresh.at[h])
     one(1 - h)
+    store(middle, middle_out)
+    store(fresh, near.at[z])
     m_onward(1)
     both(hop, COT, 2)
     m_plane(3)
@@ -652,6 +666,8 @@
             both(across_done, kind, step)
     out1.wait()
     out2.wait()
+    for copy in stored:
+        copy.wait()
     for true, copy in late:
         when(true, copy.wait_send)
 
@@ -678,8 +694,15 @@
             shape((mbs * count, wide), bf16),
         ),
         in_specs=[VMEM] * 9 + [ANY] + [VMEM],
-        out_specs=(ANY,) * 4 + (VMEM,) * 7,
+        out_specs=(ANY,) * 11,
         scratch_shapes=[
+            pltpu.VMEM((16, 2 * F + DV, count), bf16),
+            pltpu.VMEM((depth, DV), f32),
+            pltpu.VMEM((depth, DV), f32),
+            pltpu.VMEM((mbs * count, wide2), bf16),
+            pltpu.VMEM(xin.shape, f32),
+            pltpu.VMEM((mbs * count, wide), bf16),
+            pltpu.VMEM(xin.shape, bf16),
             pltpu.VMEM((wq.shape[0], wide1), bf16),
             pltpu.VMEM((wq.shape[0], wide2), bf16),
             pltpu.VMEM((ZED, wq.shape[0], wide3), bf16),
@@ -692,7 +715,7 @@
             pltpu.VMEM((16, count, DV), bf16),
             pltpu.VMEM((mbs * count, wide), f32),
             pltpu.VMEM((mbs * count, wide), f32),
-            DMA((7,)), DMA((4,)), DMA((4,)), DMA((4, 2, 4)), DMA((4, 2, 4)), DMA((3, 7, 4)), DMA((3, 7, 4)),
+            DMA((8,)), DMA((7,)), DMA((4,)), DMA((4,)), DMA((4, 2, 4)), DMA((4, 2, 4)), DMA((3, 7, 4)), DMA((3, 7, 4)),
             DMA((16,)), DMA((16,)), DMA((16,)), DMA((16,)),
             DMA((wide // COLS,)), DMA((wide // COLS,)), DMA((4, 2, 4)), DMA((4, 2, 4)),
         ],
@@ -735,9 +758,6 @@
         d_v[ks, :] = jnp.transpose(acc_v)
 
 
-FAR = (2, 1, 3, 0)
-
-
 def chunk(turn):
     return pl.ds(pl.multiple_of(turn * 16, 16), 16)
 
@@ -867,61 +887,6 @@
         arrived(self.out.at[2], self.s.at[0, 4], self.q.at[0, 4], self.me, self.h)
 
 
-class Combine:
-    def __init__(self, t, out, other, summed, landed, ls, s, q, go):
-        self.t, self.out, self.other, self.summed, self.landed = t, out, other, summed, landed
-        self.ls, self.s, self.q, self.go = ls, s, q, go
-        self.x, self.y, self.z, self.h = where_am_i()
-        self.me = index_of(self.z, self.y, self.x)
-
-    def begin(self):
-        t, h, other = self.t, self.h, self.other
-        self.own = {}
-        for d in FAR:
-            zz = (self.z + d) % ZED
-            self.own[d] = pltpu.make_async_copy(t.at[zz, h], self.summed.at[d], self.ls.at[d])
-            self.own[d].start()
-            self.go(remote(t.at[zz, 1 - h], other.at[d], self.s.at[d, 0], self.q.at[d, 0], self.me, 1 - h))
-
-    def spread(self):
-        summed, other = self.summed, self.other
-        for d in FAR:
-            zz = (self.z + d) % ZED
-            self.own[d].wait()
-            arrived(other.at[d], self.s.at[d, 0], self.q.at[d, 0], self.me, 1 - self.h)
-
-            def add(turn, carry):
-                row = chunk(turn)
-                summed[d, row, :] = (
-                    summed[d, row, :].astype(f32) + other[d, row, :].astype(f32)
-                ).astype(bf16)
-                return carry
-
-            lax.fori_loop(0, 8, add, 0)
-            if d:
-                there = index_of(zz, self.y, self.x)
-                self.go(remote(summed.at[d], self.landed.at[d], self.s.at[d, 1], self.q.at[d, 1], there, self.h))
-
-    def total(self):
-        summed, landed, out, h = self.summed, self.landed, self.out, self.h
-        for d in (1, 3, 2):
-            arrived(landed.at[d], self.s.at[d, 1], self.q.at[d, 1], self.me, h)
-
-        def body(turn, carry):
-            row = chunk(turn)
-            acc = summed[0, row, :].astype(f32)
-            for d in (1, 2, 3):
-                acc = acc + landed[d, row, :].astype(f32)
-            out[h, row, :] = acc.astype(bf16)
-            return carry
-
-        lax.fori_loop(0, 8, body, 0)
-        self.go(remote(out.at[h], out.at[h], self.s.at[0, 1], self.q.at[0, 1], self.me, 1 - h))
-
-    def done(self):
-        arrived(self.out.at[1 - self.h], self.s.at[0, 1], self.q.at[0, 1], self.me, 1 - self.h)
-
-
 class Join:
     def __init__(self, t, out, other, summed, landed, relay, ls, s, q, go, planes):
         self.t, self.out, self.other, self.summed, self.landed = t, out, other, summed, landed
@@ -967,15 +932,17 @@
                 )
                 self.go(copy, self.outer)
 
+    def join_sum(self, k):
+        arrived(self.relay.at[k - 2], self.s.at[k, 1], self.q.at[k, 1], self.me, self.h)
+        self.add(k, self.relay, k - 2)
+
+    def join_copy(self, k):
+        far = index_of(self.planes[k], self.y, self.x)
+        return remote(self.summed.at[k], self.landed.at[1], self.s.at[k, 1], self.q.at[0, 1], far, self.h)
+
     def join(self, k):
-        @pl.when(self.inner)
-        def _():
-            arrived(self.relay.at[k - 2], self.s.at[k, 1], self.q.at[k, 1], self.me, self.h)
-            self.add(k, self.relay, k - 2)
-
-        far = index_of(self.planes[k], self.y, self.x)
-        copy = remote(self.summed.at[k], self.landed.at[1], self.s.at[k, 1], self.q.at[0, 1], far, self.h)
-        self.go(copy, self.inner)
+        pl.when(self.inner)(lambda: self.join_sum(k))
+        self.go(self.join_copy(k), self.inner)
 
     def total(self):
         summed, landed, out, h = self.summed, self.landed, self.out, self.h
@@ -999,11 +966,12 @@
 
 
 def back_kernel(
-    near, gg, dg, du, hid, t, wo, wm, mid, cot, got, ratio, den,
+    near, gg, dg_in, du_in, hid_in, t, wo, wm, mid_in, cot_in, got_in, ratio_in, den_in,
     zm, d_mid, d_att, home, tb,
-    g, r1x, r1y, r2x, r2y, e2, other, summed, landed, w2, pack, d_o, d_qk, d_v,
+    g, r1x, r1y, r2x, r2y, e2, other, summed, landed, relayed, w2, pack, d_o, d_qk, d_v,
     q_t, k_t, va, da, dn_t, pack2, nbuf, gbuf, turned, stage,
-    ls, fs, bs, gs, gq, cs, cq, e1s, e1r, e2s, e2r,
+    dg, du, hid, mid, cot, got, ratio, den,
+    hs, ls, fs, bs, gs, gq, cs, cq, e1s, e1r, e2s, e2r,
 ):
     x, y, z, h = where_am_i()
     me = index_of(z, y, x)
@@ -1012,9 +980,12 @@
     room = dg.shape[1]
     late = []
 
-    def go(copy):
-        copy.start()
-        late.append(copy)
+    def go(copy, true=None):
+        if true is None:
+            copy.start()
+        else:
+            pl.when(true)(copy.start)
+        late.append((true, copy))
 
     def fetch(i):
         cols = pl.ds(pl.multiple_of(((z + ZED - 1 - i) % ZED) * 512, 512), 512)
@@ -1025,7 +996,15 @@
 
     for copy in fetch(0):
         copy.start()
-    combine = Combine(t, e2, other, summed, landed, ls, cs, cq, go)
+    pairs = (
+        (dg_in, dg), (du_in, du), (hid_in, hid), (mid_in, mid), (cot_in, cot), (got_in, got),
+        (ratio_in, ratio), (den_in, den),
+    )
+    brought = [pltpu.make_async_copy(src, dst, hs.at[n]) for n, (src, dst) in enumerate(pairs)]
+    for copy in brought:
+        copy.start()
+    planes = (z, z + 1 - 2 * (z % 2), ZED - 1 - z, (z + 2) % ZED)
+    combine = Join(t, e2, other, summed, landed, relayed, ls, cs, cq, go, planes)
     scatter = Scatter(
         g,
         lambda d: g.at[(z + d) % ZED, 1 - y, x, :, pl.ds(0, g.shape[-1] // 2)],
@@ -1037,6 +1016,8 @@
     weight = pltpu.make_async_copy(wo, w2, ls.at[4])
     weight.start()
     combine.spread()
+    for copy in brought[0:3]:
+        copy.wait()
 
     def block(i, carry):
         d = ZED - 1 - i
@@ -1068,19 +1049,70 @@
             for copy in scatter.first_copies(d):
                 copy.start()
 
-        @pl.when((i > 0) & (i < ZED - 1))
+        @pl.when(i == 1)
         def _():
             scatter.second_sum(d + 1)
             for copy in scatter.second_copies(d + 1):
                 copy.start()
 
+        for k in (3, 2):
+
+            @pl.when((i == 3 - k) & combine.inner)
+            def _():
+                combine.join_sum(k)
+                combine.join_copy(k).start()
+
         return carry
 
-    lax.fori_loop(0, ZED, block, 0)
+    lax.fori_loop(0, ZED - 1, block, 0)
     for d in (1, 2, 3):
-        late.extend(scatter.first_copies(d))
-    for d in (2, 3):
-        late.extend(scatter.second_copies(d))
+        late.extend((None, copy) for copy in scatter.first_copies(d))
+    late.extend((None, copy) for copy in scatter.second_copies(3))
+    for k in (2, 3):
+        late.append((combine.inner, combine.join_copy(k)))
+    combine.total()
+    weight.wait()
+    combine.done()
+    for copy in brought[3:]:
+        copy.wait()
+
+    for mb in range(mid.shape[0]):
+
+        def body(turn, carry):
+            row = chunk(turn)
+            m = mid[mb, row, :]
+            scale = lax.rsqrt(jnp.mean(m * m, axis=-1, keepdims=True) + epsilon)
+            hat = m * scale
+            e = e2[mb, row, :].astype(f32)
+            d_m = cot[mb, row, :].astype(f32) + scale * (
+                e - hat * jnp.mean(e * hat, axis=-1, keepdims=True)
+            )
+            d_mid[mb, row, :] = d_m
+            d_att[pl.ds(pl.multiple_of(mb * count + turn * 16, 16), 16), :] = d_m.astype(bf16)
+            return carry
+
+        lax.fori_loop(0, count // 16, body, 0)
+    for c in range(heads * DV // COLS):
+        val = mix(d_att[...], w2[:, c * COLS : (c + 1) * COLS], ((1,), (0,))).astype(bf16)
+        for mb in range(16 // heads):
+            for i in range(COLS // DV):
+                pack[c * (COLS // DV) + i + heads * mb, :, :] = val[
+                    mb * count : (mb + 1) * count, i * DV : (i + 1) * DV
+                ]
+
+    def window(source):
+        return d_o.at[pl.ds(pl.multiple_of(source * count, count), count)]
+
+    own = pltpu.make_async_copy(pack.at[me], window(me), ls.at[5])
+    own.start()
+    for d in range(1, 16):
+        there = (me + d) % 16
+        go(remote(pack.at[there], window(me), e1s.at[d], e1r.at[d], there, h))
+    scatter.second(2)
+    scatter.third(3)
+    scatter.second(1)
+    lax.fori_loop(ZED - 1, ZED, block, 0)
+    scatter.first(0)
     half = near.shape[1] // 2
     shards = []
     for r in range(2):
@@ -1097,46 +1129,21 @@
         )
         for copy in shards[r]:
             copy.start()
-    weight.wait()
-    scatter.third(3)
-    combine.total()
-    combine.done()
-
-    for mb in range(mid.shape[0]):
-
-        def body(turn, carry):
-            row = chunk(turn)
-            m = mid[mb, row, :]
-            scale = lax.rsqrt(jnp.mean(m * m, axis=-1, keepdims=True) + epsilon)
-            hat = m * scale
-            e = e2[mb, row, :].astype(f32)
-            d_m = cot[mb, row, :].astype(f32) + scale * (
-                e - hat * jnp.mean(e * hat, axis=-1, keepdims=True)
-            )
-            d_mid[mb, row, :] = d_m
-            d_att[pl.ds(pl.multiple_of(mb * count + turn * 16, 16), 16), :] = d_m.astype(bf16)
-            return carry
-
-        lax.fori_loop(0, count // 16, body, 0)
-    for c in range(heads * DV // COLS):
-        val = mix(d_att[...], w2[:, c * COLS : (c + 1) * COLS], ((1,), (0,))).astype(bf16)
-        for mb in range(16 // heads):
-            for i in range(COLS // DV):
-                pack[c * (COLS // DV) + i + heads * mb, :, :] = val[
-                    mb * count : (mb + 1) * count, i * DV : (i + 1) * DV
-                ]
-
-    def window(source):
-        return d_o.at[pl.ds(pl.multiple_of(source * count, count), count)]
-
-    own = pltpu.make_async_copy(pack.at[me], window(me), ls.at[5])
+    scatter.third(2)
+    own.wait()
+    for d in range(1, 16):
+        arrived(window((me + 16 - d) % 16), e1s.at[d], e1r.at[d], me, h)
+    attend_back_body(got, ratio, den, d_o, d_qk, d_v, q_t, k_t, va, da, dn_t)
+    for b in range(16):
+        pack2[b, 0 : 2 * F, :] = d_qk[:, b * count : (b + 1) * count].astype(bf16)
+        pack2[b, 2 * F :, :] = d_v[b * count : (b + 1) * count, :].astype(bf16)
+    own = pltpu.make_async_copy(pack2.at[me], home.at[me], ls.at[5])
     own.start()
     for d in range(1, 16):
         there = (me + d) % 16
-        go(remote(pack.at[there], window(me), e1s.at[d], e1r.at[d], there, h))
-    scatter.second(1)
-    scatter.first(0)
-    scatter.third(2)
+        go(remote(pack2.at[there], home.at[me], e2s.at[d], e2r.at[d], there, h))
+    scatter.third(1)
+    scatter.second(0)
     stored = {}
     for n in range(2 * half // COLS):
         r, c = n // (half // COLS), n % (half // COLS)
@@ -1154,29 +1161,18 @@
             stage.at[n % 2], tb.at[:, pl.ds(n * COLS, COLS)], bs.at[n % 2]
         )
         stored[n].start()
-    own.wait()
-    for d in range(1, 16):
-        arrived(window((me + 16 - d) % 16), e1s.at[d], e1r.at[d], me, h)
-    attend_back_body(got, ratio, den, d_o, d_qk, d_v, q_t, k_t, va, da, dn_t)
-    for b in range(16):
-        pack2[b, 0 : 2 * F, :] = d_qk[:, b * count : (b + 1) * count].astype(bf16)
-        pack2[b, 2 * F :, :] = d_v[b * count : (b + 1) * count, :].astype(bf16)
-    own = pltpu.make_async_copy(pack2.at[me], home.at[me], ls.at[5])
-    own.start()
-    for d in range(1, 16):
-        there = (me + d) % 16
-        go(remote(pack2.at[there], home.at[me], e2s.at[d], e2r.at[d], there, h))
+    scatter.third(0)
     stored[2 * half // COLS - 2].wait()
     stored[2 * half // COLS - 1].wait()
-    scatter.third(1)
-    scatter.second(0)
-    scatter.third(0)
     own.wait()
     for d in range(1, 16):
         arrived(home.at[(me + 16 - d) % 16], e2s.at[d], e2r.at[d], me, h)
     scatter.last()
-    for copy in late:
-        copy.wait_send()
+    for true, copy in late:
+        if true is None:
+            copy.wait_send()
+        else:
+            pl.when(true)(copy.wait_send)
 
 
 def scatter_room(wide):
@@ -1203,10 +1199,12 @@
             shape((16, 2 * F + DV, count), bf16),
             shape(near.shape, bf16),
         ),
-        in_specs=[ANY] * 2 + [VMEM] * 3 + [ANY] * 3 + [VMEM] * 5,
+        in_specs=[ANY] * 13,
         out_specs=(VMEM,) * 4 + (ANY,),
         scratch_shapes=[pltpu.VMEM((ZED, 2, 2, 128, cols), bf16)] + scatter_room(cols) + [
-            pltpu.VMEM(cot.shape, bf16), line, line, line,
+            pltpu.VMEM(cot.shape, bf16), line, line,
+            pltpu.VMEM((2, count, wide), bf16),
+            pltpu.VMEM((2, count, wide), bf16),
             pltpu.VMEM(wo.shape, bf16),
             pltpu.VMEM((16, count, DV), bf16),
             pltpu.VMEM((depth, DV), bf16),
@@ -1222,7 +1220,15 @@
             pltpu.VMEM((2, near.shape[0], 512), bf16),
             pltpu.VMEM((512, near.shape[0]), bf16),
             pltpu.VMEM((2, near.shape[0], COLS), bf16),
-            DMA((6,)), DMA((2, 2)), DMA((2,)), DMA((4, 5)), DMA((4, 5)), DMA((4, 2)), DMA((4, 2)),
+            pltpu.VMEM(dg.shape, bf16),
+            pltpu.VMEM(dg.shape, bf16),
+            pltpu.VMEM(dg.shape, bf16),
+            pltpu.VMEM(mid.shape, f32),
+            pltpu.VMEM(cot.shape, bf16),
+            pltpu.VMEM(got.shape, bf16),
+            pltpu.VMEM(ratio.shape, f32),
+            pltpu.VMEM(den.shape, f32),
+            DMA((8,)), DMA((6,)), DMA((2, 2)), DMA((2,)), DMA((4, 5)), DMA((4, 5)), DMA((5, 2)), DMA((5, 2)),
             DMA((16,)), DMA((16,)), DMA((16,)), DMA((16,)),
         ],
         compiler_params=params(),
@@ -1231,10 +1237,10 @@
 
 
 def end_kernel(
-    t, home, xh, d_att, heads_out, wa1, d_mid, xin, mid,
+    t, home, xh, d_att, heads_out, wa1, d_mid_in, xin_in, mid_in,
     za, d_in, outputs,
     g, r1x, r1y, r2x, r2y, relay, branch, other, summed, landed, relayed, w1, dqk_t, dqkv, part, swap,
-    ls, gs, gq, cs, cq, ws, wr,
+    d_mid, xin, mid, hs, ls, gs, gq, cs, cq, ws, wr,
 ):
     x, y, z, h = where_am_i()
     me = index_of(z, y, x)
@@ -1260,6 +1266,13 @@
         za, r1x, r1y, r2x, r2y, gs, gq, go, planes, relay,
     )
     combine.begin()
+    brought = [
+        pltpu.make_async_copy(d_mid_in, d_mid, hs.at[0]),
+        pltpu.make_async_copy(xin_in, xin, hs.at[1]),
+        pltpu.make_async_copy(mid_in, mid, hs.at[2]),
+    ]
+    for copy in brought:
+        copy.start()
     weight = pltpu.make_async_copy(wa1, w1, ls.at[4])
     weight.start()
     for mb in range(mbs):
@@ -1291,6 +1304,8 @@
     terms(1)
     scatter.first(1)
     weight.wait()
+    for copy in brought:
+        copy.wait()
     for c in range(wide // COLS):
         cols = pl.ds(c * COLS, COLS)
         part[:, c * COLS : (c + 1) * COLS] = mix(dqkv[...], w1[c * COLS : (c + 1) * COLS, :], ((1,), (1,)))
@@ -1352,7 +1367,7 @@
     return pl.pallas_call(
         end_kernel,
         out_shape=(shape((3, 128, cols), bf16), shape(xin.shape, bf16), shape(xin.shape, bf16)),
-        in_specs=[ANY] + [VMEM] * 4 + [ANY] + [VMEM] * 3,
+        in_specs=[ANY] + [VMEM] * 4 + [ANY] * 4,
         out_specs=(VMEM,) * 3,
         scratch_shapes=[pltpu.VMEM((ZED, 2, 2, 128, cols), bf16)] + scatter_room(cols) + [
             pltpu.VMEM((2, 128, cols), bf16),
@@ -1364,7 +1379,10 @@
             pltpu.VMEM((mbs * count, wa1.shape[1]), bf16),
             pltpu.VMEM((mbs * count, wide), f32),
             pltpu.VMEM((mbs * count, wide), f32),
-            DMA((6,)), DMA((4, 5)), DMA((4, 5)), DMA((5, 2)), DMA((5, 2)),
+            pltpu.VMEM(d_mid.shape, f32),
+            pltpu.VMEM(xin.shape, bf16),
+            pltpu.VMEM(mid.shape, f32),
+            DMA((3,)), DMA((6,)), DMA((4, 5)), DMA((4, 5)), DMA((5, 2)), DMA((5, 2)),
             DMA((wide // COLS,)), DMA((wide // COLS,)),
         ],
         compiler_params=params(),

time: 488 us -> 467 us (0.957)
  Pallas kernels: 449 us -> 428 us
    pallas_call x1, Pallas kernels: 144 us -> 126 us  [back(): pl.pallas_call(back_kernel, out_shape=(shape((ZED, 128, cols), bf16), sha...]
where the time goes in v8:
time: 467 us; the launch traced here: 459 us
  Pallas kernels  428 us (92%)
  matrix products  24 us (5%)
    pallas_call x1, Pallas kernels, front(): pl.pallas_call(front_kernel, out_shape=(shape((wide, wide1), bf16), shape...  201 us
    pallas_call x1, Pallas kernels, back(): pl.pallas_call(back_kernel, out_shape=(shape((ZED, 128, cols), bf16), sha...  126 us
    pallas_call x1, Pallas kernels, end(): pl.pallas_call(end_kernel, out_shape=(shape((3, 128, cols), bf16), shape(...  94.6 us
    dot_general x5, matrix products, mix(): return lax.dot_general(a, b, (over, ((), ())), preferred_element_type=f32)  24 us

profile of v8, /device:TPU:0, one launch (start us, length us, event | category | flops | bytes accessed | tf_op | source)
XLA Modules:
  0.0 459.3 jit_solution(11240705245407109456)
XLA Ops:
  0.6 201.2 %front.1 = (bf16[2048,1280]{1,0:T(8,128)(2,1)}, bf16[2048,1024]{1,0:T(8,128)(2,1)}, bf16[2048,2304]{1,0:T(8,128)(2,1)}, bf16[4,2,128,2048]{3,2,1,0:T(8,128)(2,1)...) custom-call(bf16[128,128]{1,0:T(8,128)(2,1)} %wq.3, ...), custom_call_target="tpu_custom_call" | custom-call | tf_op jit(solution)/shard_map/front/pallas_call | solution.py:681
  201.8 0.0 copy-start
  201.8 0.0 copy-start.1
  201.9 6.5 %fusion.1 = f32[1024,768]{1,0:T(8,128)S(1)} fusion(bf16[1024,2048]{1,0:T(8,128)(2,1)} %bitcast.15, bf16[2048,2304]{1,0:T(8,128)(2,1)} %get-tuple-element.40.wm), kind=kOutput, calls=%fused_computation.6 | convolution fusion | flops 3221225472 | bytes 10485760 | tf_op jit(solution)/shard_map/dot_general | solution.py:285
  208.3 0.0 copy-done
  208.3 0.6 copy-done.1
  208.9 3.4 fusion.5
  212.3 5.5 %multiply_convert_fusion = (bf16[1024,768]{1,0:T(8,128)(2,1)}, bf16[1024,768]{1,0:T(8,128)(2,1)S(1)}, bf16[1024,768]{1,0:T(8,128)(2,1)S(1)}) fusion(f32[1024,768]{1,0:T(8,128)S(1)} %fusion.5, f32[1024,768]{1,0:T(8,128)S(1)} %fusion.1, bf16[1024,2048]{1,0:T(8,128)(2,1)S(1)} %bitcast.19, bf16[2048,2304]{1,0:T(8,128)(2,1)S(1)} %copy-done), kind=kOutput, calls=%fused_computation.1 | convolution fusion | flops 3233021952 | bytes 18350080 | tf_op jit(solution)/shard_map/dot_general | solution.py:285
  217.8 0.0 copy-start.2
  217.8 0.0 copy-start.3
  217.9 3.5 fusion.3
  221.3 0.0 copy-done.2
  221.3 0.0 copy-done.3
  221.3 5.1 %add_convert_fusion = bf16[1024,2048]{1,0:T(8,128)(2,1)} fusion(f32[1024,2048]{1,0:T(8,128)S(1)} %fusion.3, bf16[1024,768]{1,0:T(8,128)(2,1)S(1)} %get-tuple-element.67.du_in, bf16[2048,2304]{1,0:T(8,128)(2,1)S(1)} %copy-done), kind=kOutput, calls=%fused_computation | convolution fusion | flops 3225419776 | bytes 17301504 | tf_op jit(solution)/shard_map/dot_general | solution.py:285
  226.4 126.2 %back.1 = (bf16[4,128,2304]{2,1,0:T(8,128)(2,1)}, f32[2,128,2048]{2,1,0:T(8,128)}, bf16[256,2048]{1,0:T(8,128)(2,1)}, bf16[16,160,128]{2,1,0:T(8,128)(2,1)}, bf16[1024,2048]{1,0:T(8,128)(2,1)}) custom-call(bf16[1024,2048]{1,0:T(8,128)(2,1)} %bitcast.17, bf16[1024,2048]{1,0:T(8,128)(2,1)} %bitcast.16, bf16[1024,768]{1,0:T(8,128)(2,1)} %copy-done.2, ...), custom_call_target="tpu_custom_call" | custom-call | tf_op jit(solution)/shard_map/back/pallas_call | solution.py:1193
  352.6 94.6 %end.1 = (bf16[3,128,2304]{2,1,0:T(8,128)(2,1)}, bf16[2,128,2048]{2,1,0:T(8,128)(2,1)}, bf16[2,128,2048]{2,1,0:T(8,128)(2,1)}) custom-call(bf16[4,2,128,2048]{3,2,1,0:T(8,128)(2,1)} %bitcast.20, bf16[16,160,128]{2,1,0:T(8,128)(2,1)} %get-tuple-element.47.home, bf16[256,2048]{1,0:T(8,128)(2,1)} %get-tuple-element.48.xh, ...), custom_call_target="tpu_custom_call" | custom-call | tf_op jit(solution)/shard_map/end/pallas_call | solution.py:1367
  447.2 0.0 copy-start.5
  447.2 0.0 copy-start.4
  447.2 6.6 %finish.1 = (f32[128,128]{1,0:T(8,128)}, f32[128,128]{1,0:T(8,128)}, f32[128,1024]{1,0:T(8,128)}, f32[1024,128]{1,0:T(8,128)}, f32[128,2816]{1,0:T(8,128)}, /*in...) custom-call(bf16[4,128,2304]{2,1,0:T(8,128)(2,1)} %get-tuple-element.55.zm, ...), custom_call_target="tpu_custom_call" | custom-call | tf_op jit(solution)/shard_map/finish/pallas_call | solution.py:1446
  453.8 2.6 psum.7
  456.4 0.5 slice_bitcast_fusion
  456.9 0.0 copy-done.5
  456.9 1.0 copy.24
  457.9 0.0 copy-done.4
  457.9 1.0 copy.25
Async XLA Ops:
  201.8 6.5 %copy-start = (bf16[2048,2304]{1,0:T(8,128)(2,1)S(1)}, bf16[2048,2304]{1,0:T(8,128)(2,1)}, u32[]{:S(2)}) copy-start(bf16[2048,2304]{1,0:T(8,128)(2,1)} %get-tuple-element.40.wm) | copy-start | bytes 28311556
  201.8 7.0 %copy-start.1 = (bf16[4,2,128,2048]{3,2,1,0:T(8,128)(2,1)S(1)}, bf16[4,2,128,2048]{3,2,1,0:T(8,128)(2,1)}, u32[]{:S(2)}) copy-start(bf16[4,2,128,2048]{3,2,1,0:T(8,128)(2,1)} %get-tuple-element.38) | copy-start | bytes 12582916
  217.8 3.5 copy-start.2
  217.8 3.5 copy-start.3
  447.2 9.7 %copy-start.5 = (bf16[2,128,2048]{2,1,0:T(8,128)(2,1)S(1)}, bf16[2,128,2048]{2,1,0:T(8,128)(2,1)}, u32[]{:S(2)}) copy-start(bf16[2,128,2048]{2,1,0:T(8,128)(2,1)} %get-tuple-element.81) | copy-start | bytes 3145732
  447.2 10.6 %copy-start.4 = (bf16[2,128,2048]{2,1,0:T(8,128)(2,1)S(1)}, bf16[2,128,2048]{2,1,0:T(8,128)(2,1)}, u32[]{:S(2)}) copy-start(bf16[2,128,2048]{2,1,0:T(8,128)(2,1)} %get-tuple-element.82) | copy-start | bytes 3145732

commit v9 on v8

--- a/solution.py
+++ b/solution.py
@@ -555,13 +555,17 @@
             cols = slice(mb * count, (mb + 1) * count)
             pack[t, 0:F, :] = qk[k * F : (k + 1) * F, cols]
             pack[t, F : 2 * F, :] = qk[(heads + k) * F : (heads + k + 1) * F, cols]
-    for c in range(heads * DV // COLS):
-        at = 2 * heads * F + c * COLS
-        val = mix(xh[...], w1[:, at : at + COLS], ((1,), (0,))).astype(bf16)
+
+    def valued(c, carry):
+        cols = pl.ds(pl.multiple_of(2 * heads * F + c * COLS, COLS), COLS)
+        val = mix(xh[...], w1[:, cols], ((1,), (0,))).astype(bf16)
         for mb in range(16 // heads):
             for i in range(COLS // DV):
                 t = c * (COLS // DV) + i + heads * mb
                 pack[t, 2 * F :, :] = val[mb * count : (mb + 1) * count, i * DV : (i + 1) * DV]
+        return carry
+
+    lax.fori_loop(0, heads * DV // COLS, valued, 0)
     keep = pltpu.make_async_copy(pack.at[me], got.at[me], ls.at[4])
     keep.start()
     for d in range(1, 16):
@@ -613,12 +617,20 @@
         arrived(window((me + 16 - d) % 16), e2s.at[d], e2r.at[d], me, h)
     store(heads_out, heads_store)
     wide = part.shape[1]
+
+    def pair(c):
+        cols = pl.ds(pl.multiple_of(c * COLS, COLS), COLS)
+        return remote(part.at[:, cols], other.at[:, cols], ws.at[c], wr.at[c], me, 1 - h)
+
+    def project(c, carry):
+        cols = pl.ds(pl.multiple_of(c * COLS, COLS), COLS)
+        part[:, cols] = mix(heads_out[...], w2[cols, :], ((1,), (1,)))
+        pair(c).start()
+        return carry
+
+    lax.fori_loop(0, wide // COLS, project, 0)
     for c in range(wide // COLS):
-        cols = pl.ds(c * COLS, COLS)
-        part[:, c * COLS : (c + 1) * COLS] = mix(
-            heads_out[...], w2[c * COLS : (c + 1) * COLS, :], ((1,), (1,))
-        )
-        go(remote(part.at[:, cols], other.at[:, cols], ws.at[c], wr.at[c], me, 1 - h))
+        late.append((None, pair(c)))
     m_onward(0)
     both(hop, COT, 1)
     m_plane(2)
@@ -1092,13 +1104,18 @@
             return carry
 
         lax.fori_loop(0, count // 16, body, 0)
-    for c in range(heads * DV // COLS):
-        val = mix(d_att[...], w2[:, c * COLS : (c + 1) * COLS], ((1,), (0,))).astype(bf16)
+
+    def to_heads(c, carry):
+        cols = pl.ds(pl.multiple_of(c * COLS, COLS), COLS)
+        val = mix(d_att[...], w2[:, cols], ((1,), (0,))).astype(bf16)
         for mb in range(16 // heads):
             for i in range(COLS // DV):
                 pack[c * (COLS // DV) + i + heads * mb, :, :] = val[
                     mb * count : (mb + 1) * count, i * DV : (i + 1) * DV
                 ]
+        return carry
+
+    lax.fori_loop(0, heads * DV // COLS, to_heads, 0)
 
     def window(source):
         return d_o.at[pl.ds(pl.multiple_of(source * count, count), count)]
@@ -1144,26 +1161,33 @@
         go(remote(pack2.at[there], home.at[me], e2s.at[d], e2r.at[d], there, h))
     scatter.third(1)
     scatter.second(0)
-    stored = {}
-    for n in range(2 * half // COLS):
-        r, c = n // (half // COLS), n % (half // COLS)
-        if c == 0:
-            for copy in shards[r]:
-                copy.wait()
-        if n > 1:
-            stored[n - 2].wait()
-        at = slice(c * COLS, (c + 1) * COLS)
+    for pair in shards:
+        for copy in pair:
+            copy.wait()
+    pieces = half // COLS
+
+    def save(n):
+        at = pl.ds(pl.multiple_of(n * COLS, COLS), COLS)
+        return pltpu.make_async_copy(stage.at[n % 2], tb.at[:, at], bs.at[n % 2])
+
+    def down(n, carry):
+        @pl.when(n > 1)
+        def _():
+            save(n - 2).wait()
+
+        r = n // pieces
+        at = pl.ds(pl.multiple_of((n % pieces) * COLS, COLS), COLS)
         stage[n % 2, :, :] = (
             mix(hid[:, 0:512], nbuf[r, at, :], ((1,), (1,)))
             + mix(hid[:, 512:room], gbuf[r, at, 0 : room - 512], ((1,), (1,)))
         ).astype(bf16)
-        stored[n] = pltpu.make_async_copy(
-            stage.at[n % 2], tb.at[:, pl.ds(n * COLS, COLS)], bs.at[n % 2]
-        )
-        stored[n].start()
+        save(n).start()
+        return carry
+
+    lax.fori_loop(0, 2 * pieces, down, 0)
     scatter.third(0)
-    stored[2 * half // COLS - 2].wait()
-    stored[2 * half // COLS - 1].wait()
+    save(2 * pieces - 2).wait()
+    save(2 * pieces - 1).wait()
     own.wait()
     for d in range(1, 16):
         arrived(home.at[(me + 16 - d) % 16], e2s.at[d], e2r.at[d], me, h)
@@ -1306,10 +1330,20 @@
     weight.wait()
     for copy in brought:
         copy.wait()
+
+    def pair(c):
+        cols = pl.ds(pl.multiple_of(c * COLS, COLS), COLS)
+        return remote(part.at[:, cols], swap.at[:, cols], ws.at[c], wr.at[c], me, 1 - h)
+
+    def project(c, carry):
+        cols = pl.ds(pl.multiple_of(c * COLS, COLS), COLS)
+        part[:, cols] = mix(dqkv[...], w1[cols, :], ((1,), (1,)))
+        pair(c).start()
+        return carry
+
+    lax.fori_loop(0, wide // COLS, project, 0)
     for c in range(wide // COLS):
-        cols = pl.ds(c * COLS, COLS)
-        part[:, c * COLS : (c + 1) * COLS] = mix(dqkv[...], w1[c * COLS : (c + 1) * COLS, :], ((1,), (1,)))
-        go(remote(part.at[:, cols], swap.at[:, cols], ws.at[c], wr.at[c], me, 1 - h))
+        late.append((None, pair(c)))
     scatter.second(3)
     combine.join(3)
     terms(0)

time: 467 us -> 459 us (0.983); the launches traced: 459 us -> 459 us
  no operation moved by 1% of the time
where the time goes in v9:
time: 459 us
  Pallas kernels  428 us (93%)
  matrix products  24 us (5%)
    pallas_call x1, Pallas kernels, front(): pl.pallas_call(front_kernel, out_shape=(shape((wide, wide1), bf16), shape...  201 us
    pallas_call x1, Pallas kernels, back(): pl.pallas_call(back_kernel, out_shape=(shape((ZED, 128, cols), bf16), sha...  126 us
    pallas_call x1, Pallas kernels, end(): pl.pallas_call(end_kernel, out_shape=(shape((3, 128, cols), bf16), shape(...  94.6 us
    dot_general x5, matrix products, mix(): return lax.dot_general(a, b, (over, ((), ())), preferred_element_type=f32)  24 us

profile of v9, /device:TPU:0, one launch (start us, length us, event | category | flops | bytes accessed | tf_op | source)
XLA Modules:
  0.0 458.8 jit_solution(7467814354698753605)
XLA Ops:
  0.6 201.2 %front.1 = (bf16[2048,1280]{1,0:T(8,128)(2,1)}, bf16[2048,1024]{1,0:T(8,128)(2,1)}, bf16[2048,2304]{1,0:T(8,128)(2,1)}, bf16[4,2,128,2048]{3,2,1,0:T(8,128)(2,1)...) custom-call(bf16[128,128]{1,0:T(8,128)(2,1)} %wq.3, ...), custom_call_target="tpu_custom_call" | custom-call | tf_op jit(solution)/shard_map/front/pallas_call | solution.py:693
  201.8 0.0 copy-start
  201.8 0.0 copy-start.1
  201.9 6.3 %fusion.1 = f32[1024,768]{1,0:T(8,128)S(1)} fusion(bf16[1024,2048]{1,0:T(8,128)(2,1)} %bitcast.15, bf16[2048,2304]{1,0:T(8,128)(2,1)} %get-tuple-element.40.wm), kind=kOutput, calls=%fused_computation.6 | convolution fusion | flops 3221225472 | bytes 10485760 | tf_op jit(solution)/shard_map/dot_general | solution.py:285
  208.1 0.0 copy-done
  208.2 0.7 copy-done.1
  208.9 3.4 fusion.5
  212.3 5.7 %multiply_convert_fusion = (bf16[1024,768]{1,0:T(8,128)(2,1)}, bf16[1024,768]{1,0:T(8,128)(2,1)S(1)}, bf16[1024,768]{1,0:T(8,128)(2,1)S(1)}) fusion(f32[1024,768]{1,0:T(8,128)S(1)} %fusion.5, f32[1024,768]{1,0:T(8,128)S(1)} %fusion.1, bf16[1024,2048]{1,0:T(8,128)(2,1)S(1)} %bitcast.19, bf16[2048,2304]{1,0:T(8,128)(2,1)S(1)} %copy-done), kind=kOutput, calls=%fused_computation.1 | convolution fusion | flops 3233021952 | bytes 18350080 | tf_op jit(solution)/shard_map/dot_general | solution.py:285
  218.0 0.0 copy-start.2
  218.0 0.0 copy-start.3
  218.0 3.5 fusion.3
  221.5 0.0 copy-done.2
  221.5 0.0 copy-done.3
  221.5 5.1 %add_convert_fusion = bf16[1024,2048]{1,0:T(8,128)(2,1)} fusion(f32[1024,2048]{1,0:T(8,128)S(1)} %fusion.3, bf16[1024,768]{1,0:T(8,128)(2,1)S(1)} %get-tuple-element.67.du_in, bf16[2048,2304]{1,0:T(8,128)(2,1)S(1)} %copy-done), kind=kOutput, calls=%fused_computation | convolution fusion | flops 3225419776 | bytes 17301504 | tf_op jit(solution)/shard_map/dot_general | solution.py:285
  226.6 126.0 %back.1 = (bf16[4,128,2304]{2,1,0:T(8,128)(2,1)}, f32[2,128,2048]{2,1,0:T(8,128)}, bf16[256,2048]{1,0:T(8,128)(2,1)}, bf16[16,160,128]{2,1,0:T(8,128)(2,1)}, bf16[1024,2048]{1,0:T(8,128)(2,1)}) custom-call(bf16[1024,2048]{1,0:T(8,128)(2,1)} %bitcast.17, bf16[1024,2048]{1,0:T(8,128)(2,1)} %bitcast.16, bf16[1024,768]{1,0:T(8,128)(2,1)} %copy-done.2, ...), custom_call_target="tpu_custom_call" | custom-call | tf_op jit(solution)/shard_map/back/pallas_call | solution.py:1217
  352.6 94.6 %end.1 = (bf16[3,128,2304]{2,1,0:T(8,128)(2,1)}, bf16[2,128,2048]{2,1,0:T(8,128)(2,1)}, bf16[2,128,2048]{2,1,0:T(8,128)(2,1)}) custom-call(bf16[4,2,128,2048]{3,2,1,0:T(8,128)(2,1)} %bitcast.20, bf16[16,160,128]{2,1,0:T(8,128)(2,1)} %get-tuple-element.47.home, bf16[256,2048]{1,0:T(8,128)(2,1)} %get-tuple-element.48.xh, ...), custom_call_target="tpu_custom_call" | custom-call | tf_op jit(solution)/shard_map/end/pallas_call | solution.py:1401
  447.2 0.0 copy-start.5
  447.2 0.0 copy-start.4
  447.2 6.6 %finish.1 = (f32[128,128]{1,0:T(8,128)}, f32[128,128]{1,0:T(8,128)}, f32[128,1024]{1,0:T(8,128)}, f32[1024,128]{1,0:T(8,128)}, f32[128,2816]{1,0:T(8,128)}, /*in...) custom-call(bf16[4,128,2304]{2,1,0:T(8,128)(2,1)} %get-tuple-element.55.zm, ...), custom_call_target="tpu_custom_call" | custom-call | tf_op jit(solution)/shard_map/finish/pallas_call | solution.py:1480
  453.8 2.6 psum.7
  456.4 0.5 slice_bitcast_fusion
  456.9 0.0 copy-done.5
  456.9 1.0 copy.24
  457.9 0.0 copy-done.4
  457.9 1.0 copy.25
Async XLA Ops:
  201.8 6.3 %copy-start = (bf16[2048,2304]{1,0:T(8,128)(2,1)S(1)}, bf16[2048,2304]{1,0:T(8,128)(2,1)}, u32[]{:S(2)}) copy-start(bf16[2048,2304]{1,0:T(8,128)(2,1)} %get-tuple-element.40.wm) | copy-start | bytes 28311556
  201.8 7.0 %copy-start.1 = (bf16[4,2,128,2048]{3,2,1,0:T(8,128)(2,1)S(1)}, bf16[4,2,128,2048]{3,2,1,0:T(8,128)(2,1)}, u32[]{:S(2)}) copy-start(bf16[4,2,128,2048]{3,2,1,0:T(8,128)(2,1)} %get-tuple-element.38) | copy-start | bytes 12582916
  218.0 3.5 copy-start.2
  218.0 3.5 copy-start.3
  447.2 9.7 %copy-start.5 = (bf16[2,128,2048]{2,1,0:T(8,128)(2,1)S(1)}, bf16[2,128,2048]{2,1,0:T(8,128)(2,1)}, u32[]{:S(2)}) copy-start(bf16[2,128,2048]{2,1,0:T(8,128)(2,1)} %get-tuple-element.81) | copy-start | bytes 3145732
  447.2 10.6 %copy-start.4 = (bf16[2,128,2048]{2,1,0:T(8,128)(2,1)S(1)}, bf16[2,128,2048]{2,1,0:T(8,128)(2,1)}, u32[]{:S(2)}) copy-start(bf16[2,128,2048]{2,1,0:T(8,128)(2,1)} %get-tuple-element.82) | copy-start | bytes 3145732

commit v10 on v9

--- a/solution.py
+++ b/solution.py
@@ -859,8 +859,8 @@
             there = index_of((z + d) % ZED, self.y, self.x)
             self.go(remote(fin, self.out.at[z], self.s.at[d, 4], self.q.at[d, 4], there, self.h))
 
-    def last(self):
-        for d in (1, 3, 2):
+    def last(self, ds):
+        for d in ds:
             arrived(
                 self.out.at[(self.z + ZED - d) % ZED], self.s.at[d, 4], self.q.at[d, 4], self.me, self.h
             )
@@ -979,7 +979,7 @@
 
 def back_kernel(
     near, gg, dg_in, du_in, hid_in, t, wo, wm, mid_in, cot_in, got_in, ratio_in, den_in,
-    zm, d_mid, d_att, home, tb,
+    zm, d_mid, d_att, home, tb, rest,
     g, r1x, r1y, r2x, r2y, e2, other, summed, landed, relayed, w2, pack, d_o, d_qk, d_v,
     q_t, k_t, va, da, dn_t, pack2, nbuf, gbuf, turned, stage,
     dg, du, hid, mid, cot, got, ratio, den,
@@ -1146,7 +1146,10 @@
         )
         for copy in shards[r]:
             copy.start()
-    scatter.third(2)
+    scatter.third_sum(2, scatter.fin(2))
+    resting = pltpu.make_async_copy(scatter.fin(2), rest, ls.at[6])
+    resting.start()
+    zm[(z + 2) % ZED] = jnp.zeros(zm.shape[1:], bf16)
     own.wait()
     for d in range(1, 16):
         arrived(window((me + 16 - d) % 16), e1s.at[d], e1r.at[d], me, h)
@@ -1191,7 +1194,8 @@
     own.wait()
     for d in range(1, 16):
         arrived(home.at[(me + 16 - d) % 16], e2s.at[d], e2r.at[d], me, h)
-    scatter.last()
+    scatter.last((1, 3))
+    resting.wait()
     for true, copy in late:
         if true is None:
             copy.wait_send()
@@ -1222,9 +1226,10 @@
             shape((mbs * count, wide), bf16),
             shape((16, 2 * F + DV, count), bf16),
             shape(near.shape, bf16),
+            shape((128, cols), bf16),
         ),
         in_specs=[ANY] * 13,
-        out_specs=(VMEM,) * 4 + (ANY,),
+        out_specs=(VMEM,) * 4 + (ANY,) * 2,
         scratch_shapes=[pltpu.VMEM((ZED, 2, 2, 128, cols), bf16)] + scatter_room(cols) + [
             pltpu.VMEM(cot.shape, bf16), line, line,
             pltpu.VMEM((2, count, wide), bf16),
@@ -1252,7 +1257,7 @@
             pltpu.VMEM(got.shape, bf16),
             pltpu.VMEM(ratio.shape, f32),
             pltpu.VMEM(den.shape, f32),
-            DMA((8,)), DMA((6,)), DMA((2, 2)), DMA((2,)), DMA((4, 5)), DMA((4, 5)), DMA((5, 2)), DMA((5, 2)),
+            DMA((8,)), DMA((7,)), DMA((2, 2)), DMA((2,)), DMA((4, 5)), DMA((4, 5)), DMA((5, 2)), DMA((5, 2)),
             DMA((16,)), DMA((16,)), DMA((16,)), DMA((16,)),
         ],
         compiler_params=params(),
@@ -1261,10 +1266,10 @@
 
 
 def end_kernel(
-    t, home, xh, d_att, heads_out, wa1, d_mid_in, xin_in, mid_in,
-    za, d_in, outputs,
+    t, home, xh, d_att, heads_out, wa1, d_mid_in, xin_in, mid_in, rest,
+    za, d_in, outputs, zr,
     g, r1x, r1y, r2x, r2y, relay, branch, other, summed, landed, relayed, w1, dqk_t, dqkv, part, swap,
-    d_mid, xin, mid, hs, ls, gs, gq, cs, cq, ws, wr,
+    d_mid, xin, mid, hs, ts, ls, gs, gq, cs, cq, ws, wr,
 ):
     x, y, z, h = where_am_i()
     me = index_of(z, y, x)
@@ -1289,6 +1294,8 @@
         lambda k: g.at[planes[k], y, x],
         za, r1x, r1y, r2x, r2y, gs, gq, go, planes, relay,
     )
+    there = index_of((z + 2) % ZED, y, x)
+    go(remote(rest, zr, ts.at[0], ts.at[1], there, h))
     combine.begin()
     brought = [
         pltpu.make_async_copy(d_mid_in, d_mid, hs.at[0]),
@@ -1386,6 +1393,7 @@
         lax.fori_loop(0, count // 16, body, 0)
     scatter.third_join(0)
     scatter.joined()
+    arrived(zr, ts.at[0], ts.at[1], there, h)
     for true, copy in late:
         if true is None:
             copy.wait_send()
@@ -1393,16 +1401,16 @@
             pl.when(true)(copy.wait_send)
 
 
-def end(t, home, xh, d_att, heads_out, wa1, d_mid, xin, mid):
+def end(t, home, xh, d_att, heads_out, wa1, d_mid, xin, mid, rest):
     mbs, count, wide = xin.shape
     shape = jax.ShapeDtypeStruct
     cols = wa1.shape[1] + heads_out.shape[1]
     line = pltpu.VMEM((ZED, count, wide), bf16)
     return pl.pallas_call(
         end_kernel,
-        out_shape=(shape((3, 128, cols), bf16), shape(xin.shape, bf16), shape(xin.shape, bf16)),
-        in_specs=[ANY] + [VMEM] * 4 + [ANY] * 4,
-        out_specs=(VMEM,) * 3,
+        out_shape=(shape((3, 128, cols), bf16), shape(xin.shape, bf16), shape(xin.shape, bf16), shape(rest.shape, bf16)),
+        in_specs=[ANY] + [VMEM] * 4 + [ANY] * 5,
+        out_specs=(VMEM,) * 3 + (ANY,),
         scratch_shapes=[pltpu.VMEM((ZED, 2, 2, 128, cols), bf16)] + scatter_room(cols) + [
             pltpu.VMEM((2, 128, cols), bf16),
             pltpu.VMEM(xin.shape, bf16), line, line,
@@ -1416,18 +1424,23 @@
             pltpu.VMEM(d_mid.shape, f32),
             pltpu.VMEM(xin.shape, bf16),
             pltpu.VMEM(mid.shape, f32),
-            DMA((3,)), DMA((6,)), DMA((4, 5)), DMA((4, 5)), DMA((5, 2)), DMA((5, 2)),
+            DMA((3,)), DMA((2,)), DMA((6,)), DMA((4, 5)), DMA((4, 5)), DMA((5, 2)), DMA((5, 2)),
             DMA((wide // COLS,)), DMA((wide // COLS,)),
         ],
         compiler_params=params(),
         name="end",
-    )(t, home, xh, d_att, heads_out, wa1, d_mid, xin, mid)
+    )(t, home, xh, d_att, heads_out, wa1, d_mid, xin, mid, rest)
 
 
 def finish_kernel(
-    zm, za, wq, wk, wv, wg, wu, g1, g2, o_q, o_k, o_v, o_out, o_g, o_u, o_d, gains
+    zm, zr, za, wq, wk, wv, wg, wu, g1, g2, o_q, o_k, o_v, o_out, o_g, o_u, o_d, gains
 ):
     units = wg.shape[1] // ZED
+    hole = (lax.axis_index("seq") // 4 + 2) % ZED
+
+    def quarter(n, cols):
+        return jnp.where(hole == n, zr[:, cols].astype(f32), zm[n, :, cols].astype(f32))
+
     room = zm.shape[2] // 3
     nq, nv = wq.shape[1], wv.shape[1]
     lanes = g1.shape[1]
@@ -1458,7 +1471,7 @@
             for c in range(0, units, lanes):
                 size = min(lanes, units - c)
                 cols = slice(n * units + c, n * units + c + size)
-                value = zm[n, :, base + c : base + c + size].astype(f32)
+                value = quarter(n, slice(base + c, base + c + size))
                 out[:, cols] = value * scale2[:, 0:size]
                 prod = value * w[:, cols].astype(f32)
                 if size == lanes:
@@ -1469,13 +1482,13 @@
                     )
         for c in range(0, units, lanes):
             size = min(lanes, units - c)
-            value = jnp.transpose(zm[n, :, 2 * room + c : 2 * room + c + lanes].astype(f32))
+            value = jnp.transpose(quarter(n, slice(2 * room + c, 2 * room + c + lanes)))
             o_d[n * units + c : n * units + c + size, :] = value[0:size, :]
     gains[0:1, :] = jnp.sum(jnp.transpose(first), axis=0, keepdims=True)
     gains[1:2, :] = jnp.sum(jnp.transpose(second), axis=0, keepdims=True)
 
 
-def finish(zm, za, wq, wk, wv, wg, wu, g1, g2, w_out, w_down):
+def finish(zm, zr, za, wq, wk, wv, wg, wu, g1, g2, w_out, w_down):
     shape = lambda w: jax.ShapeDtypeStruct(w.shape, f32)
     return pl.pallas_call(
         finish_kernel,
@@ -1483,11 +1496,11 @@
             shape(wq), shape(wk), shape(wv), shape(w_out), shape(wg), shape(wu), shape(w_down),
             jax.ShapeDtypeStruct((2, 128), f32),
         ),
-        in_specs=[VMEM] * 9,
+        in_specs=[VMEM] * 10,
         out_specs=(VMEM,) * 8,
         compiler_params=pltpu.CompilerParams(vmem_limit_bytes=VMEM_LIMIT),
         name="finish",
-    )(zm, za, wq, wk, wv, wg, wu, g1, g2)
+    )(zm, zr, za, wq, wk, wv, wg, wu, g1, g2)
 
 
 def fast(
@@ -1514,14 +1527,14 @@
     d_up = (d_hidden * silu).astype(bf16)
     d_n2 = (mix(d_gate, w_g, ((1,), (1,))) + mix(d_up, w_u, ((1,), (1,)))).astype(bf16)
     lines = (ZED, mbs, count, wide)
-    zm, d_mid, d_att, home, branch = back(
+    zm, d_mid, d_att, home, branch, rest = back(
         n2, up_g, d_gate, d_up, hidden, d_n2.reshape(lines), w_o, wm, middle, cotangent, got, ratio, den
     )
-    za, input_grad, outputs = end(
-        branch.reshape(lines), home, xh1, d_att, heads_out, wa1, d_mid, inputs, middle
+    za, input_grad, outputs, zr = end(
+        branch.reshape(lines), home, xh1, d_att, heads_out, wa1, d_mid, inputs, middle, rest
     )
     o_q, o_k, o_v, o_out, o_g, o_u, o_d, gains = finish(
-        zm, za, w_query, w_key, w_value, w_gate, w_up,
+        zm, zr, za, w_query, w_key, w_value, w_gate, w_up,
         gain1, gain2, w_out, w_down,
     )
     gains = lax.psum(gains, "head")

time: 459 us -> 445 us (0.969)
  Pallas kernels: 428 us -> 414 us
    pallas_call x1, Pallas kernels: 126 us -> 108 us  [back(): pl.pallas_call(back_kernel, out_shape=(shape((ZED, 128, cols), bf16), sha...]
where the time goes in v10:
time: 445 us
  Pallas kernels  414 us (93%)
  matrix products  24 us (5%)
    pallas_call x1, Pallas kernels, front(): pl.pallas_call(front_kernel, out_shape=(shape((wide, wide1), bf16), shape...  201 us
    pallas_call x1, Pallas kernels, back(): pl.pallas_call(back_kernel, out_shape=(shape((ZED, 128, cols), bf16), sha...  108 us
    pallas_call x1, Pallas kernels, end(): pl.pallas_call(end_kernel, out_shape=(shape((3, 128, cols), bf16), shape(...  98.2 us
    dot_general x5, matrix products, mix(): return lax.dot_general(a, b, (over, ((), ())), preferred_element_type=f32)  24 us

profile of v10, /device:TPU:0, one launch (start us, length us, event | category | flops | bytes accessed | tf_op | source)
XLA Modules:
  0.0 444.8 jit_solution(18239492226925852822)
XLA Ops:
  0.6 201.2 %front.1 = (bf16[2048,1280]{1,0:T(8,128)(2,1)}, bf16[2048,1024]{1,0:T(8,128)(2,1)}, bf16[2048,2304]{1,0:T(8,128)(2,1)}, bf16[4,2,128,2048]{3,2,1,0:T(8,128)(2,1)...) custom-call(bf16[128,128]{1,0:T(8,128)(2,1)} %wq.3, ...), custom_call_target="tpu_custom_call" | custom-call | tf_op jit(solution)/shard_map/front/pallas_call | solution.py:693
  201.8 0.0 copy-start
  201.8 0.0 copy-start.1
  201.9 6.3 %fusion.1 = f32[1024,768]{1,0:T(8,128)S(1)} fusion(bf16[1024,2048]{1,0:T(8,128)(2,1)} %bitcast.15, bf16[2048,2304]{1,0:T(8,128)(2,1)} %get-tuple-element.42.wm), kind=kOutput, calls=%fused_computation.6 | convolution fusion | flops 3221225472 | bytes 10485760 | tf_op jit(solution)/shard_map/dot_general | solution.py:285
  208.1 0.0 copy-done
  208.2 0.7 copy-done.1
  208.9 3.4 fusion.5
  212.3 5.7 %multiply_convert_fusion = (bf16[1024,768]{1,0:T(8,128)(2,1)}, bf16[1024,768]{1,0:T(8,128)(2,1)S(1)}, bf16[1024,768]{1,0:T(8,128)(2,1)S(1)}) fusion(f32[1024,768]{1,0:T(8,128)S(1)} %fusion.5, f32[1024,768]{1,0:T(8,128)S(1)} %fusion.1, bf16[1024,2048]{1,0:T(8,128)(2,1)S(1)} %bitcast.19, bf16[2048,2304]{1,0:T(8,128)(2,1)S(1)} %copy-done), kind=kOutput, calls=%fused_computation.1 | convolution fusion | flops 3233021952 | bytes 18350080 | tf_op jit(solution)/shard_map/dot_general | solution.py:285
  218.0 0.0 copy-start.2
  218.0 0.0 copy-start.3
  218.0 3.5 fusion.3
  221.5 0.0 copy-done.2
  221.5 0.0 copy-done.3
  221.5 5.1 %add_convert_fusion = bf16[1024,2048]{1,0:T(8,128)(2,1)} fusion(f32[1024,2048]{1,0:T(8,128)S(1)} %fusion.3, bf16[1024,768]{1,0:T(8,128)(2,1)S(1)} %get-tuple-element.71.du_in, bf16[2048,2304]{1,0:T(8,128)(2,1)S(1)} %copy-done), kind=kOutput, calls=%fused_computation | convolution fusion | flops 3225419776 | bytes 17301504 | tf_op jit(solution)/shard_map/dot_general | solution.py:285
  226.6 108.2 %back.1 = (bf16[4,128,2304]{2,1,0:T(8,128)(2,1)}, f32[2,128,2048]{2,1,0:T(8,128)}, bf16[256,2048]{1,0:T(8,128)(2,1)}, bf16[16,160,128]{2,1,0:T(8,128)(2,1)}, bf1...) custom-call(bf16[1024,2048]{1,0:T(8,128)(2,1)} %bitcast.17, bf16[1024,2048]{1,0:T(8,128)(2,1)} %bitcast.16, ...), custom_call_target="tpu_custom_call" | custom-call | tf_op jit(solution)/shard_map/back/pallas_call | solution.py:1221
  334.8 98.2 %end.1 = (bf16[3,128,2304]{2,1,0:T(8,128)(2,1)}, bf16[2,128,2048]{2,1,0:T(8,128)(2,1)}, bf16[2,128,2048]{2,1,0:T(8,128)(2,1)}, bf16[128,2304]{1,0:T(8,128)(2,1)}) custom-call(bf16[4,2,128,2048]{3,2,1,0:T(8,128)(2,1)} %bitcast.21, bf16[16,160,128]{2,1,0:T(8,128)(2,1)} %get-tuple-element.49.home, bf16[256,2048]{1,0:T(8,128)(2,1)} %get-tuple-element.50.xh, ...), custom_call_target="tpu_custom_call" | custom-call | tf_op jit(solution)/shard_map/end/pallas_call | solution.py:1409
  433.0 0.0 copy-start.5
  433.0 0.0 copy-start.4
  433.1 6.7 %finish.1 = (f32[128,128]{1,0:T(8,128)}, f32[128,128]{1,0:T(8,128)}, f32[128,1024]{1,0:T(8,128)}, f32[1024,128]{1,0:T(8,128)}, f32[128,2816]{1,0:T(8,128)}, /*in...) custom-call(bf16[4,128,2304]{2,1,0:T(8,128)(2,1)} %get-tuple-element.58.zm, ...), custom_call_target="tpu_custom_call" | custom-call | tf_op jit(solution)/shard_map/finish/pallas_call | solution.py:1493
  439.8 2.6 psum.7
  442.4 0.5 slice_bitcast_fusion
  442.9 0.0 copy-done.5
  442.9 1.0 copy.24
  443.9 0.0 copy-done.4
  443.9 1.0 copy.25
Async XLA Ops:
  201.8 6.3 %copy-start = (bf16[2048,2304]{1,0:T(8,128)(2,1)S(1)}, bf16[2048,2304]{1,0:T(8,128)(2,1)}, u32[]{:S(2)}) copy-start(bf16[2048,2304]{1,0:T(8,128)(2,1)} %get-tuple-element.42.wm) | copy-start | bytes 28311556
  201.8 7.0 %copy-start.1 = (bf16[4,2,128,2048]{3,2,1,0:T(8,128)(2,1)S(1)}, bf16[4,2,128,2048]{3,2,1,0:T(8,128)(2,1)}, u32[]{:S(2)}) copy-start(bf16[4,2,128,2048]{3,2,1,0:T(8,128)(2,1)} %get-tuple-element.40) | copy-start | bytes 12582916
  218.0 3.5 copy-start.2
  218.0 3.5 copy-start.3
  433.0 9.9 %copy-start.5 = (bf16[2,128,2048]{2,1,0:T(8,128)(2,1)S(1)}, bf16[2,128,2048]{2,1,0:T(8,128)(2,1)}, u32[]{:S(2)}) copy-start(bf16[2,128,2048]{2,1,0:T(8,128)(2,1)} %get-tuple-element.85) | copy-start | bytes 3145732
  433.0 10.8 %copy-start.4 = (bf16[2,128,2048]{2,1,0:T(8,128)(2,1)S(1)}, bf16[2,128,2048]{2,1,0:T(8,128)(2,1)}, u32[]{:S(2)}) copy-start(bf16[2,128,2048]{2,1,0:T(8,128)(2,1)} %get-tuple-element.86) | copy-start | bytes 3145732
